TPU v7x, 32 devices: a whole 2x2x4 slice. The times are simulated.
32 devices in a mesh: lon: 4 (over y, core), lat: 4 (over z), dp: 2 (over x).
Axes of the slice: x: 2, y: 2, z: 4, core: 2. Of those that a mesh axis runs over, the one named last changes fastest.
Arguments:
- tokens: bfloat16 [2, 2, 24, 48, 192], P('dp', None, 'lat', 'lon'), may hold values from -6 to 6
- grad_out: bfloat16 [2, 2, 24, 48, 192], P('dp', None, 'lat', 'lon'), may hold values from -6 to 6
- qkv_weight: bfloat16 [576, 192], P('dp'), may hold values from -0.4375 to 0.4375
- proj_weight: bfloat16 [192, 192], P('dp'), may hold values from -0.4375 to 0.4375
- norm_gain: bfloat16 [192], P('dp'), may hold values from 0.5 to 1.5
- bias_table: float32 [4, 6, 3312], P('lat'), may hold values from -2.5 to 402.5
Outputs:
- grad_tokens: bfloat16 [2, 2, 24, 48, 192], P('dp', None, 'lat', 'lon')
- grad_qkv_weight: float32 [576, 192], P('dp')
- grad_proj_weight: float32 [192, 192], P('dp')
- grad_norm_gain: float32 [192], P('dp')
- grad_bias_table: float32 [4, 6, 3312], P('lat')
All inputs are finite; a program needn't handle non-finite values.
Results may differ from a plain program's by a relative error of at most 0.015.
Values may be sent and summed in bfloat16 or wider, within the bound.
No kernel may reach another device: no remote copies, remote signals or barrier semaphores. Data moves between devices by JAX's collectives and lax.ppermute only.
A program may use at most 64 MiB of HBM per device.

v0:
```python
import math

import jax
import jax.numpy as jnp
from jax import lax
from jax.sharding import PartitionSpec as P

C = 192
H = 6
HD = 32
WZ = 2
WA = 6
WL = 12
SA = 3
SO = 6
WT = 144
POS = 3312


EPS = 1e-05
MASKED = -1e30


def passed_along(value, axis, steps):
    count = lax.axis_size(axis)
    pairs = [(source, (source + steps) % count) for source in range(count)]
    return lax.ppermute(value, axis, pairs)


def shortened(shard):
    return jax.tree.map(lambda a: a.astype(jnp.bfloat16) if a.dtype == jnp.float32 else a, shard)


def offsets_table():
    first = jnp.arange(WL)[:, None, None]
    second = jnp.arange(WL)[None, :, None]
    offset = jnp.arange(2 * WL - 1)[None, None, :]
    return (offset == first - second + WL - 1).astype(jnp.float32)


def spread_bias(table, onehot):
    window_rows = WZ * WA
    shaped = table.reshape(table.shape[0], H, window_rows, window_rows, 2 * WL - 1)
    spread = jnp.einsum("ghabr,uvr->ghaubv", shaped, onehot, precision=lax.Precision.HIGHEST)
    return spread.reshape(table.shape[0], H, WT, WT)


def gather_bias(grad_full, onehot):
    window_rows = WZ * WA
    shaped = grad_full.reshape(grad_full.shape[0], H, window_rows, WL, window_rows, WL)
    folded = jnp.einsum("ghaubv,uvr->ghabr", shaped, onehot, precision=lax.Precision.HIGHEST)
    return folded.reshape(grad_full.shape[0], H, POS)


def to_windows(grid, lat_rows, lon_cols):
    members, levels, channels = (grid.shape[0], grid.shape[1], grid.shape[4])
    lat_types = lat_rows // WA
    lon_windows = lon_cols // WL
    parts = grid.reshape(members, levels, lat_types, WA, lon_windows, WL, channels)
    parts = parts.transpose(2, 0, 4, 1, 3, 5, 6)
    return parts.reshape(lat_types, members * lon_windows, WT, channels)


def from_windows(blocks, members, lat_rows, lon_cols):
    lat_types = lat_rows // WA
    lon_windows = lon_cols // WL
    channels = blocks.shape[-1]
    parts = blocks.reshape(lat_types, members, lon_windows, WZ, WA, WL, channels)
    return parts.transpose(1, 3, 0, 4, 2, 5, 6).reshape(members, WZ, lat_rows, lon_cols, channels)


def window_grads(
    window_x, window_dy, window_flag, table, qkv_weight, proj_weight, norm_gain, onehot
):
    groups, count = (window_x.shape[0], window_x.shape[1])
    flat_x = window_x.reshape(-1, C).astype(jnp.float32)
    average = jnp.mean(flat_x, axis=-1, keepdims=True)
    centred = flat_x - average
    variance = jnp.mean(centred * centred, axis=-1, keepdims=True)
    inverse = lax.rsqrt(variance + EPS)
    unit = centred * inverse
    gain_value = norm_gain.astype(jnp.float32)
    normed = (unit * gain_value).astype(jnp.bfloat16)
    projected = jnp.dot(normed, qkv_weight.T, preferred_element_type=jnp.float32).astype(
        jnp.bfloat16
    )
    split = projected.reshape(groups, count, WT, 3, H, HD)
    queries = split[:, :, :, 0]
    key_part = split[:, :, :, 1]
    values = split[:, :, :, 2]
    head_scale = 1.0 / math.sqrt(HD)
    bias_full = spread_bias(table, onehot)
    scores = (
        jnp.einsum("gwqhd,gwkhd->gwhqk", queries, key_part, preferred_element_type=jnp.float32)
        * head_scale
    )
    scores = scores + bias_full[:, None]
    allowed = window_flag[:, :, None, :, None] == window_flag[:, :, None, None, :]
    scores = jnp.where(allowed, scores, MASKED)
    highest = jnp.max(scores, axis=-1, keepdims=True)
    expo = jnp.exp(scores - highest)
    probs = expo / jnp.sum(expo, axis=-1, keepdims=True)
    probs_low = probs.astype(jnp.bfloat16)
    attended = jnp.einsum(
        "gwhqk,gwkhd->gwqhd", probs_low, values, preferred_element_type=jnp.float32
    )
    attended = attended.astype(jnp.bfloat16).reshape(-1, C)
    flat_dy = window_dy.reshape(-1, C)
    grad_proj = jnp.dot(flat_dy.T, attended, preferred_element_type=jnp.float32)
    grad_att = jnp.dot(flat_dy, proj_weight, preferred_element_type=jnp.float32).astype(
        jnp.bfloat16
    )
    grad_att = grad_att.reshape(groups, count, WT, H, HD)
    grad_probs = jnp.einsum(
        "gwqhd,gwkhd->gwhqk", grad_att, values, preferred_element_type=jnp.float32
    )
    grad_values = jnp.einsum(
        "gwhqk,gwqhd->gwkhd", probs_low, grad_att, preferred_element_type=jnp.float32
    )
    grad_scores = probs * (grad_probs - jnp.sum(probs * grad_probs, axis=-1, keepdims=True))
    scores_low = grad_scores.astype(jnp.bfloat16)
    grad_queries = (
        jnp.einsum("gwhqk,gwkhd->gwqhd", scores_low, key_part, preferred_element_type=jnp.float32)
        * head_scale
    )
    grad_keys = (
        jnp.einsum("gwhqk,gwqhd->gwkhd", scores_low, queries, preferred_element_type=jnp.float32)
        * head_scale
    )
    grad_qkv = (
        jnp.stack([grad_queries, grad_keys, grad_values], axis=3)
        .reshape(-1, 3 * C)
        .astype(jnp.bfloat16)
    )
    grad_qkv_w = jnp.dot(grad_qkv.T, normed, preferred_element_type=jnp.float32)
    grad_normed = jnp.dot(grad_qkv, qkv_weight, preferred_element_type=jnp.float32)
    grad_gain = jnp.sum(grad_normed * unit, axis=0)
    scaled = grad_normed * gain_value
    grad_x = inverse * (
        scaled
        - jnp.mean(scaled, axis=-1, keepdims=True)
        - unit * jnp.mean(scaled * unit, axis=-1, keepdims=True)
    )
    grad_table = gather_bias(jnp.sum(grad_scores, axis=1), onehot)
    return (grad_x.reshape(groups, count, WT, C), grad_qkv_w, grad_proj, grad_gain, grad_table)


def body(tokens, grad_out, qkv_weight, proj_weight, norm_gain, bias_table):
    full_qkv, full_proj, full_gain = (
        lax.all_gather(qkv_weight, "dp", axis=0, tiled=True),
        lax.all_gather(proj_weight, "dp", axis=0, tiled=True),
        lax.all_gather(norm_gain, "dp", axis=0, tiled=True),
    )
    members, levels, lat_rows, lon_cols = (
        tokens.shape[0],
        tokens.shape[1],
        tokens.shape[2],
        tokens.shape[3],
    )
    ahead = passed_along((tokens[:, :, :, :SO], grad_out[:, :, :, :SO]), "lon", -1)
    lon_tokens = jnp.concatenate([tokens[:, :, :, SO:], ahead[0]], axis=3)
    lon_grads = jnp.concatenate([grad_out[:, :, :, SO:], ahead[1]], axis=3)
    above = passed_along((lon_tokens[:, :, :SA], lon_grads[:, :, :SA]), "lat", -1)
    shifted = jnp.concatenate([lon_tokens[:, :, SA:], above[0]], axis=2)
    shifted_dy = jnp.concatenate([lon_grads[:, :, SA:], above[1]], axis=2)
    pole_device = lax.axis_index("lat") == lax.axis_size("lat") - 1
    wrapped = jnp.logical_and(jnp.arange(lat_rows) >= lat_rows - SA, pole_device)
    grid_shape = (members, levels, lat_rows, lon_cols, 1)
    flag_grid = jnp.broadcast_to(wrapped[None, None, :, None, None], grid_shape)
    outputs = window_grads(
        to_windows(shifted, lat_rows, lon_cols),
        to_windows(shifted_dy, lat_rows, lon_cols),
        to_windows(flag_grid, lat_rows, lon_cols)[..., 0],
        bias_table,
        full_qkv,
        full_proj,
        full_gain,
        offsets_table(),
    )
    grad_blocks, grad_qkv_w, grad_proj, grad_gain, grad_table = outputs
    table_sum = lax.psum(grad_table, ("lon", "dp"))
    grad_shifted = from_windows(grad_blocks, members, lat_rows, lon_cols)
    below = passed_along(grad_shifted[:, :, lat_rows - SA :].astype(jnp.bfloat16), "lat", 1).astype(
        jnp.float32
    )
    lat_restored = jnp.concatenate([below, grad_shifted[:, :, : lat_rows - SA]], axis=2)
    behind = passed_along(shortened(lat_restored[:, :, :, lon_cols - SO :]), "lon", 1)
    restored = jnp.concatenate([behind, lat_restored[:, :, :, : lon_cols - SO]], axis=3)
    grad_tokens = (grad_out.astype(jnp.float32) + restored).astype(jnp.bfloat16)
    summed = lax.psum((grad_qkv_w, grad_proj, grad_gain), ("lon", "lat"))
    shares = (
        lax.psum_scatter(
            summed[0].astype(jnp.bfloat16), "dp", scatter_dimension=0, tiled=True
        ).astype(jnp.float32),
        lax.psum_scatter(
            summed[1].astype(jnp.bfloat16), "dp", scatter_dimension=0, tiled=True
        ).astype(jnp.float32),
        lax.psum_scatter(
            summed[2].astype(jnp.bfloat16), "dp", scatter_dimension=0, tiled=True
        ).astype(jnp.float32),
    )
    return (grad_tokens, shares[0], shares[1], shares[2], table_sum)


def solution(mesh):
    return jax.shard_map(
        body,
        mesh=mesh,
        in_specs=(
            P("dp", None, "lat", "lon", None),
            P("dp", None, "lat", "lon", None),
            P("dp", None),
            P("dp", None),
            P("dp"),
            P("lat", None, None),
        ),
        out_specs=(
            P("dp", None, "lat", "lon", None),
            P("dp", None),
            P("dp", None),
            P("dp"),
            P("lat", None, None),
        ),
        check_vma=False,
    )
```

profile of v0, /device:TPU:0, one launch (start us, length us, event | category | flops | bytes accessed | tf_op | source)
XLA Modules:
  0.0 192.5 jit_solution(13003009651287583203)
XLA Ops:
  8.1 0.9 fusion.26
  9.0 2.5 %collective-permute-start = (bf16[1,2,6,6,192]{4,1,3,2,0:T(2,128)(2,1)S(1)}, bf16[1,2,6,6,192]{4,1,3,2,0:T(2,128)(2,1)S(1)}, u32[]{:S(2)}, u32[]{:S(2)}) collective-permute-start(bf16[1,2,6,6,192]{4,1,3,2,0:T(2,128)(2,1)S(1)} %get-tuple-element.24), channel_id=1, source_target_pairs={{0,24},{8,0},{16,8},{24,16},{1,25},{9,1},{17,9},{25,17},{2,26},{10... | collective-permute-start | bytes 82952 | tf_op jit(solution)/shard_map/ppermute | solution.py:27
  13.0 1.1 reduce.8
  14.8 4.9 %convolution_bitcast_fusion = f32[1,6,12,12,12,12]{4,5,2,1,3,0:T(8,128)} fusion(f32[6,12,12,23,1]{3,2,1,0,4:T(8,128)S(1)} %reshape.415, pred[12,12,23,1,1]{2,0,1,4,3:T(8,128)(4,1)S(1)} %fusion.16), kind=kOutput, calls=%fused_computation.1 | convolution fusion | flops 34338816 | bytes 580464 | tf_op jit(solution)/shard_map/ghabr,uvr->ghaubv/dot_general | solution.py:44
  19.7 6.3 %all_gather.10 = bf16[576,192]{1,0:T(8,128)(2,1)S(1)} all-gather(bf16[288,192]{1,0:T(8,128)(2,1)S(1)} %copy-done.5), channel_id=1, replica_groups=mesh['lon'=4,'lat'=4,'dp'=2] {'dp'}, dimensions={0}, use_global_device_ids=true | all-gather | bytes 331776 | tf_op jit(solution)/shard_map/all_gather | solution.py:150
  27.4 4.9 %all-reduce = bf16[192]{0:T(256)(128)(2,1)S(1)} all-reduce(bf16[192]{0:T(256)(128)(2,1)S(1)} %dynamic-update-slice), channel_id=1, replica_groups=mesh['lon'=4,'lat'=4,'dp'=2] {'dp'}, use_global_device_ids=true, to_apply=%add | all-reduce | flops 192 | bytes 768
  32.4 11.7 %copy.70 = f32[1,6,12,12,12,12]{3,2,5,4,1,0:T(8,128)} copy(f32[1,6,12,12,12,12]{4,5,2,1,3,0:T(8,128)} %convolution_bitcast_fusion) | data formatting | bytes 995328 | tf_op jit(solution)/shard_map/broadcast_in_dim;reshape | solution.py:97
  44.1 4.9 %reshape.419 = f32[6,144,144]{1,2,0:T(8,128)S(1)} reshape(f32[1,6,12,12,12,12]{3,2,5,4,1,0:T(8,128)} %copy.70) | data formatting | bytes 995328 | tf_op jit(solution)/shard_map/broadcast_in_dim;reshape | solution.py:97
  49.0 4.8 %all_gather.11 = bf16[192,192]{1,0:T(8,128)(2,1)S(1)} all-gather(bf16[96,192]{1,0:T(8,128)(2,1)S(1)} %copy-done.9), channel_id=1, replica_groups=mesh['lon'=4,'lat'=4,'dp'=2] {'dp'}, dimensions={0}, use_global_device_ids=true | all-gather | bytes 110592 | tf_op jit(solution)/shard_map/all_gather | solution.py:151
  53.9 3.7 %collective-permute-start.1 = (bf16[1,2,3,12,192]{4,1,3,2,0:T(2,128)(2,1)S(1)}, bf16[1,2,3,12,192]{4,1,3,2,0:T(2,128)(2,1)S(1)}, u32[]{:S(2)}, u32[]{:S(2)}) collective-permute-start(bf16[1,2,3,12,192]{4,1,3,2,0:T(2,128)(2,1)S(1)} %get-tuple-element.22), channel_id=1, source_target_pairs={{0,6},{2,0},{4,2},{6,4},{1,7},{3,1},{5,3},{7,5},{8,14},{10,8},{12,... | collective-permute-start | bytes 82952 | tf_op jit(solution)/shard_map/ppermute | solution.py:27
  60.4 1.5 collective-permute-done.3
  64.6 1.9 convolution_bitcast_fusion.2
  66.5 1.2 multiply_reduce_fusion
  69.0 1.0 convolution_convert_fusion.1
  70.1 5.0 %reshape.406 = f32[6,12,12,12,12]{2,1,4,3,0:T(8,128)} reshape(f32[6,144,144]{1,2,0:T(8,128)S(1)} %subtract_multiply_fusion) | data formatting | bytes 995328 | tf_op jit(solution)/shard_map/reshape.46
  76.3 6.0 %convolution_bitcast_fusion.1 = f32[6,12,12,23]{3,1,2,0:T(8,128)S(1)} fusion(f32[6,12,12,12,12]{2,1,4,3,0:T(8,128)} %reshape.406, s32[12,12]{0,1:T(8,128)S(1)} %copy-done.8), kind=kOutput, calls=%fused_computation.7 | convolution fusion | flops 34342128 | bytes 577728 | tf_op jit(solution)/shard_map/ghaubv,uvr->ghabr/dot_general | solution.py:51
  82.5 0.9 reshape.407
  83.4 77.7 %all-reduce.7 = (bf16[576,192]{1,0:T(8,128)(2,1)}, bf16[192,192]{1,0:T(8,128)(2,1)}, bf16[192]{0:T(256)(128)(2,1)S(1)}) all-reduce(f32[576,192]{1,0:T(8,128)S(1)} %fusion.30, f32[192,192]{1,0:T(8,128)S(1)} %fusion.31, f32[192]{0:T(256)S(1)} %get-tuple-element.15), channel_id=1, replica_groups=mesh['lon'=4,'lat'=4,'dp'=2] {'lon','lat'}, use_global_device_ids=true, to_apply=%region_7.8 | all-reduce | flops 147648 | bytes 885888 | tf_op jit(solution)/shard_map/psum | solution.py:190
  162.2 4.9 %all-reduce.1 = bf16[192]{0:T(256)(128)(2,1)S(1)} all-reduce(bf16[192]{0:T(256)(128)(2,1)S(1)} %get-tuple-element.20), channel_id=4, replica_groups=mesh['lon'=4,'lat'=4,'dp'=2] {'dp'}, use_global_device_ids=true, to_apply=%region_13.14.clone | all-reduce | flops 192 | bytes 768
  168.1 1.6 copy.60
  169.7 1.3 collective-permute-done.5
  171.8 1.4 convert_element_type.150
  173.2 10.2 %reduce-scatter.3.cloned.1.call-done = bf16[288,192]{1,0:T(8,128)(2,1)} async-done(((bf16[576,192]{1,0:T(8,128)(2,1)}), bf16[288,192]{1,0:T(8,128)(2,1)}) %reduce-scatter.3.cloned.1.call-update) | async-done | bytes 110608 | tf_op jit(solution)/shard_map/reduce_scatter | solution.py:192
  183.4 1.6 convert_element_type.145
  (106 shorter events, 13.2 us)
Async XLA Ops:
  8.0 17.9 %copy-start.15 = (u32[32]{0:T(128)S(1)}, u32[32]{0:T(128)}, u32[]{:S(2)}) copy-start(u32[32]{0:T(128)} %constant.36) | copy-start | bytes 388
  8.0 11.7 %copy-start.5 = (bf16[288,192]{1,0:T(8,128)(2,1)S(1)}, bf16[288,192]{1,0:T(8,128)(2,1)}, u32[]{:S(2)}) copy-start(bf16[288,192]{1,0:T(8,128)(2,1)} %param.8) | copy-start | bytes 331780
  8.0 19.2 %copy-start.16 = (bf16[96]{0:T(256)(128)(2,1)S(1)}, bf16[96]{0:T(256)(128)(2,1)}, u32[]{:S(2)}) copy-start(bf16[96]{0:T(256)(128)(2,1)} %param.10) | copy-start | bytes 580
  8.0 160.1 %all-reduce.6.cloned.1.call-start = ((), (), s32[]{:S(2)}) async-start(), calls=%async_computation.4 | async-start | bytes 212992 | tf_op jit(solution)/shard_map/psum | solution.py:181
  9.0 44.9 %collective-permute-start = (bf16[1,2,6,6,192]{4,1,3,2,0:T(2,128)(2,1)S(1)}, bf16[1,2,6,6,192]{4,1,3,2,0:T(2,128)(2,1)S(1)}, u32[]{:S(2)}, u32[]{:S(2)}) collective-permute-start(bf16[1,2,6,6,192]{4,1,3,2,0:T(2,128)(2,1)S(1)} %get-tuple-element.24), channel_id=1, source_target_pairs={{0,24},{8,0},{16,8},{24,16},{1,25},{9,1},{17,9},{25,17},{2,26},{10... | collective-permute-start | bytes 82952 | tf_op jit(solution)/shard_map/ppermute | solution.py:27
  12.3 45.3 %collective-permute-start.2 = (bf16[1,2,6,6,192]{4,1,3,2,0:T(2,128)(2,1)S(1)}, bf16[1,2,6,6,192]{4,1,3,2,0:T(2,128)(2,1)S(1)}, u32[]{:S(2)}, u32[]{:S(2)}) collective-permute-start(bf16[1,2,6,6,192]{4,1,3,2,0:T(2,128)(2,1)S(1)} %get-tuple-element.28), channel_id=1, source_target_pairs={{0,24},{8,0},{16,8},{24,16},{1,25},{9,1},{17,9},{25,17},{2,26},{10... | collective-permute-start | bytes 82952 | tf_op jit(solution)/shard_map/ppermute | solution.py:27
  13.0 19.4 %copy-start.7 = (s32[12,12]{0,1:T(8,128)}, s32[12,12]{0,1:T(8,128)S(1)}, u32[]{:S(2)}) copy-start(s32[12,12]{0,1:T(8,128)S(1)} %subtract_add_fusion) | copy-start | bytes 1732
  44.1 5.0 %copy-start.9 = (bf16[96,192]{1,0:T(8,128)(2,1)S(1)}, bf16[96,192]{1,0:T(8,128)(2,1)}, u32[]{:S(2)}) copy-start(bf16[96,192]{1,0:T(8,128)(2,1)} %param.9) | copy-start | bytes 110596
  53.9 5.3 %collective-permute-start.1 = (bf16[1,2,3,12,192]{4,1,3,2,0:T(2,128)(2,1)S(1)}, bf16[1,2,3,12,192]{4,1,3,2,0:T(2,128)(2,1)S(1)}, u32[]{:S(2)}, u32[]{:S(2)}) collective-permute-start(bf16[1,2,3,12,192]{4,1,3,2,0:T(2,128)(2,1)S(1)} %get-tuple-element.22), channel_id=1, source_target_pairs={{0,6},{2,0},{4,2},{6,4},{1,7},{3,1},{5,3},{7,5},{8,14},{10,8},{12,... | collective-permute-start | bytes 82952 | tf_op jit(solution)/shard_map/ppermute | solution.py:27
  57.7 4.2 %collective-permute-start.3 = (bf16[1,2,3,12,192]{4,1,3,2,0:T(2,128)(2,1)S(1)}, bf16[1,2,3,12,192]{4,1,3,2,0:T(2,128)(2,1)S(1)}, u32[]{:S(2)}, u32[]{:S(2)}) collective-permute-start(bf16[1,2,3,12,192]{4,1,3,2,0:T(2,128)(2,1)S(1)} %get-tuple-element.26), channel_id=1, source_target_pairs={{0,6},{2,0},{4,2},{6,4},{1,7},{3,1},{5,3},{7,5},{8,14},{10,8},{12,... | collective-permute-start | bytes 82952 | tf_op jit(solution)/shard_map/ppermute | solution.py:27
  59.7 3.7 %copy-start.2 = (f32[2,6,12]{0,2,1:T(8,128)}, f32[2,6,12]{0,2,1:T(8,128)S(1)}, u32[]{:S(2)}) copy-start(f32[2,6,12]{0,2,1:T(8,128)S(1)} %add_rsqrt_fusion) | copy-start | bytes 1732
  60.1 3.3 %copy-start.11 = (f32[144]{0:T(256)}, f32[144]{0:T(256)S(1)}, u32[]{:S(2)}) copy-start(f32[144]{0:T(256)S(1)} %div.25) | copy-start | bytes 1732
  64.6 3.1 %copy-start.10 = (f32[6,144]{1,0:T(8,128)}, f32[6,144]{1,0:T(8,128)S(1)}, u32[]{:S(2)}) copy-start(f32[6,144]{1,0:T(8,128)S(1)} %get-tuple-element.31) | copy-start | bytes 10372
  68.5 6.5 %copy-start.6 = (bf16[1,1,144,1,6,32]{2,5,4,3,1,0:T(8,128)(2,1)S(1)}, bf16[1,1,144,1,6,32]{2,5,4,3,1,0:T(8,128)(2,1)}, u32[]{:S(2)}) copy-start(bf16[1,1,144,1,6,32]{2,5,4,3,1,0:T(8,128)(2,1)} %convolution_bitcast_fusion.2) | copy-start | bytes 165892
  68.5 6.6 %copy-start.12 = (f32[144]{0:T(256)S(1)}, f32[144]{0:T(256)}, u32[]{:S(2)}) copy-start(f32[144]{0:T(256)} %copy-done.11) | copy-start | bytes 1732
  68.5 6.6 %copy-start.14 = (f32[144]{0:T(256)S(1)}, f32[144]{0:T(256)}, u32[]{:S(2)}) copy-start(f32[144]{0:T(256)} %copy-done.13) | copy-start | bytes 1732
  68.8 6.8 %copy-start.1 = (bf16[1,2,3,12,192]{4,1,3,2,0:T(2,128)(2,1)S(1)}, bf16[1,2,3,12,192]{4,1,3,2,0:T(2,128)(2,1)}, u32[]{:S(2)}) copy-start(bf16[1,2,3,12,192]{4,1,3,2,0:T(2,128)(2,1)} %copy-done) | copy-start | bytes 82948
  68.8 6.7 %copy-start.3 = (f32[2,6,12]{0,2,1:T(8,128)S(1)}, f32[2,6,12]{0,2,1:T(8,128)}, u32[]{:S(2)}) copy-start(f32[2,6,12]{0,2,1:T(8,128)} %copy-done.2) | copy-start | bytes 1732
  69.0 7.3 %copy-start.8 = (s32[12,12]{0,1:T(8,128)S(1)}, s32[12,12]{0,1:T(8,128)}, u32[]{:S(2)}) copy-start(s32[12,12]{0,1:T(8,128)} %copy-done.7) | copy-start | bytes 1732
  75.8 95.2 %copy-start.4 = (bf16[1,2,6,12,192]{4,1,3,2,0:T(2,128)(2,1)S(1)}, bf16[1,2,6,12,192]{4,1,3,2,0:T(2,128)(2,1)}, u32[]{:S(2)}) copy-start(bf16[1,2,6,12,192]{4,1,3,2,0:T(2,128)(2,1)} %param.7) | copy-start | bytes 165892
  83.4 88.4 %reduce-scatter.5.cloned.1.call-start = ((), (), s32[]{:S(2)}) async-start(), calls=%async_computation.3 | async-start | bytes 147456 | tf_op jit(solution)/shard_map/reduce_scatter | solution.py:195
  161.2 22.2 %reduce-scatter.3.cloned.1.call-start = ((), (), s32[]{:S(2)}) async-start(), calls=%async_computation.2 | async-start | bytes 442368 | tf_op jit(solution)/shard_map/reduce_scatter | solution.py:192
  161.5 5.9 %collective-permute-start.4 = (bf16[1,2,3,12,192]{4,3,2,1,0:T(8,128)(2,1)S(1)}, bf16[1,2,3,12,192]{4,3,2,1,0:T(8,128)(2,1)S(1)}, u32[]{:S(2)}, u32[]{:S(2)}) collective-permute-start(bf16[1,2,3,12,192]{4,3,2,1,0:T(8,128)(2,1)S(1)} %slice.103), channel_id=1, source_target_pairs={{0,2},{2,4},{4,6},{6,0},{1,3},{3,5},{5,7},{7,1},{8,10},{10,12},{12... | collective-permute-start | bytes 82952 | tf_op jit(solution)/shard_map/ppermute | solution.py:27
  167.4 3.6 %collective-permute-start.5 = (bf16[1,2,6,6,192]{4,3,2,1,0:T(8,128)(2,1)S(1)}, bf16[1,2,6,6,192]{4,3,2,1,0:T(8,128)(2,1)S(1)}, u32[]{:S(2)}, u32[]{:S(2)}) collective-permute-start(bf16[1,2,6,6,192]{4,3,2,1,0:T(8,128)(2,1)S(1)} %fusion.15), channel_id=1, source_target_pairs={{0,8},{8,16},{16,24},{24,0},{1,9},{9,17},{17,25},{25,1},{2,10},{10... | collective-permute-start | bytes 82952 | tf_op jit(solution)/shard_map/ppermute | solution.py:27
  (2 other events, 3.7 us)
Sparse Core Ops, SparseCore 0:
  83.5 51.0 all-reduce.5
Sparse Core Ops, SparseCore 1:
  161.3 7.5 reduce-scatter.4
  171.5 11.9 reduce-scatter.2
where the time goes:
time: 193 us
  blocking collectives  98.6 us (51%)
  local copies, waits for them, and re-layouts  29.6 us (15%)
  between operations  17.3 us (9%)
  matrix products  17 us (9%)
  waiting for transfers between devices  14.2 us (7%)
  other arithmetic  8 us (4%)
  starting transfers between devices  7.77 us (4%)
    psum x1, blocking collectives, body(): summed = lax.psum((grad_qkv_w, grad_proj, grad_gain), ('lon', 'lat'))  77.7 us
    another operation x2, local copies, waits for them, and re-layouts, window_grads(): scores = scores + bias_full[:, None]  16.6 us
    reduce_scatter x1, waiting for transfers between devices, body(): lax.psum_scatter(summed[0].astype(jnp.bfloat16), 'dp', scatter_dimension=...  10.2 us
    unnamed x2, blocking collectives  9.86 us
    ppermute x6, starting transfers between devices, passed_along(): return lax.ppermute(value, axis, pairs)  7.64 us
    all_gather x1, blocking collectives, body(): lax.all_gather(qkv_weight, 'dp', axis=0, tiled=True)  6.26 us
    dot_general x1, matrix products, gather_bias(): jnp.einsum('ghaubv,uvr->ghabr', shaped, onehot, precision=lax.Precision.H...  5.99 us
    another operation x2, local copies, waits for them, and re-layouts  5.3 us
  transfers between devices with their start and end apart: 9, of which 5 were waited for; matrix products, arithmetic and copies ran while one was open for 16% of the time, Pallas kernels for 0%

commit v1 on v0

v1 whole, which is shorter than its diff:
```python
import functools
import math

import jax
import jax.numpy as jnp
import numpy as np
from jax import lax
from jax.experimental import pallas as pl
from jax.experimental.pallas import tpu as pltpu
from jax.sharding import PartitionSpec as P

C = 192
H = 6
HD = 32
WZ = 2
WA = 6
WL = 12
SA = 3
SO = 6
WT = 144
POS = 3312
EPS = 1e-05
MASKED = -1e30

ROWS = WZ * WA
SPAN = 2 * WL - 1
QUAD = WZ * SA * 8
HALF = ROWS // 2 * SPAN
WIDE = 256
EXT = 2 * H * ROWS + 8
BF = jnp.bfloat16
F32 = jnp.float32
VMEM = pl.BlockSpec(memory_space=pltpu.VMEM)
SMEM = pl.BlockSpec(memory_space=pltpu.SMEM)


def token_order():
    order = np.zeros((WT, 4 * QUAD), np.float32)
    for z in range(WZ):
        for a in range(WA):
            for o in range(WL):
                south, east = a >= SA, o >= SO
                quadrant = 2 * south + east
                column = o - SO if east else o + 2
                row = (z * SA + a % SA) * 8 + column
                order[(z * WA + a) * WL + o, quadrant * QUAD + row] = 1.0
    return order


def matmul(a, b):
    return lax.dot_general(a, b, (((1,), (0,)), ((), ())), preferred_element_type=F32)


def matmul_t(a, b):
    return lax.dot_general(a, b, (((1,), (1,)), ((), ())), preferred_element_type=F32)


def over_12(index):
    return lax.shift_right_logical(index * 5462, 16)


def pack_kernel(tok, dy, east, south, corner):
    def strip(ref, rows, cols):
        part = ref[:, rows : rows + SA].astype(F32)
        return part[:, :, cols : cols + 8].reshape(QUAD, C).astype(BF)

    for index, ref in enumerate((tok, dy)):
        at = slice(index * QUAD, (index + 1) * QUAD)
        east[at] = strip(ref, SA, 0)
        south[at] = strip(ref, 0, 4)
        corner[at] = strip(ref, 0, 0)


def offsets(height, width, half):
    row = lax.broadcasted_iota(jnp.int32, (height, width), 0)
    col = lax.broadcasted_iota(jnp.int32, (height, width), 1)
    block = over_12(col)
    return row, block * SPAN - (col - block * WL) + WL - 1 - half


def bias_kernel(place, table, out):
    values = table[...]
    high = values.astype(BF)
    rest = values - high.astype(F32)
    middle = rest.astype(BF)
    low = (rest - middle.astype(F32)).astype(BF)
    stacked = jnp.concatenate([high, middle, low], axis=0)
    row, target = offsets(ROWS * SPAN, WIDE, 0)
    count = H * ROWS
    here = lax.broadcasted_iota(jnp.int32, (count, WIDE), 0)
    here = here - over_12(here) * ROWS
    there = over_12(lax.broadcasted_iota(jnp.int32, (count, WIDE), 1))

    def wrapped(index):
        return jnp.where(index >= WA, index - WA, index) >= SA

    crossing = jnp.logical_and(wrapped(here) != wrapped(there), place[2] > 0)
    for u in range(WL):
        onehot = jnp.where(row == target + u, 1.0, 0.0).astype(BF)
        spread = matmul(stacked, onehot)
        spread = spread[:count] + spread[count : 2 * count] + spread[2 * count :]
        spread = jnp.where(crossing, MASKED, spread)
        out[0, pl.ds(u, count, stride=WL), :] = spread[:, :128]
        out[1, pl.ds(u, count, stride=WL), :] = spread[:, 128:]


def main_kernel(
    parts, place, tok, dy, east, south, corner, bias, order, order_t, *refs
):
    dense = refs[:parts]
    send, keep, extra, quads, qkv_w, proj_w, sums, scores_grad = refs[parts:]
    n_qkv, n_proj = 3 * C // parts, C // parts
    gain = None
    for k in range(parts):
        at = lax.rem(place[0] + k, parts)
        qkv_w[pl.ds(pl.multiple_of(at * n_qkv, 16), n_qkv), :] = dense[k][:n_qkv]
        proj_w[pl.ds(pl.multiple_of(at * n_proj, 16), n_proj), :] = dense[k][n_qkv : n_qkv + n_proj]
        term = dense[k][n_qkv + n_proj : n_qkv + n_proj + 8].astype(F32)[:1]
        gain = term if gain is None else gain + term

    def own(ref):
        part = ref[:, SA:].astype(F32)
        return part[:, :, 4:12].reshape(QUAD, C).astype(BF)

    def window(ref, index):
        at = slice(index * QUAD, (index + 1) * QUAD)
        return jnp.concatenate([own(ref), east[at], south[at], corner[at]], axis=0)

    x = matmul(order[...], window(tok, 0))
    dyw = matmul(order[...], window(dy, 1)).astype(BF)
    average = jnp.sum(x, axis=-1, keepdims=True) * (1.0 / C)
    centred = x - average
    variance = jnp.sum(centred * centred, axis=-1, keepdims=True) * (1.0 / C)
    inverse = lax.rsqrt(variance + EPS)
    unit = centred * inverse
    normed = (unit * gain).astype(BF)
    qkv_t = matmul_t(qkv_w[...], normed).astype(BF)
    query = matmul_t(normed, qkv_w[:C]).astype(BF)
    grad_att32 = matmul(dyw, proj_w[...]).astype(BF).astype(F32)
    grad_att = grad_att32.astype(BF)
    grad_att_t = grad_att32.T.astype(BF)
    dy_t = dyw.astype(F32).T.astype(BF)
    scale = 1.0 / math.sqrt(HD)

    def alone(part, head):
        pieces = []
        if head:
            pieces.append(jnp.zeros((head * HD, WT), BF))
        pieces.append(part)
        if head < H - 1:
            pieces.append(jnp.zeros(((H - 1 - head) * HD, WT), BF))
        return jnp.concatenate(pieces, axis=0)

    def both(ref, at):
        rows = slice(at, at + WT)
        return jnp.concatenate([ref[0, rows], ref[1, rows, : WT - 128]], axis=1)

    attended_t, grad_q, grad_k, grad_v = [], [], [], []
    for head in range(H):
        at = head * HD
        q_t = qkv_t[at : at + HD]
        k_t = qkv_t[C + at : C + at + HD]
        v_t = qkv_t[2 * C + at : 2 * C + at + HD]
        scores = matmul(query, alone(k_t, head)) * scale + both(bias, head * WT)
        expo = jnp.exp(scores - jnp.max(scores, axis=-1, keepdims=True))
        probs = expo * (1.0 / jnp.sum(expo, axis=-1, keepdims=True))
        probs_low = probs.astype(BF)
        attended_t.append(matmul_t(v_t, probs_low))
        grad_probs = matmul(grad_att, alone(v_t, head))
        grad_v.append(matmul(grad_att_t[at : at + HD], probs_low))
        mean = jnp.sum(probs * grad_probs, axis=-1, keepdims=True)
        grad_scores = probs * (grad_probs - mean)
        scores_grad[0, head * WT : (head + 1) * WT] = grad_scores[:, :128]
        scores_grad[1, head * WT : (head + 1) * WT, : WT - 128] = grad_scores[:, 128:]
        scores_low = grad_scores.astype(BF)
        grad_q.append(matmul_t(k_t, scores_low) * scale)
        grad_k.append(matmul(q_t, scores_low) * scale)
    grad_qkv_t32 = jnp.concatenate(grad_q + grad_k + grad_v, axis=0)
    grad_qkv_t = grad_qkv_t32.astype(BF)
    grad_qkv_w = matmul(grad_qkv_t, normed)
    grad_proj = matmul_t(dy_t, jnp.concatenate(attended_t, axis=0).astype(BF))
    each = n_qkv + n_proj
    for k in range(parts):
        sums[k * each : k * each + n_qkv] = grad_qkv_w[k * n_qkv : (k + 1) * n_qkv]
        sums[k * each + n_qkv : (k + 1) * each] = grad_proj[k * n_proj : (k + 1) * n_proj]
    for k in range(parts):
        mine = k * each + place[1] * (each // 2)
        other = k * each + (1 - place[1]) * (each // 2)
        rows = slice(k * (each // 2), (k + 1) * (each // 2))
        keep[rows] = sums[pl.ds(pl.multiple_of(mine, 16), each // 2), :]
        send[rows] = sums[pl.ds(pl.multiple_of(other, 16), each // 2), :].astype(BF)

    grad_qkv = grad_qkv_t32.T.astype(BF)
    grad_normed = matmul(grad_qkv, qkv_w[...])
    grad_gain = jnp.sum(grad_normed * unit, axis=0, keepdims=True)
    scaled = grad_normed * gain
    first = jnp.sum(scaled, axis=-1, keepdims=True) * (1.0 / C)
    second = jnp.sum(scaled * unit, axis=-1, keepdims=True) * (1.0 / C)
    grad_x = inverse * (scaled - first - unit * second)
    quads[...] = matmul(order_t[...], grad_x.astype(BF)).astype(BF)

    count = H * ROWS
    for half in range(2):
        row, target = offsets(C, WT, half * HALF)
        target = jnp.where(row < HALF, target, -WT)
        total = jnp.zeros((count, C), F32)
        for u in range(WL):
            onehot = jnp.where(row == target + u, 1.0, 0.0).astype(BF)
            rows = pl.ds(u, count, stride=WL)
            wide = jnp.concatenate(
                [scores_grad[0, rows, :], scores_grad[1, rows, :][:, : WT - 128]], axis=1
            )
            total += matmul_t(wide.astype(BF), onehot)
        extra[half * count : (half + 1) * count] = total.astype(BF)
    extra[2 * count : EXT] = jnp.broadcast_to(grad_gain, (8, C)).astype(BF)


def finish_kernel(dy, quad, south, lon_halo, out):
    def low(ref, at):
        value = ref[at : at + QUAD].astype(F32).reshape(WZ, SA, 8, C)
        return jnp.concatenate([value, jnp.zeros((WZ, SA, 4, C), F32)], axis=2)

    def high(ref, at):
        value = ref[at : at + QUAD].astype(F32).reshape(WZ, SA, 8, C)
        return jnp.concatenate([jnp.zeros((WZ, SA, 4, C), F32), value], axis=2)

    upper = dy[:, :SA].astype(F32) + low(lon_halo, QUAD) + high(south, 0)
    lower = dy[:, SA:].astype(F32) + low(lon_halo, 0) + high(quad, 0)
    out[:, :SA] = upper.astype(BF)
    out[:, SA:] = lower.astype(BF)


def call(kernel, outs, scratch=(), specs=None, flops=1000000, nbytes=1000000):
    return pl.pallas_call(
        kernel,
        out_shape=outs,
        in_specs=specs,
        out_specs=jax.tree.map(lambda _: VMEM, outs),
        scratch_shapes=list(scratch),
        compiler_params=pltpu.CompilerParams(vmem_limit_bytes=40 << 20),
        cost_estimate=pl.CostEstimate(flops=flops, bytes_accessed=nbytes, transcendentals=0),
    )


def shaped(rows, cols, dtype):
    return jax.ShapeDtypeStruct((rows, cols), dtype)


def exchanged(value, axis, flip):
    count = lax.axis_size(axis)
    return lax.ppermute(value, axis, [(i, i ^ flip) for i in range(count)])


def passed_along(value, axis, steps):
    count = lax.axis_size(axis)
    return lax.ppermute(value, axis, [(i, (i + steps) % count) for i in range(count)])


def passed_diagonally(value, steps):
    rows, cols = lax.axis_size("lon"), lax.axis_size("lat")
    pairs = [
        (i * cols + j, ((i + steps) % rows) * cols + (j + steps) % cols)
        for i in range(rows)
        for j in range(cols)
    ]
    return lax.ppermute(value, ("lon", "lat"), pairs)


def body(tokens, grad_out, qkv_weight, proj_weight, norm_gain, bias_table):
    parts = lax.axis_size("dp")
    dp, lon, lat = lax.axis_index("dp"), lax.axis_index("lon"), lax.axis_index("lat")
    lon_count, lat_count = lax.axis_size("lon"), lax.axis_size("lat")
    n_qkv, n_proj = 3 * C // parts, C // parts
    each = n_qkv + n_proj
    half = each // 2
    side = (lon ^ (lon >> 1)) & 1
    place = jnp.stack([dp, side, lat == lat_count - 1]).astype(jnp.int32)
    tok = tokens.reshape(WZ, WA, WL, C)
    dy = grad_out.reshape(WZ, WA, WL, C)

    gain_row = lax.dynamic_update_slice(jnp.zeros((C,), BF), norm_gain, (dp * n_proj,))
    dense = jnp.concatenate(
        [qkv_weight, proj_weight, jnp.broadcast_to(gain_row, (8, C))], axis=0
    )
    strips = [shaped(2 * QUAD, C, BF)] * 3
    east, south, corner = call(pack_kernel, strips, specs=[VMEM] * 2)(tok, dy)
    gathered = [dense] + [passed_along(dense, "dp", -k) for k in range(1, parts)]
    east = passed_along(east, "lon", -1)
    south = passed_along(south, "lat", -1)
    corner = passed_diagonally(corner, -1)
    bias = call(bias_kernel, jax.ShapeDtypeStruct((2, H * WT, 128), F32), specs=[SMEM, VMEM], flops=200000000)(
        place, bias_table.reshape(H * ROWS, ROWS * SPAN)
    )
    order = token_order()
    outs = [
        shaped(parts * half, C, BF),
        shaped(parts * half, C, F32),
        shaped(EXT, C, BF),
        shaped(4 * QUAD, C, BF),
    ]
    scratch = [
        pltpu.VMEM((3 * C, C), BF),
        pltpu.VMEM((C, C), BF),
        pltpu.VMEM((4 * C, C), F32),
        pltpu.VMEM((2, H * WT, 128), F32),
    ]
    send, keep, extra, quads = call(
        functools.partial(main_kernel, parts), outs, scratch, specs=[SMEM] + [VMEM] * (8 + parts)
    )(
        place, tok, dy, east, south, corner, bias,
        jnp.asarray(order, BF), jnp.asarray(order.T, BF), *gathered,
    )
    if (lon_count, lat_count, parts) == (4, 4, 2):
        first = keep + exchanged(send, "lon", 1).astype(F32)
        mine = lax.dynamic_slice_in_dim(first, dp * half, half)
        theirs = lax.dynamic_slice_in_dim(first, (1 - dp) * half, half).astype(BF)
        got = exchanged(jnp.concatenate([theirs, extra]), "dp", 1)
        dense_sum = (mine + got[:half].astype(F32)).astype(BF)
        extra = extra + got[half:]
        dense_sum = jnp.concatenate([dense_sum, extra[2 * H * ROWS :]])
        extra = extra[: 2 * H * ROWS]
        full = half + 8
        south_quads = quads[2 * QUAD :]
        got = exchanged(jnp.concatenate([dense_sum, south_quads]), "lat", 1)
        dense_sum = dense_sum + got[:full]
        south_halo = got[full:]
        got = exchanged(jnp.concatenate([dense_sum, south_quads]), "lat", 3)
        dense_sum = dense_sum + got[:full]
        south_halo = jnp.where(lat % 2 == 1, south_halo, got[full:])
        east_quads = jnp.concatenate([quads[QUAD : 2 * QUAD], south_halo[QUAD:]])
        got = exchanged(jnp.concatenate([dense_sum, extra, east_quads]), "lon", 3)
        dense_sum = dense_sum + got[:full]
        extra = extra + got[full : half + EXT]
        east_halo = got[half + EXT :]
        got = exchanged(jnp.concatenate([dense_sum, extra, east_quads]), "lon", 1)
        extra = extra.astype(F32) + got[full : half + EXT].astype(F32)
        east_halo = jnp.where(lon % 2 == 1, got[half + EXT :], east_halo)
        gain_sum = dense_sum[half].astype(F32) + got[half].astype(F32)
        dense_sum = dense_sum[:half]
        gain_sum = lax.dynamic_slice_in_dim(gain_sum, dp * n_proj, n_proj)
        total = jnp.where(
            side == 0,
            jnp.concatenate([dense_sum, got[:half]]),
            jnp.concatenate([got[:half], dense_sum]),
        ).astype(F32)
    else:
        paired = jnp.stack([keep.reshape(parts, half, C), send.reshape(parts, half, C).astype(F32)])
        paired = jnp.where(side == 0, paired, paired[::-1])
        dense_sum = paired.transpose(1, 0, 2, 3).reshape(parts * each, C)
        dense_sum = lax.psum(dense_sum, ("lon", "lat"))
        total = lax.psum_scatter(dense_sum, "dp", scatter_dimension=0, tiled=True)
        extra = extra.astype(F32)
        gain_sum = lax.psum(extra[2 * H * ROWS], ("lon", "lat"))
        gain_sum = lax.psum_scatter(gain_sum, "dp", scatter_dimension=0, tiled=True)
        extra = lax.psum(extra, ("lon", "dp"))
        south_halo = passed_along(quads[2 * QUAD :], "lat", 1)
        east_halo = passed_along(
            jnp.concatenate([quads[QUAD : 2 * QUAD], south_halo[QUAD:]]), "lon", 1
        )
    count = H * ROWS
    table = jnp.concatenate([extra[:count, :HALF], extra[count : 2 * count, :HALF]], axis=1)
    grad_tokens = call(
        finish_kernel, jax.ShapeDtypeStruct((WZ, WA, WL, C), BF), specs=[VMEM] * 4
    )(dy, quads, south_halo, east_halo)
    return (
        grad_tokens.reshape(tokens.shape),
        total[:n_qkv],
        total[n_qkv:],
        gain_sum,
        table.reshape(1, H, POS),
    )


def solution(mesh):
    spec = P("dp", None, "lat", "lon", None)
    return jax.shard_map(
        body,
        mesh=mesh,
        in_specs=(spec, spec, P("dp", None), P("dp", None), P("dp"), P("lat", None, None)),
        out_specs=(spec, P("dp", None), P("dp", None), P("dp"), P("lat", None, None)),
        check_vma=False,
    )
```

time: 193 us -> 54.4 us (0.28)
  blocking collectives: 98.6 us -> 0 us
  local copies, waits for them, and re-layouts: 29.6 us -> 5.3 us
  matrix products: 17 us -> 0 us
  between operations: 17.3 us -> 0.97 us
  waiting for transfers between devices: 14.2 us -> 26.3 us
  Pallas kernels: 0 us -> 6.71 us
  other arithmetic: 8 us -> 2.35 us
  starting transfers between devices: 7.77 us -> 12.6 us
    psum x1 -> x0, blocking collectives: 77.7 us -> none  [body(): summed = lax.psum((grad_qkv_w, grad_proj, grad_gain), ('lon', 'lat'))]
    ppermute x6 -> x10, waiting for transfers between devices: 3.91 us -> 26.3 us  [the longest x6 25.3 us: exchanged(): return lax.ppermute(value, axis, [(i, i ^ flip) for i in range(count)])]
    another operation x6 -> x0, local copies, waits for them, and re-layouts: 22 us -> none  [the longest x2 16.6 us: window_grads(): scores = scores + bias_full[:, None]]
    dot_general x13 -> x0, matrix products: 17 us -> none  [the longest x1 5.99 us: gather_bias(): jnp.einsum('ghaubv,uvr->ghabr', shaped, onehot, precision=lax.Precision.H...]
    all_gather x2 -> x0, blocking collectives: 11 us -> none  [the longest x1 6.26 us: body(): lax.all_gather(qkv_weight, 'dp', axis=0, tiled=True)]
    reduce_scatter x2 -> x0, waiting for transfers between devices: 10.2 us -> none  [the longest x1 10.2 us: body(): lax.psum_scatter(summed[0].astype(jnp.bfloat16), 'dp', scatter_dimension=...]
    unnamed x2 -> x0, blocking collectives: 9.86 us -> none
    pallas_call x0 -> x4, Pallas kernels: none -> 6.71 us  [the longest x1 5.08 us: body(): call(functools.partial(main_kernel, parts), outs, scratch, specs=[SMEM] +...]
  transfers between devices with their start and end apart: 9 -> 10, of which waited for: 5 -> 7; matrix products, arithmetic and copies ran while one was open for 16% -> 1% of each run, Pallas kernels for 0% -> 3%
where the time goes in v1:
time: 54.4 us; the launch traced here: 54.2 us
  waiting for transfers between devices  26.3 us (48%)
  starting transfers between devices  12.6 us (23%)
  Pallas kernels  6.71 us (12%)
  local copies, waits for them, and re-layouts  5.3 us (10%)
  other arithmetic  2.35 us (4%)
  between operations  0.97 us (2%)
    ppermute x6, waiting for transfers between devices, exchanged(): return lax.ppermute(value, axis, [(i, i ^ flip) for i in range(count)])  25.3 us
    ppermute x3, starting transfers between devices, passed_along(): lax.ppermute(value, axis, [(i, (i + steps) % count) for i in range(count)])  7.34 us
    pallas_call x1, Pallas kernels, body(): call(functools.partial(main_kernel, parts), outs, scratch, specs=[SMEM] +...  5.08 us
    ppermute x6, starting transfers between devices, exchanged(): return lax.ppermute(value, axis, [(i, i ^ flip) for i in range(count)])  4.67 us
    unnamed x19, local copies, waits for them, and re-layouts  1.85 us
    pallas_call x1, Pallas kernels, body(): call(bias_kernel, jax.ShapeDtypeStruct((2, H * WT, 128), F32), specs=[SME...  1.56 us
  transfers between devices with their start and end apart: 10, of which 7 were waited for; matrix products, arithmetic and copies ran while one was open for 1% of the time, Pallas kernels for 3%

profile of v1, /device:TPU:0, one launch (start us, length us, event | category | flops | bytes accessed | tf_op | source)
XLA Modules:
  0.0 54.2 jit_solution(4374472211484819064)
XLA Ops:
  0.7 0.6 %copy-done.8 = bf16[96]{0:T(256)(128)(2,1)S(1)} copy-done((bf16[96]{0:T(256)(128)(2,1)S(1)}, bf16[96]{0:T(256)(128)(2,1)}, u32[]{:S(2)}) %copy-start.8) | copy-done | bytes 216
  1.5 1.0 %pad_maximum_fusion.4.refs_0_ = bf16[392,192]{1,0:T(8,128)(2,1)S(1)} fusion(bf16[8,192]{1,0:T(8,128)(2,1)S(1)} %broadcast_in_dim.7, bf16[96,192]{1,0:T(8,128)(2,1)} %param.11, bf16[288,192]{1,0:T(8,128)(2,1)} %param.10), kind=kLoop, calls=%fused_computation.5 | loop fusion | flops 451584 | bytes 301056 | tf_op jit(solution)/shard_map/concatenate | solution.py:282
  2.5 3.0 %collective-permute-start.3 = (bf16[392,192]{1,0:T(8,128)(2,1)S(1)}, bf16[392,192]{1,0:T(8,128)(2,1)S(1)}, u32[]{:S(2)}, u32[]{:S(2)}) collective-permute-start(bf16[392,192]{1,0:T(8,128)(2,1)S(1)} %pad_maximum_fusion.4.refs_0_), channel_id=1, source_target_pairs={{0,1},{1,0},{2,3},{3,2},{4,5},{5,4},{6,7},{7,6},{8,9},{9,8},{10,11... | collective-permute-start | bytes 451592 | tf_op jit(solution)/shard_map/ppermute | solution.py:256
  5.6 0.7 %collective-permute-start = (bf16[96,192]{1,0:T(8,128)(2,1)S(1)}, bf16[96,192]{1,0:T(8,128)(2,1)S(1)}, u32[]{:S(2)}, u32[]{:S(2)}) collective-permute-start(bf16[96,192]{1,0:T(8,128)(2,1)S(1)} %get-tuple-element.12), channel_id=1, source_target_pairs={{0,24},{8,0},{16,8},{24,16},{1,25},{9,1},{17,9},{25,17},{2,26},{10... | collective-permute-start | bytes 110600 | tf_op jit(solution)/shard_map/ppermute | solution.py:256
  6.3 3.6 %collective-permute-start.1 = (bf16[96,192]{1,0:T(8,128)(2,1)S(1)}, bf16[96,192]{1,0:T(8,128)(2,1)S(1)}, u32[]{:S(2)}, u32[]{:S(2)}) collective-permute-start(bf16[96,192]{1,0:T(8,128)(2,1)S(1)} %get-tuple-element.13), channel_id=1, source_target_pairs={{0,6},{2,0},{4,2},{6,4},{1,7},{3,1},{5,3},{7,5},{8,14},{10,8},{12,... | collective-permute-start | bytes 110600 | tf_op jit(solution)/shard_map/ppermute | solution.py:256
  9.9 0.6 %collective-permute-start.2 = (bf16[96,192]{1,0:T(8,128)(2,1)S(1)}, bf16[96,192]{1,0:T(8,128)(2,1)S(1)}, u32[]{:S(2)}, u32[]{:S(2)}) collective-permute-start(bf16[96,192]{1,0:T(8,128)(2,1)S(1)} %get-tuple-element.14), channel_id=1, source_target_pairs={{0,30},{2,24},{4,26},{6,28},{8,6},{10,0},{12,2},{14,4},{16,14},{18... | collective-permute-start | bytes 110600 | tf_op jit(solution)/shard_map/ppermute | solution.py:266
  10.9 1.6 %shard_map.120.bias = f32[2,864,128]{2,1,0:T(8,128)S(1)} custom-call(s32[3]{0:T(128)S(1)} %pad_add_fusion.place, f32[72,276]{1,0:T(8,128)S(1)} %reshape.31.table), custom_call_target="tpu_custom_call" | custom-call | flops 200000000 | bytes 1000000 | tf_op jit(solution)/shard_map/pallas_call | solution.py:291
  12.5 0.9 %collective-permute-done.2.corner = bf16[96,192]{1,0:T(8,128)(2,1)S(1)} collective-permute-done((bf16[96,192]{1,0:T(8,128)(2,1)S(1)}, bf16[96,192]{1,0:T(8,128)(2,1)S(1)}, u32[]{:S(2)}, u32[]{:S(2)}) %collective-permute-start.2) | collective-permute-done | bytes 36896 | tf_op jit(solution)/shard_map/ppermute | solution.py:266
  13.4 5.1 %shard_map.121 = (bf16[384,192]{1,0:T(8,128)(2,1)S(1)}, f32[384,192]{1,0:T(8,128)S(1)}, bf16[152,192]{1,0:T(8,128)(2,1)S(1)}, bf16[192,192]{1,0:T(8,128)(2,1)S(1)}) custom-call(s32[3]{0:T(128)S(1)} %pad_add_fusion.place, bf16[2,6,12,192]{3,2,1,0:T(8,128)(2,1)S(1)} %get-tuple-element.31.tok, bf16[2,6,12,192]{3,2,1,0:T(8,128)(2,1)S(1)} %get-tuple-element.32.dy, ...), custom_call_target="tpu_custom_call" | custom-call | flops 1000000 | bytes 1000000 | tf_op jit(solution)/shard_map/pallas_call | solution.py:307
  18.5 0.8 %collective-permute-start.4 = (bf16[384,192]{1,0:T(8,128)(2,1)S(1)}, bf16[384,192]{1,0:T(8,128)(2,1)S(1)}, u32[]{:S(2)}, u32[]{:S(2)}) collective-permute-start(bf16[384,192]{1,0:T(8,128)(2,1)S(1)} %get-tuple-element.17), channel_id=1, source_target_pairs={{0,8},{8,0},{16,24},{24,16},{1,9},{9,1},{17,25},{25,17},{2,10},{10... | collective-permute-start | bytes 442376 | tf_op jit(solution)/shard_map/ppermute | solution.py:251
  19.3 1.1 %collective-permute-done.4 = bf16[384,192]{1,0:T(8,128)(2,1)S(1)} collective-permute-done((bf16[384,192]{1,0:T(8,128)(2,1)S(1)}, bf16[384,192]{1,0:T(8,128)(2,1)S(1)}, u32[]{:S(2)}, u32[]{:S(2)}) %collective-permute-start.4) | collective-permute-done | bytes 147488 | tf_op jit(solution)/shard_map/ppermute | solution.py:251
  20.5 0.6 %collective-permute-start.5 = (bf16[344,192]{1,0:T(8,128)(2,1)S(1)}, bf16[344,192]{1,0:T(8,128)(2,1)S(1)}, u32[]{:S(2)}, u32[]{:S(2)}) collective-permute-start(bf16[344,192]{1,0:T(8,128)(2,1)S(1)} %pad_maximum_fusion.7), channel_id=1, source_target_pairs={{0,1},{1,0},{2,3},{3,2},{4,5},{5,4},{6,7},{7,6},{8,9},{9,8},{10,11... | collective-permute-start | bytes 396296 | tf_op jit(solution)/shard_map/ppermute | solution.py:251
  21.1 6.2 %collective-permute-done.5 = bf16[344,192]{1,0:T(8,128)(2,1)S(1)} collective-permute-done((bf16[344,192]{1,0:T(8,128)(2,1)S(1)}, bf16[344,192]{1,0:T(8,128)(2,1)S(1)}, u32[]{:S(2)}, u32[]{:S(2)}) %collective-permute-start.5) | collective-permute-done | bytes 132128 | tf_op jit(solution)/shard_map/ppermute | solution.py:251
  27.6 5.3 %collective-permute-done.6 = bf16[296,192]{1,0:T(8,128)(2,1)S(1)} collective-permute-done((bf16[296,192]{1,0:T(8,128)(2,1)S(1)}, bf16[296,192]{1,0:T(8,128)(2,1)S(1)}, u32[]{:S(2)}, u32[]{:S(2)}) %collective-permute-start.6) | collective-permute-done | bytes 113696 | tf_op jit(solution)/shard_map/ppermute | solution.py:251
  32.9 3.0 %collective-permute-start.7 = (bf16[296,192]{1,0:T(8,128)(2,1)S(1)}, bf16[296,192]{1,0:T(8,128)(2,1)S(1)}, u32[]{:S(2)}, u32[]{:S(2)}) collective-permute-start(bf16[296,192]{1,0:T(8,128)(2,1)S(1)} %pad_maximum_fusion.5), channel_id=1, source_target_pairs={{0,6},{2,4},{4,2},{6,0},{1,7},{3,5},{5,3},{7,1},{8,14},{10,12},{12... | collective-permute-start | bytes 341000 | tf_op jit(solution)/shard_map/ppermute | solution.py:251
  35.9 4.2 %collective-permute-done.7 = bf16[296,192]{1,0:T(8,128)(2,1)S(1)} collective-permute-done((bf16[296,192]{1,0:T(8,128)(2,1)S(1)}, bf16[296,192]{1,0:T(8,128)(2,1)S(1)}, u32[]{:S(2)}, u32[]{:S(2)}) %collective-permute-start.7) | collective-permute-done | bytes 113696 | tf_op jit(solution)/shard_map/ppermute | solution.py:251
  40.1 0.9 %slice-done.1 = bf16[144,192]{1,0:T(8,128)(2,1)S(1)} async-done(((bf16[152,192]{1,0:T(8,128)(2,1)}), bf16[144,192]{1,0:T(8,128)(2,1)S(1)}, s32[]{:S(2)}) %slice-start.1) | async-done | bytes 55320 | tf_op jit(solution)/shard_map/slice | solution.py:321
  41.1 7.6 %collective-permute-done.8 = bf16[440,192]{1,0:T(8,128)(2,1)S(1)} collective-permute-done((bf16[440,192]{1,0:T(8,128)(2,1)S(1)}, bf16[440,192]{1,0:T(8,128)(2,1)S(1)}, u32[]{:S(2)}, u32[]{:S(2)}) %collective-permute-start.8) | collective-permute-done | bytes 168992 | tf_op jit(solution)/shard_map/ppermute | solution.py:251
  49.4 1.0 %collective-permute-done.9 = bf16[440,192]{1,0:T(8,128)(2,1)S(1)} collective-permute-done((bf16[440,192]{1,0:T(8,128)(2,1)S(1)}, bf16[440,192]{1,0:T(8,128)(2,1)S(1)}, u32[]{:S(2)}, u32[]{:S(2)}) %collective-permute-start.9) | collective-permute-done | bytes 168992 | tf_op jit(solution)/shard_map/ppermute | solution.py:251
  50.5 0.7 %slice.112 = f32[288,192]{1,0:T(8,128)} slice(f32[384,192]{1,0:T(8,128)S(1)} %fusion), slice={[0:288], [0:192]} | slice | bytes 442368 | tf_op jit(solution)/shard_map/slice | solution.py:367
  51.2 0.6 %slice.113 = f32[96,192]{1,0:T(8,128)} slice(f32[384,192]{1,0:T(8,128)S(1)} %fusion), slice={[288:384], [0:192]} | slice | bytes 147456 | tf_op jit(solution)/shard_map/slice | solution.py:368
  52.0 0.8 %reshape.35 = f32[1,6,3312]{2,0,1:T(1,128)} reshape(f32[72,276]{1,0:T(8,128)S(1)} %pad_maximum_fusion.8) | data formatting | bytes 158976 | tf_op jit(solution)/shard_map/reshape | solution.py:370
  52.9 0.7 %copy.19 = bf16[1,2,6,12,192]{4,1,3,2,0:T(2,128)(2,1)} copy(bf16[1,2,6,12,192]{4,3,2,1,0:T(8,128)(2,1)S(1)} %bitcast.10) | data formatting | bytes 110592
  53.6 0.6 %fusion.3 = f32[96]{0:T(128)} fusion(bf16[1,192]{1,0:T(2,128)(2,1)S(1)} %slice.115, s32[]{:T(128)S(6)} %select_n.43, bf16[1,192]{1,0:T(2,128)(2,1)S(1)} %slice.114), kind=kLoop, calls=%fused_computation.28 | loop fusion | flops 288 | bytes 772 | tf_op jit(solution)/shard_map/dynamic_slice | solution.py:340
  (61 shorter events, 2.1 us)
Async XLA Ops:
  0.6 0.7 %copy-start.8 = (bf16[96]{0:T(256)(128)(2,1)S(1)}, bf16[96]{0:T(256)(128)(2,1)}, u32[]{:S(2)}) copy-start(bf16[96]{0:T(256)(128)(2,1)} %param.12) | copy-start | bytes 580
  1.5 4.0 %copy-start.6 = (bf16[1,2,6,12,192]{4,1,3,2,0:T(2,128)(2,1)S(1)}, bf16[1,2,6,12,192]{4,1,3,2,0:T(2,128)(2,1)}, u32[]{:S(2)}) copy-start(bf16[1,2,6,12,192]{4,1,3,2,0:T(2,128)(2,1)} %param.8) | copy-start | bytes 165892
  1.5 4.0 %copy-start.7 = (bf16[1,2,6,12,192]{4,1,3,2,0:T(2,128)(2,1)S(1)}, bf16[1,2,6,12,192]{4,1,3,2,0:T(2,128)(2,1)}, u32[]{:S(2)}) copy-start(bf16[1,2,6,12,192]{4,1,3,2,0:T(2,128)(2,1)} %param.9) | copy-start | bytes 165892
  2.5 10.9 %collective-permute-start.3 = (bf16[392,192]{1,0:T(8,128)(2,1)S(1)}, bf16[392,192]{1,0:T(8,128)(2,1)S(1)}, u32[]{:S(2)}, u32[]{:S(2)}) collective-permute-start(bf16[392,192]{1,0:T(8,128)(2,1)S(1)} %pad_maximum_fusion.4.refs_0_), channel_id=1, source_target_pairs={{0,1},{1,0},{2,3},{3,2},{4,5},{5,4},{6,7},{7,6},{8,9},{9,8},{10,11... | collective-permute-start | bytes 451592 | tf_op jit(solution)/shard_map/ppermute | solution.py:256
  5.5 5.0 %copy-start.5 = (f32[1,6,3312]{2,0,1:T(1,128)S(1)}, f32[1,6,3312]{2,0,1:T(1,128)}, u32[]{:S(2)}) copy-start(f32[1,6,3312]{2,0,1:T(1,128)} %param.13) | copy-start | bytes 238468
  5.6 6.9 %collective-permute-start = (bf16[96,192]{1,0:T(8,128)(2,1)S(1)}, bf16[96,192]{1,0:T(8,128)(2,1)S(1)}, u32[]{:S(2)}, u32[]{:S(2)}) collective-permute-start(bf16[96,192]{1,0:T(8,128)(2,1)S(1)} %get-tuple-element.12), channel_id=1, source_target_pairs={{0,24},{8,0},{16,8},{24,16},{1,25},{9,1},{17,9},{25,17},{2,26},{10... | collective-permute-start | bytes 110600 | tf_op jit(solution)/shard_map/ppermute | solution.py:256
  6.3 6.2 %collective-permute-start.1 = (bf16[96,192]{1,0:T(8,128)(2,1)S(1)}, bf16[96,192]{1,0:T(8,128)(2,1)S(1)}, u32[]{:S(2)}, u32[]{:S(2)}) collective-permute-start(bf16[96,192]{1,0:T(8,128)(2,1)S(1)} %get-tuple-element.13), channel_id=1, source_target_pairs={{0,6},{2,0},{4,2},{6,4},{1,7},{3,1},{5,3},{7,5},{8,14},{10,8},{12,... | collective-permute-start | bytes 110600 | tf_op jit(solution)/shard_map/ppermute | solution.py:256
  9.9 3.5 %collective-permute-start.2 = (bf16[96,192]{1,0:T(8,128)(2,1)S(1)}, bf16[96,192]{1,0:T(8,128)(2,1)S(1)}, u32[]{:S(2)}, u32[]{:S(2)}) collective-permute-start(bf16[96,192]{1,0:T(8,128)(2,1)S(1)} %get-tuple-element.14), channel_id=1, source_target_pairs={{0,30},{2,24},{4,26},{6,28},{8,6},{10,0},{12,2},{14,4},{16,14},{18... | collective-permute-start | bytes 110600 | tf_op jit(solution)/shard_map/ppermute | solution.py:266
  10.9 2.6 %copy-start = (bf16[192,144]{1,0:T(8,128)(2,1)S(1)}, bf16[192,144]{1,0:T(8,128)(2,1)}, u32[]{:S(2)}) copy-start(bf16[192,144]{1,0:T(8,128)(2,1)} %constant.46.clone.order_t) | copy-start | bytes 165892
  10.9 2.6 %copy-start.1 = (bf16[144,192]{1,0:T(8,128)(2,1)S(1)}, bf16[144,192]{1,0:T(8,128)(2,1)}, u32[]{:S(2)}) copy-start(bf16[144,192]{1,0:T(8,128)(2,1)} %constant.45.clone.order) | copy-start | bytes 165892
  18.5 1.8 %collective-permute-start.4 = (bf16[384,192]{1,0:T(8,128)(2,1)S(1)}, bf16[384,192]{1,0:T(8,128)(2,1)S(1)}, u32[]{:S(2)}, u32[]{:S(2)}) collective-permute-start(bf16[384,192]{1,0:T(8,128)(2,1)S(1)} %get-tuple-element.17), channel_id=1, source_target_pairs={{0,8},{8,0},{16,24},{24,16},{1,9},{9,1},{17,25},{25,17},{2,10},{10... | collective-permute-start | bytes 442376 | tf_op jit(solution)/shard_map/ppermute | solution.py:251
  20.5 6.8 %collective-permute-start.5 = (bf16[344,192]{1,0:T(8,128)(2,1)S(1)}, bf16[344,192]{1,0:T(8,128)(2,1)S(1)}, u32[]{:S(2)}, u32[]{:S(2)}) collective-permute-start(bf16[344,192]{1,0:T(8,128)(2,1)S(1)} %pad_maximum_fusion.7), channel_id=1, source_target_pairs={{0,1},{1,0},{2,3},{3,2},{4,5},{5,4},{6,7},{7,6},{8,9},{9,8},{10,11... | collective-permute-start | bytes 396296 | tf_op jit(solution)/shard_map/ppermute | solution.py:251
  27.3 8.6 %copy-start.3 = (bf16[152,192]{1,0:T(8,128)(2,1)}, bf16[152,192]{1,0:T(8,128)(2,1)S(1)}, u32[]{:S(2)}) copy-start(bf16[152,192]{1,0:T(8,128)(2,1)S(1)} %slice_add_fusion.3) | copy-start | bytes 175108
  27.4 5.5 %collective-permute-start.6 = (bf16[296,192]{1,0:T(8,128)(2,1)S(1)}, bf16[296,192]{1,0:T(8,128)(2,1)S(1)}, u32[]{:S(2)}, u32[]{:S(2)}) collective-permute-start(bf16[296,192]{1,0:T(8,128)(2,1)S(1)} %pad_maximum_fusion.6), channel_id=1, source_target_pairs={{0,2},{2,0},{4,6},{6,4},{1,3},{3,1},{5,7},{7,5},{8,10},{10,8},{12,... | collective-permute-start | bytes 341000 | tf_op jit(solution)/shard_map/ppermute | solution.py:251
  32.9 7.2 %collective-permute-start.7 = (bf16[296,192]{1,0:T(8,128)(2,1)S(1)}, bf16[296,192]{1,0:T(8,128)(2,1)S(1)}, u32[]{:S(2)}, u32[]{:S(2)}) collective-permute-start(bf16[296,192]{1,0:T(8,128)(2,1)S(1)} %pad_maximum_fusion.5), channel_id=1, source_target_pairs={{0,6},{2,4},{4,2},{6,0},{1,7},{3,5},{5,3},{7,1},{8,14},{10,12},{12... | collective-permute-start | bytes 341000 | tf_op jit(solution)/shard_map/ppermute | solution.py:251
  40.1 0.9 %slice-start.1 = ((bf16[152,192]{1,0:T(8,128)(2,1)}), bf16[144,192]{1,0:T(8,128)(2,1)S(1)}, s32[]{:S(2)}) async-start(bf16[152,192]{1,0:T(8,128)(2,1)} %copy-done.3), calls=%async_computation.1 | async-start | bytes 147456 | tf_op jit(solution)/shard_map/slice | solution.py:321
  41.0 7.7 %copy-start.4 = (bf16[152,192]{1,0:T(8,128)(2,1)S(1)}, bf16[152,192]{1,0:T(8,128)(2,1)}, u32[]{:S(2)}) copy-start(bf16[152,192]{1,0:T(8,128)(2,1)} %copy-done.3) | copy-start | bytes 175108
  41.0 7.7 %collective-permute-start.8 = (bf16[440,192]{1,0:T(8,128)(2,1)S(1)}, bf16[440,192]{1,0:T(8,128)(2,1)S(1)}, u32[]{:S(2)}, u32[]{:S(2)}) collective-permute-start(bf16[440,192]{1,0:T(8,128)(2,1)S(1)} %pad_maximum_fusion.1), channel_id=1, source_target_pairs={{0,24},{8,16},{16,8},{24,0},{1,25},{9,17},{17,9},{25,1},{2,26},{10... | collective-permute-start | bytes 506888 | tf_op jit(solution)/shard_map/ppermute | solution.py:251
  48.8 0.6 %copy-start.2 = (bf16[200,192]{1,0:T(8,128)(2,1)}, bf16[200,192]{1,0:T(8,128)(2,1)S(1)}, u32[]{:S(2)}) copy-start(bf16[200,192]{1,0:T(8,128)(2,1)S(1)} %slice_add_fusion) | copy-start | bytes 230404
  48.9 1.5 %collective-permute-start.9 = (bf16[440,192]{1,0:T(8,128)(2,1)S(1)}, bf16[440,192]{1,0:T(8,128)(2,1)S(1)}, u32[]{:S(2)}, u32[]{:S(2)}) collective-permute-start(bf16[440,192]{1,0:T(8,128)(2,1)S(1)} %pad_maximum_fusion), channel_id=1, source_target_pairs={{0,8},{8,0},{16,24},{24,16},{1,9},{9,1},{17,25},{25,17},{2,10},{10... | collective-permute-start | bytes 506888 | tf_op jit(solution)/shard_map/ppermute | solution.py:251
  49.4 1.0 %slice-start = ((bf16[200,192]{1,0:T(8,128)(2,1)}), bf16[192,192]{1,0:T(8,128)(2,1)S(1)}, s32[]{:S(2)}) async-start(bf16[200,192]{1,0:T(8,128)(2,1)} %copy-done.2), calls=%async_computation | async-start | bytes 196608 | tf_op jit(solution)/shard_map/slice | solution.py:339

commit v2 on v1

v2 whole, which is shorter than its diff:
```python
import functools
import math

import jax
import jax.numpy as jnp
import numpy as np
from jax import lax
from jax.experimental import pallas as pl
from jax.experimental.pallas import tpu as pltpu
from jax.sharding import PartitionSpec as P

C = 192
H = 6
HD = 32
WZ = 2
WA = 6
WL = 12
SA = 3
SO = 6
WT = 144
POS = 3312
EPS = 1e-05
MASKED = -1e30

ROWS = WZ * WA
SPAN = 2 * WL - 1
QUAD = WZ * SA * 8
WIDE = 256
LEAD = 11 * SPAN
HALO = 3 * QUAD // 2
TABLE = H * ROWS + 16
BF = jnp.bfloat16
F32 = jnp.float32
VMEM = pl.BlockSpec(memory_space=pltpu.VMEM)


def dp_index():
    return lax.axis_index("dp")


def side_index():
    column = lax.axis_index("lon")
    return lax.rem(column + lax.div(column, 2), 2)


def last_row():
    return lax.axis_index("lat") == lax.axis_size("lat") - 1


def token_order():
    order = np.zeros((WT, 4 * QUAD), np.float32)
    for z in range(WZ):
        for a in range(WA):
            for o in range(WL):
                south, east = a >= SA, o >= SO
                quadrant = 2 * south + east
                column = o - SO if east else o + 2
                row = (z * SA + a % SA) * 8 + column
                order[(z * WA + a) * WL + o, quadrant * QUAD + row] = 1.0
    return order


def matmul(a, b):
    return lax.dot_general(a, b, (((1,), (0,)), ((), ())), preferred_element_type=F32)


def matmul_t(a, b):
    return lax.dot_general(a, b, (((1,), (1,)), ((), ())), preferred_element_type=F32)


def over_12(index):
    return lax.shift_right_logical(index * 5462, 16)


def spread_lanes(row, position, parts):
    width = row.shape[1]
    full = jnp.zeros((1, C), F32)
    for k in range(parts):
        pieces = [row]
        if k:
            pieces.insert(0, jnp.zeros((1, k * width), F32))
        if k < parts - 1:
            pieces.append(jnp.zeros((1, (parts - 1 - k) * width), F32))
        full = jnp.where(position == k, jnp.concatenate(pieces, axis=1), full)
    return full


def pack_kernel(parts, tok, dy, qkv, proj, gain, dense, east, south, corner):
    n_qkv, n_proj = 3 * C // parts, C // parts
    dense[:n_qkv] = qkv[...]
    dense[n_qkv : n_qkv + n_proj] = proj[...]
    row = spread_lanes(gain[...].astype(F32), dp_index(), parts)
    dense[n_qkv + n_proj :] = jnp.broadcast_to(row, (16, C)).astype(BF)

    def strip(ref, rows, cols):
        part = ref[:, rows : rows + SA].astype(F32)
        return part[:, :, cols : cols + 8].reshape(QUAD, C).astype(BF)

    for index, ref in enumerate((tok, dy)):
        at = slice(index * QUAD, (index + 1) * QUAD)
        east[at] = strip(ref, SA, 0)
        south[at] = strip(ref, 0, 4)
        corner[at] = strip(ref, 0, 0)


def folded(value):
    rows = value.shape[0]
    top, tail = value[: 3 * rows // 4], value[3 * rows // 4 :]
    side = jnp.concatenate([tail[:, at : at + 64] for at in (0, 64, 128)], axis=0)
    return jnp.concatenate([top, side], axis=1)


def unfolded(value):
    rows = value.shape[0] // 3
    side = value[:, C:]
    tail = jnp.concatenate([side[k * rows : (k + 1) * rows] for k in range(3)], axis=1)
    return jnp.concatenate([value[:, :C], tail], axis=0)


def offsets(height, width, half):
    row = lax.broadcasted_iota(jnp.int32, (height, width), 0)
    col = lax.broadcasted_iota(jnp.int32, (height, width), 1)
    block = over_12(col)
    return row, block * SPAN - (col - block * WL) + WL - 1 - half


def bias_kernel(table, out):
    values = table[...]
    high = values.astype(BF)
    rest = values - high.astype(F32)
    middle = rest.astype(BF)
    low = (rest - middle.astype(F32)).astype(BF)
    stacked = jnp.concatenate([high, middle, low], axis=0)
    row, target = offsets(ROWS * SPAN, WIDE, 0)
    count = H * ROWS
    here = lax.broadcasted_iota(jnp.int32, (count, WIDE), 0)
    here = here - over_12(here) * ROWS
    there = over_12(lax.broadcasted_iota(jnp.int32, (count, WIDE), 1))

    def wrapped(index):
        return jnp.where(index >= WA, index - WA, index) >= SA

    crossing = jnp.logical_and(wrapped(here) != wrapped(there), last_row())
    for u in range(WL):
        onehot = jnp.where(row == target + u, 1.0, 0.0).astype(BF)
        spread = matmul(stacked, onehot)
        spread = spread[:count] + spread[count : 2 * count] + spread[2 * count :]
        spread = jnp.where(crossing, MASKED, spread)
        out[0, pl.ds(u, count, stride=WL), :] = spread[:, :128]
        out[1, pl.ds(u, count, stride=WL), :] = spread[:, 128:]


def main_kernel(
    parts, tok, dy, east, south, corner, bias, order, *refs
):
    dense = refs[:parts]
    send, keep, gain_sum, scores_grad, grad_qkv, unit_out, scale_out, qkv_w, proj_w, sums = refs[parts:]
    n_qkv, n_proj = 3 * C // parts, C // parts
    gain = None
    for k in range(parts):
        at = lax.rem(dp_index() + k, parts)
        qkv_w[pl.ds(pl.multiple_of(at * n_qkv, 16), n_qkv), :] = dense[k][:n_qkv]
        proj_w[pl.ds(pl.multiple_of(at * n_proj, 16), n_proj), :] = dense[k][n_qkv : n_qkv + n_proj]
        term = dense[k][n_qkv + n_proj : n_qkv + n_proj + 16].astype(F32)[:1]
        gain = term if gain is None else gain + term

    def own(ref):
        part = ref[:, SA:].astype(F32)
        return part[:, :, 4:12].reshape(QUAD, C).astype(BF)

    def window(ref, index):
        at = slice(index * QUAD, (index + 1) * QUAD)
        return jnp.concatenate([own(ref), east[at], south[at], corner[at]], axis=0)

    x = matmul(order[...], window(tok, 0))
    dyw = matmul(order[...], window(dy, 1)).astype(BF)
    average = jnp.sum(x, axis=-1, keepdims=True) * (1.0 / C)
    centred = x - average
    variance = jnp.sum(centred * centred, axis=-1, keepdims=True) * (1.0 / C)
    inverse = lax.rsqrt(variance + EPS)
    unit = centred * inverse
    normed = (unit * gain).astype(BF)
    qkv_t = matmul_t(qkv_w[...], normed).astype(BF)
    query = matmul_t(normed, qkv_w[:C]).astype(BF)
    grad_att32 = matmul(dyw, proj_w[...]).astype(BF).astype(F32)
    grad_att = grad_att32.astype(BF)
    grad_att_t = grad_att32.T.astype(BF)
    dy_t = dyw.astype(F32).T.astype(BF)
    scale = 1.0 / math.sqrt(HD)

    def alone(part, head):
        pieces = []
        if head:
            pieces.append(jnp.zeros((head * HD, WT), BF))
        pieces.append(part)
        if head < H - 1:
            pieces.append(jnp.zeros(((H - 1 - head) * HD, WT), BF))
        return jnp.concatenate(pieces, axis=0)

    def both(ref, at):
        rows = slice(at, at + WT)
        return jnp.concatenate([ref[0, rows], ref[1, rows, : WT - 128]], axis=1)

    attended_t, grad_q, grad_k, grad_v = [], [], [], []
    for head in range(H):
        at = head * HD
        q_t = qkv_t[at : at + HD]
        k_t = qkv_t[C + at : C + at + HD]
        v_t = qkv_t[2 * C + at : 2 * C + at + HD]
        scores = matmul(query, alone(k_t, head)) * scale + both(bias, head * WT)
        expo = jnp.exp(scores - jnp.max(scores, axis=-1, keepdims=True))
        probs = expo * (1.0 / jnp.sum(expo, axis=-1, keepdims=True))
        probs_low = probs.astype(BF)
        attended_t.append(matmul_t(v_t, probs_low))
        grad_probs = matmul(grad_att, alone(v_t, head))
        grad_v.append(matmul(grad_att_t[at : at + HD], probs_low))
        mean = jnp.sum(probs * grad_probs, axis=-1, keepdims=True)
        grad_scores = probs * (grad_probs - mean)
        scores_grad[0, head * WT : (head + 1) * WT] = grad_scores[:, :128]
        scores_grad[1, head * WT : (head + 1) * WT, : WT - 128] = grad_scores[:, 128:]
        scores_low = grad_scores.astype(BF)
        grad_q.append(matmul_t(k_t, scores_low) * scale)
        grad_k.append(matmul(q_t, scores_low) * scale)
    grad_qkv_t32 = jnp.concatenate(grad_q + grad_k + grad_v, axis=0)
    grad_qkv_t = grad_qkv_t32.astype(BF)
    grad_qkv_w = matmul(grad_qkv_t, normed)
    grad_proj = matmul_t(dy_t, jnp.concatenate(attended_t, axis=0).astype(BF))
    each = n_qkv + n_proj
    for k in range(parts):
        sums[k * each : k * each + n_qkv] = grad_qkv_w[k * n_qkv : (k + 1) * n_qkv]
        sums[k * each + n_qkv : (k + 1) * each] = grad_proj[k * n_proj : (k + 1) * n_proj]
    half = each // 2
    for k in range(parts):
        mine = k * each + side_index() * half
        other = k * each + (1 - side_index()) * half
        rows = slice(k * 3 * half // 4, (k + 1) * 3 * half // 4)
        keep[rows] = folded(sums[pl.ds(pl.multiple_of(mine, 16), half), :])
        send[rows] = folded(sums[pl.ds(pl.multiple_of(other, 16), half), :]).astype(BF)
    weighted = jnp.sum(grad_qkv_w * qkv_w[...].astype(F32), axis=0, keepdims=True)
    gain_sum[...] = jnp.broadcast_to(weighted / gain, (16, C))
    grad_qkv[...] = grad_qkv_t32
    unit_out[...] = unit
    scale_out[:WT] = jnp.broadcast_to(inverse, (WT, C))
    scale_out[WT:] = jnp.broadcast_to(gain, (16, C))


def table_kernel(scores_grad, table):
    count = H * ROWS
    row, target = offsets(288, WT, 0)
    total = jnp.zeros((count, 288), F32)
    for u in range(WL):
        onehot = jnp.where(row == target + u, 1.0, 0.0).astype(BF)
        rows = pl.ds(u, count, stride=WL)
        wide = jnp.concatenate(
            [scores_grad[0, rows, :], scores_grad[1, rows, :][:, : WT - 128]], axis=1
        )
        total += matmul_t(wide.astype(BF), onehot)
    tail = total[:, LEAD : LEAD + SPAN]
    tail = jnp.concatenate([tail[h * ROWS : (h + 1) * ROWS] for h in range(H)], axis=1)
    tail = jnp.concatenate([tail, jnp.zeros((ROWS, WIDE - H * SPAN), F32)], axis=1)
    table[:count] = total[:, :WIDE]
    table[count:] = jnp.concatenate([tail, jnp.zeros((16 - ROWS, WIDE), F32)], axis=0)


def token_kernel(grad_qkv_t, unit, scales, qkv_w, order_t, quads):
    grad_normed = matmul(grad_qkv_t[...].T.astype(BF), qkv_w[...])
    inverse = scales[:WT]
    scaled = grad_normed * scales[WT : WT + 1]
    first = jnp.sum(scaled, axis=-1, keepdims=True) * (1.0 / C)
    second = jnp.sum(scaled * unit[...], axis=-1, keepdims=True) * (1.0 / C)
    grad_x = inverse * (scaled - first - unit[...] * second)
    quads[...] = matmul(order_t[...], grad_x.astype(BF)).astype(BF)


def widened(rows):
    return jnp.concatenate([rows, jnp.zeros((rows.shape[0], WIDE - C), F32)], axis=1)


def dp_kernel(keep, got, gain_sum, table, mine, out):
    rows = keep.shape[0] // 2
    first = pl.ds(pl.multiple_of(dp_index() * rows, 16), rows)
    second = pl.ds(pl.multiple_of((1 - dp_index()) * rows, 16), rows)
    mine[...] = keep[first, :] + got[first, :].astype(F32)
    theirs = keep[second, :] + got[second, :].astype(F32)
    out[...] = jnp.concatenate([theirs, widened(gain_sum[...]), table[...]], axis=0).astype(BF)


def lat_kernel(mine, sent, got, quads, out, table):
    rows = mine.shape[0]
    sent, got = sent[...].astype(F32), got[...].astype(F32)
    dense = mine[...] + got[:rows]
    gain_sum = sent[rows : rows + 16] + got[rows : rows + 16]
    table[...] = (sent[rows + 16 :] + got[rows + 16 :]).astype(BF)
    halo = folded(quads[2 * QUAD :].astype(F32))
    out[...] = jnp.concatenate([dense, gain_sum, halo], axis=0).astype(BF)


def lat_next_kernel(sent, got, out):
    sent, got = sent[...].astype(F32), got[...].astype(F32)
    rows = sent.shape[0] - HALO
    out[...] = jnp.concatenate([sent[:rows] + got[:rows], sent[rows:]], axis=0).astype(BF)


def lon_kernel(sent, got, before, quads, table, out, south):
    sent, got, before = sent[...].astype(F32), got[...].astype(F32), before[...].astype(F32)
    rows = sent.shape[0] - HALO
    halo = jnp.where(lax.rem(lax.axis_index("lat"), 2) == 1, before[rows:], got[rows:])
    halo = unfolded(halo)
    south[...] = halo[:QUAD].astype(BF)
    east = jnp.concatenate([quads[QUAD : 2 * QUAD].astype(F32), halo[QUAD:]], axis=0)
    out[...] = jnp.concatenate(
        [sent[:rows] + got[:rows], folded(east), table[...].astype(F32)], axis=0
    ).astype(BF)


def lon_next_kernel(sent, got, out):
    sent, got = sent[...].astype(F32), got[...].astype(F32)
    rows = sent.shape[0] - HALO - TABLE
    out[...] = jnp.concatenate(
        [sent[:rows] + got[:rows], sent[rows : rows + HALO], sent[rows + HALO :] + got[rows + HALO :]],
        axis=0,
    ).astype(BF)


def last_kernel(
    dy, quads, south, before, sent, got, tokens_out, qkv_out, proj_out, gain_out, table_out,
    dense_s, gain_s, table_s, sems,
):
    sent, got, before = sent[...].astype(F32), got[...].astype(F32), before[...].astype(F32)
    rows = sent.shape[0] - HALO - TABLE - 16
    half = 4 * rows // 3
    dense_s[pl.ds(pl.multiple_of(side_index() * half, 16), half), :] = unfolded(sent[:rows])
    dense_s[pl.ds(pl.multiple_of((1 - side_index()) * half, 16), half), :] = unfolded(got[:rows])
    n_qkv = 3 * half // 2
    copies = [
        pltpu.make_async_copy(dense_s.at[:n_qkv], qkv_out, sems.at[0]),
        pltpu.make_async_copy(dense_s.at[n_qkv:], proj_out, sems.at[1]),
    ]
    for copy in copies:
        copy.start()
    at = rows + 16
    halo = jnp.where(lax.rem(lax.axis_index("lon"), 2) == 1, got[at : at + HALO], before[at : at + HALO])
    finish_tokens(dy, quads, south[...].astype(F32), unfolded(halo), tokens_out)
    table = sent[at + HALO :] + got[at + HALO :]
    count = H * ROWS
    tail = table[count : count + ROWS]
    tail = jnp.concatenate([tail[:, h * SPAN : (h + 1) * SPAN] for h in range(H)], axis=0)
    table = jnp.concatenate([table[:count, :LEAD], tail], axis=1)
    for h in range(H):
        pieces = [table[h * ROWS + a : h * ROWS + a + 1] for a in range(ROWS)]
        table_s[h] = jnp.concatenate(pieces, axis=1)
    copies.append(pltpu.make_async_copy(table_s, table_out, sems.at[2]))
    copies[-1].start()
    gain_sum = sent[rows : rows + 1] + got[rows : rows + 1]
    gain_s[...] = jnp.where(dp_index() == 0, gain_sum[:, : C // 2], gain_sum[:, C // 2 : C])
    copies.append(pltpu.make_async_copy(gain_s, gain_out, sems.at[3]))
    copies[-1].start()
    for copy in copies:
        copy.wait()


def finish_tokens(dy, quad, south, lon_halo, out):
    gap = jnp.zeros((WZ, SA, 4, C), F32)

    def low(value):
        return jnp.concatenate([value.reshape(WZ, SA, 8, C), gap], axis=2)

    def high(value):
        return jnp.concatenate([gap, value.reshape(WZ, SA, 8, C)], axis=2)

    upper = dy[:, :SA].astype(F32) + low(lon_halo[QUAD:]) + high(south)
    lower = dy[:, SA:].astype(F32) + low(lon_halo[:QUAD]) + high(quad[:QUAD].astype(F32))
    out[:, :SA] = upper.astype(BF)
    out[:, SA:] = lower.astype(BF)


def finish_kernel(dy, quad, south, lon_halo, out):
    finish_tokens(dy, quad, south[...].astype(F32), lon_halo[...].astype(F32), out)


def call(kernel, outs, scratch=(), specs=None, flops=1000000, nbytes=1000000, out_specs=None):
    return pl.pallas_call(
        kernel,
        out_shape=outs,
        in_specs=specs,
        out_specs=jax.tree.map(lambda _: VMEM, outs) if out_specs is None else out_specs,
        scratch_shapes=list(scratch),
        compiler_params=pltpu.CompilerParams(vmem_limit_bytes=24 << 20),
        cost_estimate=pl.CostEstimate(flops=flops, bytes_accessed=nbytes, transcendentals=0),
    )


def shaped(rows, cols, dtype):
    return jax.ShapeDtypeStruct((rows, cols), dtype)


def exchanged(value, axis, flip):
    count = lax.axis_size(axis)
    return lax.ppermute(value, axis, [(i, i ^ flip) for i in range(count)])


def passed_along(value, axis, steps):
    count = lax.axis_size(axis)
    return lax.ppermute(value, axis, [(i, (i + steps) % count) for i in range(count)])


def passed_diagonally(value, steps):
    rows, cols = lax.axis_size("lon"), lax.axis_size("lat")
    pairs = [
        (i * cols + j, ((i + steps) % rows) * cols + (j + steps) % cols)
        for i in range(rows)
        for j in range(cols)
    ]
    return lax.ppermute(value, ("lon", "lat"), pairs)


def body(tokens, grad_out, qkv_weight, proj_weight, norm_gain, bias_table):
    parts = lax.axis_size("dp")
    lon_count, lat_count = lax.axis_size("lon"), lax.axis_size("lat")
    n_qkv, n_proj = 3 * C // parts, C // parts
    each = n_qkv + n_proj
    half = each // 2
    tok = tokens.reshape(WZ, WA, WL, C)
    dy = grad_out.reshape(WZ, WA, WL, C)

    strips = [shaped(2 * QUAD, C, BF)] * 3
    dense, east, south, corner = call(
        functools.partial(pack_kernel, parts),
        [shaped(each + 16, C, BF)] + strips,
        specs=[VMEM] * 5,
    )(tok, dy, qkv_weight, proj_weight, norm_gain.reshape(1, n_proj))
    gathered = [dense] + [passed_along(dense, "dp", -k) for k in range(1, parts)]
    east = passed_along(east, "lon", -1)
    south = passed_along(south, "lat", -1)
    corner = passed_diagonally(corner, -1)
    bias = call(
        bias_kernel,
        jax.ShapeDtypeStruct((2, H * WT, 128), F32),
        specs=[VMEM],
        flops=200000000,
    )(bias_table.reshape(H * ROWS, ROWS * SPAN))
    order = token_order()
    packed = parts * 3 * half // 4
    outs = [
        shaped(packed, WIDE, BF),
        shaped(packed, WIDE, F32),
        shaped(16, C, F32),
        jax.ShapeDtypeStruct((2, H * WT, 128), F32),
        shaped(3 * C, WT, F32),
        shaped(WT, C, F32),
        shaped(WT + 16, C, F32),
        shaped(3 * C, C, BF),
    ]
    scratch = [pltpu.VMEM((C, C), BF), pltpu.VMEM((4 * C, C), F32)]
    send, keep, gain_sum, scores_grad, grad_qkv, unit, scales, qkv_full = call(
        functools.partial(main_kernel, parts), outs, scratch, specs=[VMEM] * (7 + parts)
    )(tok, dy, east, south, corner, bias, jnp.asarray(order, BF), *gathered)
    fast = (lon_count, lat_count, parts) == (4, 4, 2)
    if fast:
        got = exchanged(send, "lon", 1)
    table = call(table_kernel, shaped(TABLE, WIDE, F32), specs=[VMEM], flops=200000000)(scores_grad)
    if fast:
        mine, sent = call(
            dp_kernel,
            [shaped(packed // 2, WIDE, F32), shaped(packed // 2 + 16 + TABLE, WIDE, BF)],
            specs=[VMEM] * 4,
        )(keep, got, gain_sum, table)
        got = exchanged(sent, "dp", 1)
    quads = call(token_kernel, shaped(4 * QUAD, C, BF), specs=[VMEM] * 5, flops=100000000)(
        grad_qkv, unit, scales, qkv_full, jnp.asarray(order.T, BF)
    )
    if fast:
        rows = packed // 2 + 16
        lat_shape = shaped(rows + HALO, WIDE, BF)
        sent, table = call(
            lat_kernel, [lat_shape, shaped(TABLE, WIDE, BF)], specs=[VMEM] * 4
        )(mine, sent, got, quads)
        before = exchanged(sent, "lat", 1)
        sent = call(lat_next_kernel, lat_shape, specs=[VMEM] * 2)(sent, before)
        got = exchanged(sent, "lat", 3)
        lon_shape = shaped(rows + HALO + TABLE, WIDE, BF)
        sent, south = call(
            lon_kernel, [lon_shape, shaped(QUAD, C, BF)], specs=[VMEM] * 5
        )(sent, got, before, quads, table)
        before = exchanged(sent, "lon", 3)
        sent = call(lon_next_kernel, lon_shape, specs=[VMEM] * 2)(sent, before)
        got = exchanged(sent, "lon", 1)
        tile = (WZ, WA, WL, C)
        grad_tokens, grad_qkv_w, grad_proj, grad_gain, grad_table = call(
            last_kernel,
            [
                jax.ShapeDtypeStruct(tile, BF),
                shaped(n_qkv, C, F32),
                shaped(n_proj, C, F32),
                shaped(1, n_proj, F32),
                jax.ShapeDtypeStruct((H, 1, POS), F32),
            ],
            [
                pltpu.VMEM((each, C), F32),
                pltpu.VMEM((1, n_proj), F32),
                pltpu.VMEM((H, 1, POS), F32),
                pltpu.SemaphoreType.DMA((4,)),
            ],
            specs=[VMEM] * 6,
            out_specs=[VMEM] + [pl.BlockSpec(memory_space=pltpu.HBM)] * 4,
        )(dy, quads, south, before, sent, got)
        return (
            grad_tokens.reshape(tokens.shape),
            grad_qkv_w,
            grad_proj,
            grad_gain.reshape(n_proj),
            grad_table.reshape(1, H, POS),
        )
    pair = jnp.stack([keep, send.astype(F32)]).reshape(2, parts, packed // parts, WIDE)
    pair = jnp.where(side_index() == 0, pair, pair[::-1])
    pair = jax.vmap(jax.vmap(unfolded))(pair)
    dense_sum = lax.psum(pair.transpose(1, 0, 2, 3).reshape(parts * each, C), ("lon", "lat"))
    total = lax.psum_scatter(dense_sum, "dp", scatter_dimension=0, tiled=True)
    grad_gain = lax.psum(gain_sum[0], ("lon", "lat"))
    grad_gain = lax.psum_scatter(grad_gain, "dp", scatter_dimension=0, tiled=True)
    table = lax.psum(table, ("lon", "dp"))
    count = H * ROWS
    tail = table[count : count + ROWS, : H * SPAN].reshape(ROWS, H, SPAN)
    tail = tail.transpose(1, 0, 2).reshape(count, SPAN)
    table = jnp.concatenate([table[:count, :LEAD], tail], axis=1)
    south_halo = passed_along(quads[2 * QUAD :], "lat", 1)
    east_halo = jnp.concatenate([quads[QUAD : 2 * QUAD], south_halo[QUAD:]])
    east_halo = passed_along(east_halo, "lon", 1)
    grad_tokens = call(
        finish_kernel, jax.ShapeDtypeStruct((WZ, WA, WL, C), BF), specs=[VMEM] * 4
    )(dy, quads, south_halo[:QUAD], east_halo)
    return (
        grad_tokens.reshape(tokens.shape),
        total[:n_qkv],
        total[n_qkv:],
        grad_gain,
        table.reshape(1, H, POS),
    )


def solution(mesh):
    spec = P("dp", None, "lat", "lon", None)
    return jax.shard_map(
        body,
        mesh=mesh,
        in_specs=(spec, spec, P("dp", None), P("dp", None), P("dp"), P("lat", None, None)),
        out_specs=(spec, P("dp", None), P("dp", None), P("dp"), P("lat", None, None)),
        check_vma=False,
    )
```

time: 54.4 us -> 46.6 us (0.86)
  waiting for transfers between devices: 26.3 us -> 22.4 us
  local copies, waits for them, and re-layouts: 5.3 us -> 2.69 us
  other arithmetic: 2.35 us -> 0.2 us
  Pallas kernels: 6.71 us -> 8.09 us
    ppermute x6, waiting for transfers between devices: 25.3 us -> 20.8 us  [exchanged(): return lax.ppermute(value, axis, [(i, i ^ flip) for i in range(count)])]
    slice x14 -> x0, local copies, waits for them, and re-layouts: 2.28 us -> none  [the longest x2 0.86 us: body(): extra = extra[:2 * H * ROWS]]
    pallas_call x4 -> x11, Pallas kernels: 6.71 us -> 8.09 us  [the longest x1 4.06 us: body(): call(functools.partial(main_kernel, parts), outs, scratch, specs=[VMEM] *...]
    concatenate x7 -> x0, other arithmetic: 1.25 us -> none  [the longest x1 1.01 us: body(): jnp.concatenate([qkv_weight, proj_weight, jnp.broadcast_to(gain_row, (8,...]
    reshape x1, local copies, waits for them, and re-layouts: 0.02 us -> 0.98 us  [body(): tok = tokens.reshape(WZ, WA, WL, C)]
    reshape x1 -> x0, local copies, waits for them, and re-layouts: 0.82 us -> none  [body(): table.reshape(1, H, POS)]
    dynamic_slice x1 -> x0, other arithmetic: 0.59 us -> none  [body(): gain_sum = lax.dynamic_slice_in_dim(gain_sum, dp * n_proj, n_proj)]
    ppermute x1, waiting for transfers between devices: 0.94 us -> 1.5 us  [passed_diagonally(): return lax.ppermute(value, ('lon', 'lat'), pairs)]
  transfers between devices with their start and end apart: 10 -> 10, of which waited for: 7 -> 8; matrix products, arithmetic and copies ran while one was open for 1% -> 1% of each run, Pallas kernels for 3% -> 5%
where the time goes in v2:
time: 46.6 us; the launch traced here: 46.4 us
  waiting for transfers between devices  22.4 us (48%)
  starting transfers between devices  12.3 us (26%)
  Pallas kernels  8.09 us (17%)
  local copies, waits for them, and re-layouts  2.69 us (6%)
  between operations  0.78 us (2%)
    ppermute x6, waiting for transfers between devices, exchanged(): return lax.ppermute(value, axis, [(i, i ^ flip) for i in range(count)])  20.8 us
    ppermute x3, starting transfers between devices, passed_along(): lax.ppermute(value, axis, [(i, (i + steps) % count) for i in range(count)])  7.24 us
    ppermute x6, starting transfers between devices, exchanged(): return lax.ppermute(value, axis, [(i, i ^ flip) for i in range(count)])  4.46 us
    pallas_call x1, Pallas kernels, body(): call(functools.partial(main_kernel, parts), outs, scratch, specs=[VMEM] *...  4.06 us
    unnamed x13, local copies, waits for them, and re-layouts  1.59 us
    ppermute x1, waiting for transfers between devices, passed_diagonally(): return lax.ppermute(value, ('lon', 'lat'), pairs)  1.5 us
    pallas_call x1, Pallas kernels, body(): call(last_kernel, [jax.ShapeDtypeStruct(tile, BF), shaped(n_qkv, C, F32),...  1.12 us
    pallas_call x1, Pallas kernels, body(): call(bias_kernel, jax.ShapeDtypeStruct((2, H * WT, 128), F32), specs=[VME...  1.03 us
  transfers between devices with their start and end apart: 10, of which 8 were waited for; matrix products, arithmetic and copies ran while one was open for 1% of the time, Pallas kernels for 5%

profile of v2, /device:TPU:0, one launch (start us, length us, event | category | flops | bytes accessed | tf_op | source)
XLA Modules:
  0.0 46.4 jit_solution(4805880139205110939)
XLA Ops:
  0.7 1.0 %copy_bitcast_fusion = (bf16[2,6,12,192]{3,2,1,0:T(8,128)(2,1)S(1)}, bf16[2,6,12,192]{3,2,1,0:T(8,128)(2,1)S(1)}) fusion(bf16[1,2,6,12,192]{4,1,3,2,0:T(2,128)(2,1)} %param.8, bf16[1,2,6,12,192]{4,1,3,2,0:T(2,128)(2,1)} %param.9), kind=kLoop, calls=%fused_computation | loop fusion | bytes 221184 | tf_op jit(solution)/shard_map/reshape | solution.py:423
  1.7 0.6 %copy-done.4 = bf16[96]{0:T(256)(128)(2,1)S(1)} copy-done((bf16[96]{0:T(256)(128)(2,1)S(1)}, bf16[96]{0:T(256)(128)(2,1)}, u32[]{:S(2)}) %copy-start.4) | copy-done | bytes 216
  2.4 3.0 %collective-permute-start.3 = (bf16[400,192]{1,0:T(8,128)(2,1)S(1)}, bf16[400,192]{1,0:T(8,128)(2,1)S(1)}, u32[]{:S(2)}, u32[]{:S(2)}) collective-permute-start(bf16[400,192]{1,0:T(8,128)(2,1)S(1)} %get-tuple-element.31.refs_0_), channel_id=1, source_target_pairs={{0,1},{1,0},{2,3},{3,2},{4,5},{5,4},{6,7},{7,6},{8,9},{9,8},{10,11... | collective-permute-start | bytes 460808 | tf_op jit(solution)/shard_map/ppermute | solution.py:404
  5.3 0.7 %collective-permute-start = (bf16[96,192]{1,0:T(8,128)(2,1)S(1)}, bf16[96,192]{1,0:T(8,128)(2,1)S(1)}, u32[]{:S(2)}, u32[]{:S(2)}) collective-permute-start(bf16[96,192]{1,0:T(8,128)(2,1)S(1)} %get-tuple-element.28), channel_id=1, source_target_pairs={{0,24},{8,0},{16,8},{24,16},{1,25},{9,1},{17,9},{25,17},{2,26},{10... | collective-permute-start | bytes 110600 | tf_op jit(solution)/shard_map/ppermute | solution.py:404
  6.0 3.6 %collective-permute-start.1 = (bf16[96,192]{1,0:T(8,128)(2,1)S(1)}, bf16[96,192]{1,0:T(8,128)(2,1)S(1)}, u32[]{:S(2)}, u32[]{:S(2)}) collective-permute-start(bf16[96,192]{1,0:T(8,128)(2,1)S(1)} %get-tuple-element.29), channel_id=1, source_target_pairs={{0,6},{2,0},{4,2},{6,4},{1,7},{3,1},{5,3},{7,5},{8,14},{10,8},{12,... | collective-permute-start | bytes 110600 | tf_op jit(solution)/shard_map/ppermute | solution.py:404
  9.6 0.6 %collective-permute-start.2 = (bf16[96,192]{1,0:T(8,128)(2,1)S(1)}, bf16[96,192]{1,0:T(8,128)(2,1)S(1)}, u32[]{:S(2)}, u32[]{:S(2)}) collective-permute-start(bf16[96,192]{1,0:T(8,128)(2,1)S(1)} %get-tuple-element.30), channel_id=1, source_target_pairs={{0,30},{2,24},{4,26},{6,28},{8,6},{10,0},{12,2},{14,4},{16,14},{18... | collective-permute-start | bytes 110600 | tf_op jit(solution)/shard_map/ppermute | solution.py:414
  10.2 0.2 reduce
  10.5 1.0 %shard_map.120.bias = f32[2,864,128]{2,1,0:T(8,128)S(1)} custom-call(f32[72,276]{1,0:T(8,128)S(1)} %reshape.34.table), custom_call_target="tpu_custom_call" | custom-call | flops 200000000 | bytes 1000000 | tf_op jit(solution)/shard_map/pallas_call | solution.py:436
  11.6 1.5 %collective-permute-done.2.corner = bf16[96,192]{1,0:T(8,128)(2,1)S(1)} collective-permute-done((bf16[96,192]{1,0:T(8,128)(2,1)S(1)}, bf16[96,192]{1,0:T(8,128)(2,1)S(1)}, u32[]{:S(2)}, u32[]{:S(2)}) %collective-permute-start.2) | collective-permute-done | bytes 36896 | tf_op jit(solution)/shard_map/ppermute | solution.py:414
  13.1 4.1 %shard_map.121 = (bf16[288,256]{1,0:T(8,128)(2,1)S(1)}, f32[288,256]{1,0:T(8,128)S(1)}, f32[16,192]{1,0:T(8,128)S(1)}, f32[2,864,128]{2,1,0:T(8,128)S(1)}, f32[5...) custom-call(bf16[2,6,12,192]{3,2,1,0:T(8,128)(2,1)S(1)} %get-tuple-element.56, ...), custom_call_target="tpu_custom_call" | custom-call | flops 1000000 | bytes 1000000 | tf_op jit(solution)/shard_map/pallas_call | solution.py:455
  17.2 0.7 %collective-permute-start.4 = (bf16[288,256]{1,0:T(8,128)(2,1)S(1)}, bf16[288,256]{1,0:T(8,128)(2,1)S(1)}, u32[]{:S(2)}, u32[]{:S(2)}) collective-permute-start(bf16[288,256]{1,0:T(8,128)(2,1)S(1)} %get-tuple-element.37), channel_id=1, source_target_pairs={{0,8},{8,0},{16,24},{24,16},{1,9},{9,1},{17,25},{25,17},{2,10},{10... | collective-permute-start | bytes 442376 | tf_op jit(solution)/shard_map/ppermute | solution.py:399
  17.9 0.8 %shard_map.123.table = f32[88,256]{1,0:T(8,128)S(1)} custom-call(f32[2,864,128]{2,1,0:T(8,128)S(1)} %get-tuple-element.39.scores_grad), custom_call_target="tpu_custom_call" | custom-call | flops 200000000 | bytes 1000000 | tf_op jit(solution)/shard_map/pallas_call | solution.py:461
  18.9 0.6 %collective-permute-start.5 = (bf16[248,256]{1,0:T(8,128)(2,1)S(1)}, bf16[248,256]{1,0:T(8,128)(2,1)S(1)}, u32[]{:S(2)}, u32[]{:S(2)}) collective-permute-start(bf16[248,256]{1,0:T(8,128)(2,1)S(1)} %get-tuple-element.41.sent), channel_id=1, source_target_pairs={{0,1},{1,0},{2,3},{3,2},{4,5},{5,4},{6,7},{7,6},{8,9},{9,8},{10,11... | collective-permute-start | bytes 380936 | tf_op jit(solution)/shard_map/ppermute | solution.py:399
  19.6 0.2 copy-done.1
  19.8 0.5 %shard_map.122.quads = bf16[192,192]{1,0:T(8,128)(2,1)S(1)} custom-call(f32[576,144]{1,0:T(8,128)S(1)} %get-tuple-element.32.grad_qkv_t, f32[144,192]{1,0:T(8,128)S(1)} %get-tuple-element.33.unit, f32[160,192]{1,0:T(8,128)S(1)} %get-tuple-element.34.scales, bf16[576,192]{1,0:T(8,128)(2,1)S(1)} %get-tuple-element.35.qkv_w, bf16[192,144]{1,0:T(8,128)(2,1)S(1)} %copy-done.1), custom_call_target="tpu_custom_call" | custom-call | flops 100000000 | bytes 1000000 | tf_op jit(solution)/shard_map/pallas_call | solution.py:469
  20.3 4.4 %collective-permute-done.5.got = bf16[248,256]{1,0:T(8,128)(2,1)S(1)} collective-permute-done((bf16[248,256]{1,0:T(8,128)(2,1)S(1)}, bf16[248,256]{1,0:T(8,128)(2,1)S(1)}, u32[]{:S(2)}, u32[]{:S(2)}) %collective-permute-start.5) | collective-permute-done | bytes 127008 | tf_op jit(solution)/shard_map/ppermute | solution.py:399
  24.9 4.8 %collective-permute-done.6.got.before = bf16[232,256]{1,0:T(8,128)(2,1)S(1)} collective-permute-done((bf16[232,256]{1,0:T(8,128)(2,1)S(1)}, bf16[232,256]{1,0:T(8,128)(2,1)S(1)}, u32[]{:S(2)}, u32[]{:S(2)}) %collective-permute-start.6) | collective-permute-done | bytes 118816 | tf_op jit(solution)/shard_map/ppermute | solution.py:399
  29.7 3.0 %collective-permute-start.7 = (bf16[232,256]{1,0:T(8,128)(2,1)S(1)}, bf16[232,256]{1,0:T(8,128)(2,1)S(1)}, u32[]{:S(2)}, u32[]{:S(2)}) collective-permute-start(bf16[232,256]{1,0:T(8,128)(2,1)S(1)} %shard_map.126.sent), channel_id=1, source_target_pairs={{0,6},{2,4},{4,2},{6,0},{1,7},{3,5},{5,3},{7,1},{8,14},{10,12},{12... | collective-permute-start | bytes 356360 | tf_op jit(solution)/shard_map/ppermute | solution.py:399
  32.8 3.7 %collective-permute-done.7.got = bf16[232,256]{1,0:T(8,128)(2,1)S(1)} collective-permute-done((bf16[232,256]{1,0:T(8,128)(2,1)S(1)}, bf16[232,256]{1,0:T(8,128)(2,1)S(1)}, u32[]{:S(2)}, u32[]{:S(2)}) %collective-permute-start.7) | collective-permute-done | bytes 118816 | tf_op jit(solution)/shard_map/ppermute | solution.py:399
  36.4 0.2 shard_map.127
  36.7 6.4 %collective-permute-done.8.got.before = bf16[320,256]{1,0:T(8,128)(2,1)S(1)} collective-permute-done((bf16[320,256]{1,0:T(8,128)(2,1)S(1)}, bf16[320,256]{1,0:T(8,128)(2,1)S(1)}, u32[]{:S(2)}, u32[]{:S(2)}) %collective-permute-start.8) | collective-permute-done | bytes 163872 | tf_op jit(solution)/shard_map/ppermute | solution.py:399
  43.2 1.4 %collective-permute-done.9.got = bf16[320,256]{1,0:T(8,128)(2,1)S(1)} collective-permute-done((bf16[320,256]{1,0:T(8,128)(2,1)S(1)}, bf16[320,256]{1,0:T(8,128)(2,1)S(1)}, u32[]{:S(2)}, u32[]{:S(2)}) %collective-permute-start.9) | collective-permute-done | bytes 163872 | tf_op jit(solution)/shard_map/ppermute | solution.py:399
  44.6 1.1 %shard_map.129 = (bf16[2,6,12,192]{3,2,1,0:T(8,128)(2,1)S(1)}, f32[288,192]{1,0:T(8,128)}, f32[96,192]{1,0:T(8,128)}, f32[1,96]{1,0:T(1,128)}, f32[6,1,3312]{2,1,0:T(1,128)}) custom-call(bf16[2,6,12,192]{3,2,1,0:T(8,128)(2,1)S(1)} %get-tuple-element.57.dy, bf16[192,192]{1,0:T(8,128)(2,1)S(1)} %shard_map.122.quads, ...), custom_call_target="tpu_custom_call" | custom-call | flops 1000000 | bytes 1000000 | tf_op jit(solution)/shard_map/pallas_call | solution.py:489
  45.7 0.7 %copy.15 = bf16[1,2,6,12,192]{4,1,3,2,0:T(2,128)(2,1)} copy(bf16[1,2,6,12,192]{4,3,2,1,0:T(8,128)(2,1)S(1)} %bitcast.8) | data formatting | bytes 110592
  (23 shorter events, 0.9 us)
Async XLA Ops:
  0.6 1.0 %copy-start.3 = (bf16[96,192]{1,0:T(8,128)(2,1)S(1)}, bf16[96,192]{1,0:T(8,128)(2,1)}, u32[]{:S(2)}) copy-start(bf16[96,192]{1,0:T(8,128)(2,1)} %proj.1) | copy-start | bytes 110596
  0.6 1.0 %copy-start = (bf16[288,192]{1,0:T(8,128)(2,1)S(1)}, bf16[288,192]{1,0:T(8,128)(2,1)}, u32[]{:S(2)}) copy-start(bf16[288,192]{1,0:T(8,128)(2,1)} %qkv.1) | copy-start | bytes 331780
  1.6 0.7 %copy-start.4 = (bf16[96]{0:T(256)(128)(2,1)S(1)}, bf16[96]{0:T(256)(128)(2,1)}, u32[]{:S(2)}) copy-start(bf16[96]{0:T(256)(128)(2,1)} %param.12) | copy-start | bytes 580
  2.3 7.9 %copy-start.5 = (f32[1,6,3312]{2,0,1:T(1,128)S(1)}, f32[1,6,3312]{2,0,1:T(1,128)}, u32[]{:S(2)}) copy-start(f32[1,6,3312]{2,0,1:T(1,128)} %param.13) | copy-start | bytes 238468
  2.4 10.8 %collective-permute-start.3 = (bf16[400,192]{1,0:T(8,128)(2,1)S(1)}, bf16[400,192]{1,0:T(8,128)(2,1)S(1)}, u32[]{:S(2)}, u32[]{:S(2)}) collective-permute-start(bf16[400,192]{1,0:T(8,128)(2,1)S(1)} %get-tuple-element.31.refs_0_), channel_id=1, source_target_pairs={{0,1},{1,0},{2,3},{3,2},{4,5},{5,4},{6,7},{7,6},{8,9},{9,8},{10,11... | collective-permute-start | bytes 460808 | tf_op jit(solution)/shard_map/ppermute | solution.py:404
  5.3 6.2 %collective-permute-start = (bf16[96,192]{1,0:T(8,128)(2,1)S(1)}, bf16[96,192]{1,0:T(8,128)(2,1)S(1)}, u32[]{:S(2)}, u32[]{:S(2)}) collective-permute-start(bf16[96,192]{1,0:T(8,128)(2,1)S(1)} %get-tuple-element.28), channel_id=1, source_target_pairs={{0,24},{8,0},{16,8},{24,16},{1,25},{9,1},{17,9},{25,17},{2,26},{10... | collective-permute-start | bytes 110600 | tf_op jit(solution)/shard_map/ppermute | solution.py:404
  6.0 5.6 %collective-permute-start.1 = (bf16[96,192]{1,0:T(8,128)(2,1)S(1)}, bf16[96,192]{1,0:T(8,128)(2,1)S(1)}, u32[]{:S(2)}, u32[]{:S(2)}) collective-permute-start(bf16[96,192]{1,0:T(8,128)(2,1)S(1)} %get-tuple-element.29), channel_id=1, source_target_pairs={{0,6},{2,0},{4,2},{6,4},{1,7},{3,1},{5,3},{7,5},{8,14},{10,8},{12,... | collective-permute-start | bytes 110600 | tf_op jit(solution)/shard_map/ppermute | solution.py:404
  9.6 3.5 %collective-permute-start.2 = (bf16[96,192]{1,0:T(8,128)(2,1)S(1)}, bf16[96,192]{1,0:T(8,128)(2,1)S(1)}, u32[]{:S(2)}, u32[]{:S(2)}) collective-permute-start(bf16[96,192]{1,0:T(8,128)(2,1)S(1)} %get-tuple-element.30), channel_id=1, source_target_pairs={{0,30},{2,24},{4,26},{6,28},{8,6},{10,0},{12,2},{14,4},{16,14},{18... | collective-permute-start | bytes 110600 | tf_op jit(solution)/shard_map/ppermute | solution.py:414
  10.5 2.6 %copy-start.2 = (bf16[144,192]{1,0:T(8,128)(2,1)S(1)}, bf16[144,192]{1,0:T(8,128)(2,1)}, u32[]{:S(2)}) copy-start(bf16[144,192]{1,0:T(8,128)(2,1)} %constant.4.clone.order) | copy-start | bytes 165892
  17.2 1.7 %collective-permute-start.4 = (bf16[288,256]{1,0:T(8,128)(2,1)S(1)}, bf16[288,256]{1,0:T(8,128)(2,1)S(1)}, u32[]{:S(2)}, u32[]{:S(2)}) collective-permute-start(bf16[288,256]{1,0:T(8,128)(2,1)S(1)} %get-tuple-element.37), channel_id=1, source_target_pairs={{0,8},{8,0},{16,24},{24,16},{1,9},{9,1},{17,25},{25,17},{2,10},{10... | collective-permute-start | bytes 442376 | tf_op jit(solution)/shard_map/ppermute | solution.py:399
  18.9 0.9 %copy-start.1 = (bf16[192,144]{1,0:T(8,128)(2,1)S(1)}, bf16[192,144]{1,0:T(8,128)(2,1)}, u32[]{:S(2)}) copy-start(bf16[192,144]{1,0:T(8,128)(2,1)} %constant.5.clone.order_t) | copy-start | bytes 165892
  18.9 5.7 %collective-permute-start.5 = (bf16[248,256]{1,0:T(8,128)(2,1)S(1)}, bf16[248,256]{1,0:T(8,128)(2,1)S(1)}, u32[]{:S(2)}, u32[]{:S(2)}) collective-permute-start(bf16[248,256]{1,0:T(8,128)(2,1)S(1)} %get-tuple-element.41.sent), channel_id=1, source_target_pairs={{0,1},{1,0},{2,3},{3,2},{4,5},{5,4},{6,7},{7,6},{8,9},{9,8},{10,11... | collective-permute-start | bytes 380936 | tf_op jit(solution)/shard_map/ppermute | solution.py:399
  24.8 4.9 %collective-permute-start.6 = (bf16[232,256]{1,0:T(8,128)(2,1)S(1)}, bf16[232,256]{1,0:T(8,128)(2,1)S(1)}, u32[]{:S(2)}, u32[]{:S(2)}) collective-permute-start(bf16[232,256]{1,0:T(8,128)(2,1)S(1)} %get-tuple-element.42.sent), channel_id=1, source_target_pairs={{0,2},{2,0},{4,6},{6,4},{1,3},{3,1},{5,7},{7,5},{8,10},{10,8},{12,... | collective-permute-start | bytes 356360 | tf_op jit(solution)/shard_map/ppermute | solution.py:399
  29.7 6.7 %collective-permute-start.7 = (bf16[232,256]{1,0:T(8,128)(2,1)S(1)}, bf16[232,256]{1,0:T(8,128)(2,1)S(1)}, u32[]{:S(2)}, u32[]{:S(2)}) collective-permute-start(bf16[232,256]{1,0:T(8,128)(2,1)S(1)} %shard_map.126.sent), channel_id=1, source_target_pairs={{0,6},{2,4},{4,2},{6,0},{1,7},{3,5},{5,3},{7,1},{8,14},{10,12},{12... | collective-permute-start | bytes 356360 | tf_op jit(solution)/shard_map/ppermute | solution.py:399
  36.7 6.4 %collective-permute-start.8 = (bf16[320,256]{1,0:T(8,128)(2,1)S(1)}, bf16[320,256]{1,0:T(8,128)(2,1)S(1)}, u32[]{:S(2)}, u32[]{:S(2)}) collective-permute-start(bf16[320,256]{1,0:T(8,128)(2,1)S(1)} %get-tuple-element.45.sent), channel_id=1, source_target_pairs={{0,24},{8,16},{16,8},{24,0},{1,25},{9,17},{17,9},{25,1},{2,26},{10... | collective-permute-start | bytes 491528 | tf_op jit(solution)/shard_map/ppermute | solution.py:399
  43.1 1.5 %collective-permute-start.9 = (bf16[320,256]{1,0:T(8,128)(2,1)S(1)}, bf16[320,256]{1,0:T(8,128)(2,1)S(1)}, u32[]{:S(2)}, u32[]{:S(2)}) collective-permute-start(bf16[320,256]{1,0:T(8,128)(2,1)S(1)} %shard_map.128.sent), channel_id=1, source_target_pairs={{0,8},{8,0},{16,24},{24,16},{1,9},{9,1},{17,25},{25,17},{2,10},{10... | collective-permute-start | bytes 491528 | tf_op jit(solution)/shard_map/ppermute | solution.py:399

commit v3 on v2

v3 whole, which is shorter than its diff:
```python
import functools
import math

import jax
import jax.numpy as jnp
import numpy as np
from jax import lax
from jax.experimental import pallas as pl
from jax.experimental.pallas import tpu as pltpu
from jax.sharding import PartitionSpec as P

C = 192
H = 6
HD = 32
WZ = 2
WA = 6
WL = 12
SA = 3
SO = 6
WT = 144
POS = 3312
EPS = 1e-05
MASKED = -1e30

ROWS = WZ * WA
SPAN = 2 * WL - 1
QUAD = WZ * SA * 8
WIDE = 256
LEAD = 11 * SPAN
HALO = 3 * QUAD // 2
TABLE = H * ROWS + 16
BF = jnp.bfloat16
F32 = jnp.float32
VMEM = pl.BlockSpec(memory_space=pltpu.VMEM)


def dp_index():
    return lax.axis_index("dp")


def side_index():
    column = lax.axis_index("lon")
    return lax.rem(column + lax.div(column, 2), 2)


def last_row():
    return lax.axis_index("lat") == lax.axis_size("lat") - 1


def token_order():
    order = np.zeros((WT, 4 * QUAD), np.float32)
    for z in range(WZ):
        for a in range(WA):
            for o in range(WL):
                south, east = a >= SA, o >= SO
                quadrant = 2 * south + east
                column = o - SO if east else o + 2
                row = (z * SA + a % SA) * 8 + column
                order[(z * WA + a) * WL + o, quadrant * QUAD + row] = 1.0
    return order


def matmul(a, b):
    return lax.dot_general(a, b, (((1,), (0,)), ((), ())), preferred_element_type=F32)


def matmul_t(a, b):
    return lax.dot_general(a, b, (((1,), (1,)), ((), ())), preferred_element_type=F32)


def over_12(index):
    return lax.shift_right_logical(index * 5462, 16)


def spread_lanes(row, position, parts):
    width = row.shape[1]
    full = jnp.zeros((1, C), F32)
    for k in range(parts):
        pieces = [row]
        if k:
            pieces.insert(0, jnp.zeros((1, k * width), F32))
        if k < parts - 1:
            pieces.append(jnp.zeros((1, (parts - 1 - k) * width), F32))
        full = jnp.where(position == k, jnp.concatenate(pieces, axis=1), full)
    return full


def folded(value):
    rows = value.shape[0]
    top, tail = value[: 3 * rows // 4], value[3 * rows // 4 :]
    side = jnp.concatenate([tail[:, at : at + 64] for at in (0, 64, 128)], axis=0)
    return jnp.concatenate([top, side], axis=1)


def unfolded(value):
    rows = value.shape[0] // 3
    side = value[:, C:]
    tail = jnp.concatenate([side[k * rows : (k + 1) * rows] for k in range(3)], axis=1)
    return jnp.concatenate([value[:, :C], tail], axis=0)


def pack_kernel(parts, tok, dy, qkv, proj, gain, dense, east, south, corner):
    n_qkv, n_proj = 3 * C // parts, C // parts
    dense[:n_qkv] = qkv[...]
    dense[n_qkv : n_qkv + n_proj] = proj[...]
    row = spread_lanes(gain[...].astype(F32), dp_index(), parts)
    dense[n_qkv + n_proj :] = jnp.broadcast_to(row, (16, C)).astype(BF)

    def strips(rows, cols):
        pair = []
        for ref in (tok, dy):
            part = ref[:, rows : rows + SA].astype(F32)
            pair.append(part[:, :, cols : cols + 8].reshape(QUAD, C))
        return folded(jnp.concatenate(pair, axis=0)).astype(BF)

    east[...] = strips(SA, 0)
    south[...] = strips(0, 4)
    corner[...] = strips(0, 0)


def offsets(height, width, half):
    row = lax.broadcasted_iota(jnp.int32, (height, width), 0)
    col = lax.broadcasted_iota(jnp.int32, (height, width), 1)
    block = over_12(col)
    return row, block * SPAN - (col - block * WL) + WL - 1 - half


def bias_kernel(table, out):
    values = table[...]
    high = values.astype(BF)
    rest = values - high.astype(F32)
    middle = rest.astype(BF)
    low = (rest - middle.astype(F32)).astype(BF)
    stacked = jnp.concatenate([high, middle, low], axis=0)
    row, target = offsets(ROWS * SPAN, WIDE, 0)
    count = H * ROWS
    here = lax.broadcasted_iota(jnp.int32, (count, WIDE), 0)
    here = here - over_12(here) * ROWS
    there = over_12(lax.broadcasted_iota(jnp.int32, (count, WIDE), 1))

    def wrapped(index):
        return jnp.where(index >= WA, index - WA, index) >= SA

    crossing = jnp.logical_and(wrapped(here) != wrapped(there), last_row())
    for u in range(WL):
        onehot = jnp.where(row == target + u, 1.0, 0.0).astype(BF)
        spread = matmul(stacked, onehot)
        spread = spread[:count] + spread[count : 2 * count] + spread[2 * count :]
        spread = jnp.where(crossing, MASKED, spread)
        out[0, pl.ds(u, count, stride=WL), :] = spread[:, :128]
        out[1, pl.ds(u, count, stride=WL), :] = spread[:, 128:]


def main_kernel(
    parts, pieces, south, corner, east, tok, dy, bias, order, *refs
):
    dense = refs[:parts]
    send, keep, gain_sum, scores_grad, grad_qkv, unit_out, scale_out, qkv_w, proj_w, sums = refs[parts:]
    n_qkv, n_proj = 3 * C // parts, C // parts
    gain = None
    for k in range(parts):
        at = lax.rem(dp_index() + k, parts)
        qkv_w[pl.ds(pl.multiple_of(at * n_qkv, 16), n_qkv), :] = dense[k][:n_qkv]
        proj_w[pl.ds(pl.multiple_of(at * n_proj, 16), n_proj), :] = dense[k][n_qkv : n_qkv + n_proj]
        term = dense[k][n_qkv + n_proj : n_qkv + n_proj + 16].astype(F32)[:1]
        gain = term if gain is None else gain + term

    def own(ref):
        part = ref[:, SA:].astype(F32)
        return part[:, :, 4:12].reshape(QUAD, C).astype(BF)

    halos = [unfolded(ref[...].astype(F32)).astype(BF) for ref in (east, south, corner)]

    def window(ref, index):
        at = slice(index * QUAD, (index + 1) * QUAD)
        return jnp.concatenate([own(ref)] + [halo[at] for halo in halos], axis=0)

    x = matmul(order[...], window(tok, 0))
    dyw = matmul(order[...], window(dy, 1)).astype(BF)
    average = jnp.sum(x, axis=-1, keepdims=True) * (1.0 / C)
    centred = x - average
    variance = jnp.sum(centred * centred, axis=-1, keepdims=True) * (1.0 / C)
    inverse = lax.rsqrt(variance + EPS)
    unit = centred * inverse
    normed = (unit * gain).astype(BF)
    qkv_t = matmul_t(qkv_w[...], normed).astype(BF)
    query = matmul_t(normed, qkv_w[:C]).astype(BF)
    grad_att32 = matmul(dyw, proj_w[...]).astype(BF).astype(F32)
    grad_att = grad_att32.astype(BF)
    grad_att_t = grad_att32.T.astype(BF)
    dy_t = dyw.astype(F32).T.astype(BF)
    scale = 1.0 / math.sqrt(HD)

    def alone(part, head):
        pieces = []
        if head:
            pieces.append(jnp.zeros((head * HD, WT), BF))
        pieces.append(part)
        if head < H - 1:
            pieces.append(jnp.zeros(((H - 1 - head) * HD, WT), BF))
        return jnp.concatenate(pieces, axis=0)

    def both(ref, at):
        rows = slice(at, at + WT)
        return jnp.concatenate([ref[0, rows], ref[1, rows, : WT - 128]], axis=1)

    attended_t, grad_q, grad_k, grad_v = [], [], [], []
    for head in range(H):
        at = head * HD
        q_t = qkv_t[at : at + HD]
        k_t = qkv_t[C + at : C + at + HD]
        v_t = qkv_t[2 * C + at : 2 * C + at + HD]
        scores = matmul(query, alone(k_t, head)) * scale + both(bias, head * WT)
        expo = jnp.exp(scores - jnp.max(scores, axis=-1, keepdims=True))
        probs = expo * (1.0 / jnp.sum(expo, axis=-1, keepdims=True))
        probs_low = probs.astype(BF)
        attended_t.append(matmul_t(v_t, probs_low))
        grad_probs = matmul(grad_att, alone(v_t, head))
        grad_v.append(matmul(grad_att_t[at : at + HD], probs_low))
        mean = jnp.sum(probs * grad_probs, axis=-1, keepdims=True)
        grad_scores = probs * (grad_probs - mean)
        scores_grad[0, head * WT : (head + 1) * WT] = grad_scores[:, :128]
        scores_grad[1, head * WT : (head + 1) * WT, : WT - 128] = grad_scores[:, 128:]
        scores_low = grad_scores.astype(BF)
        grad_q.append(matmul_t(k_t, scores_low) * scale)
        grad_k.append(matmul(q_t, scores_low) * scale)
    grad_qkv_t32 = jnp.concatenate(grad_q + grad_k + grad_v, axis=0)
    grad_qkv_t = grad_qkv_t32.astype(BF)
    grad_qkv_w = matmul(grad_qkv_t, normed)
    grad_proj = matmul_t(dy_t, jnp.concatenate(attended_t, axis=0).astype(BF))
    each = n_qkv + n_proj
    for k in range(parts):
        sums[k * each : k * each + n_qkv] = grad_qkv_w[k * n_qkv : (k + 1) * n_qkv]
        sums[k * each + n_qkv : (k + 1) * each] = grad_proj[k * n_proj : (k + 1) * n_proj]
    half = each // 2
    size = half // pieces
    for k in range(parts):
        for p in range(pieces):
            mine = k * each + side_index() * half + p * size
            other = k * each + (1 - side_index()) * half + p * size
            at = (k * pieces + p) * 3 * size // 4
            rows = slice(at, at + 3 * size // 4)
            keep[rows] = folded(sums[pl.ds(pl.multiple_of(mine, 16), size), :])
            send[rows] = folded(sums[pl.ds(pl.multiple_of(other, 16), size), :]).astype(BF)
    weighted = jnp.sum(grad_qkv_w * qkv_w[...].astype(F32), axis=0, keepdims=True)
    gain_sum[...] = jnp.broadcast_to(weighted / gain, (8, C))
    grad_qkv[...] = grad_qkv_t32
    unit_out[...] = unit
    scale_out[:WT] = jnp.broadcast_to(inverse, (WT, C))
    scale_out[WT:] = jnp.broadcast_to(gain, (16, C))


def table_kernel(scores_grad, table):
    count = H * ROWS
    row, target = offsets(288, WT, 0)
    total = jnp.zeros((count, 288), F32)
    for u in range(WL):
        onehot = jnp.where(row == target + u, 1.0, 0.0).astype(BF)
        rows = pl.ds(u, count, stride=WL)
        wide = jnp.concatenate(
            [scores_grad[0, rows, :], scores_grad[1, rows, :][:, : WT - 128]], axis=1
        )
        total += matmul_t(wide.astype(BF), onehot)
    tail = total[:, LEAD : LEAD + SPAN]
    tail = jnp.concatenate([tail[h * ROWS : (h + 1) * ROWS] for h in range(H)], axis=1)
    tail = jnp.concatenate([tail, jnp.zeros((ROWS, WIDE - H * SPAN), F32)], axis=1)
    rest = jnp.zeros((16 - ROWS, WIDE), F32)
    table[...] = jnp.concatenate([total[:, :WIDE], tail, rest], axis=0).astype(BF)


def token_kernel(grad_qkv_t, unit, scales, qkv_w, order_t, quads, south):
    grad_normed = matmul(grad_qkv_t[...].T.astype(BF), qkv_w[...])
    inverse = scales[:WT]
    scaled = grad_normed * scales[WT : WT + 1]
    first = jnp.sum(scaled, axis=-1, keepdims=True) * (1.0 / C)
    second = jnp.sum(scaled * unit[...], axis=-1, keepdims=True) * (1.0 / C)
    grad_x = inverse * (scaled - first - unit[...] * second)
    every = matmul(order_t[...], grad_x.astype(BF))
    quads[...] = every[: 2 * QUAD].astype(BF)
    south[...] = folded(every[2 * QUAD :]).astype(BF)


def east_kernel(quads, south, east):
    corner = unfolded(south[...].astype(F32))[QUAD:]
    east[...] = folded(jnp.concatenate([quads[QUAD:].astype(F32), corner], axis=0)).astype(BF)


def finish_kernel(dy, quads, south, east, out):
    gap = jnp.zeros((WZ, SA, 4, C), F32)

    def low(value):
        return jnp.concatenate([value.reshape(WZ, SA, 8, C), gap], axis=2)

    def high(value):
        return jnp.concatenate([gap, value.reshape(WZ, SA, 8, C)], axis=2)

    lon_halo = unfolded(east[...].astype(F32))
    lat_halo = unfolded(south[...].astype(F32))[:QUAD]
    upper = dy[:, :SA].astype(F32) + low(lon_halo[QUAD:]) + high(lat_halo)
    lower = dy[:, SA:].astype(F32) + low(lon_halo[:QUAD]) + high(quads[:QUAD].astype(F32))
    out[:, :SA] = upper.astype(BF)
    out[:, SA:] = lower.astype(BF)


def widened(rows):
    return jnp.concatenate([rows, jnp.zeros((rows.shape[0], WIDE - C), F32)], axis=1)


def chip_index():
    return lax.div(lax.axis_index("lon"), 2)


def plane_kernel(keep, got, gain_sum, table, mine, to_dp, to_lon, to_both):
    rows = keep.shape[0] // 4

    def piece(other_dp, other_chip):
        dp = dp_index() if not other_dp else 1 - dp_index()
        chip = chip_index() if not other_chip else 1 - chip_index()
        at = pl.ds(pl.multiple_of((2 * dp + chip) * rows, 8), rows)
        return keep[at, :] + got[at, :].astype(F32)

    mine[...] = piece(False, False)
    to_dp[...] = jnp.concatenate(
        [piece(True, False), widened(gain_sum[...]), table[...].astype(F32)], axis=0
    ).astype(BF)
    to_lon[...] = piece(False, True).astype(BF)
    to_both[...] = piece(True, True).astype(BF)


def plane_sum_kernel(mine, sent, from_both, from_dp, from_lon, halo, out, table):
    rows = mine.shape[0]
    got = from_dp[...].astype(F32)
    dense = mine[...] + got[:rows] + from_lon[...].astype(F32) + from_both[...].astype(F32)
    shared = sent[...].astype(F32)[rows:] + got[rows:]
    out[...] = jnp.concatenate([dense, shared[:8], halo[...].astype(F32)], axis=0).astype(BF)
    table[...] = shared[8:].astype(BF)


def sum_kernel(sent, got, out):
    out[...] = (sent[...].astype(F32) + got[...].astype(F32)).astype(BF)


def relay_kernel(sent, got, out):
    sent, got = sent[...].astype(F32), got[...].astype(F32)
    rows = sent.shape[0] - HALO
    out[...] = jnp.concatenate([sent[:rows] + got[:rows], sent[rows:]], axis=0).astype(BF)


def lon_kernel(sent, got, before, quads, out, south, east):
    sent, got = sent[...].astype(F32), got[...].astype(F32)
    rows = sent.shape[0] - HALO
    halo = jnp.where(
        lax.rem(lax.axis_index("lat"), 2) == 1, before[...].astype(F32)[rows:], got[rows:]
    )
    south[...] = halo.astype(BF)
    corner = unfolded(halo)[QUAD:]
    halo = folded(jnp.concatenate([quads[QUAD:].astype(F32), corner], axis=0))
    east[...] = halo.astype(BF)
    out[...] = jnp.concatenate([sent[:rows] + got[:rows], halo], axis=0).astype(BF)


def join_kernel(sent, got, out):
    sent, got = sent[...].astype(F32), got[...].astype(F32)
    rows = sent.shape[0] - HALO - 8
    first = chip_index() == 0
    low = jnp.where(first, sent[:rows], got[:rows])
    high = jnp.where(first, got[:rows], sent[:rows])
    gain_sum = sent[rows : rows + 8] + got[rows : rows + 8]
    out[...] = jnp.concatenate([low, high, gain_sum], axis=0).astype(BF)


def choose_kernel(got, earlier, out):
    rows = earlier.shape[0] - HALO
    earlier = earlier[...].astype(F32)[rows:]
    odd = lax.rem(lax.axis_index("lon"), 2) == 1
    out[...] = jnp.where(odd, got[...].astype(F32), earlier).astype(BF)


def last_table_kernel(sent, got, table_out, table_s, sem):
    table = sent[...].astype(F32) + got[...].astype(F32)
    count = H * ROWS
    tail = table[count : count + ROWS]
    tail = jnp.concatenate([tail[:, h * SPAN : (h + 1) * SPAN] for h in range(H)], axis=0)
    table = jnp.concatenate([table[:count, :LEAD], tail], axis=1)
    for h in range(H):
        rows = [table[h * ROWS + a : h * ROWS + a + 1] for a in range(ROWS)]
        table_s[h] = jnp.concatenate(rows, axis=1)
    copy = pltpu.make_async_copy(table_s, table_out, sem)
    copy.start()
    copy.wait()


def last_kernel(sent, got, qkv_out, proj_out, gain_out, dense_s, gain_s, sems):
    sent, got = sent[...].astype(F32), got[...].astype(F32)
    rows = (sent.shape[0] - 8) // 2
    size = 4 * rows // 3
    gain_sum = sent[2 * rows : 2 * rows + 1] + got[2 * rows : 2 * rows + 1]
    gain_s[...] = jnp.where(dp_index() == 0, gain_sum[:, : C // 2], gain_sum[:, C // 2 : C])
    for side, value in ((side_index(), sent), (1 - side_index(), got)):
        for p in range(2):
            at = pl.ds(pl.multiple_of((2 * side + p) * size, 16), size)
            dense_s[at, :] = unfolded(value[p * rows : (p + 1) * rows])
    copies = [
        pltpu.make_async_copy(dense_s.at[: 3 * size], qkv_out, sems.at[0]),
        pltpu.make_async_copy(dense_s.at[3 * size :], proj_out, sems.at[1]),
        pltpu.make_async_copy(gain_s, gain_out, sems.at[2]),
    ]
    for copy in copies:
        copy.start()
    for copy in copies:
        copy.wait()


def call(kernel, outs, scratch=(), specs=None, flops=1000000, nbytes=1000000, out_specs=None):
    return pl.pallas_call(
        kernel,
        out_shape=outs,
        in_specs=specs,
        out_specs=jax.tree.map(lambda _: VMEM, outs) if out_specs is None else out_specs,
        scratch_shapes=list(scratch),
        compiler_params=pltpu.CompilerParams(vmem_limit_bytes=24 << 20),
        cost_estimate=pl.CostEstimate(flops=flops, bytes_accessed=nbytes, transcendentals=0),
    )


def shaped(rows, cols, dtype):
    return jax.ShapeDtypeStruct((rows, cols), dtype)


def exchanged(value, axis, flip):
    count = lax.axis_size(axis)
    return lax.ppermute(value, axis, [(i, i ^ flip) for i in range(count)])


def exchanged_both(value):
    pairs = [(2 * i + k, 2 * (i ^ 3) + (1 - k)) for i in range(4) for k in range(2)]
    return lax.ppermute(value, ("lon", "dp"), pairs)


def tied(*values):
    return lax.optimization_barrier(values)


def passed_along(value, axis, steps):
    count = lax.axis_size(axis)
    return lax.ppermute(value, axis, [(i, (i + steps) % count) for i in range(count)])


def passed_diagonally(value, steps):
    rows, cols = lax.axis_size("lon"), lax.axis_size("lat")
    pairs = [
        (i * cols + j, ((i + steps) % rows) * cols + (j + steps) % cols)
        for i in range(rows)
        for j in range(cols)
    ]
    return lax.ppermute(value, ("lon", "lat"), pairs)


def body(tokens, grad_out, qkv_weight, proj_weight, norm_gain, bias_table):
    parts = lax.axis_size("dp")
    lon_count, lat_count = lax.axis_size("lon"), lax.axis_size("lat")
    fast = (lon_count, lat_count, parts) == (4, 4, 2)
    n_qkv, n_proj = 3 * C // parts, C // parts
    each = n_qkv + n_proj
    half = each // 2
    tok = tokens.reshape(WZ, WA, WL, C)
    dy = grad_out.reshape(WZ, WA, WL, C)

    strips = [shaped(HALO, WIDE, BF)] * 3
    dense, east, south, corner = call(
        functools.partial(pack_kernel, parts), [shaped(each + 16, C, BF)] + strips, specs=[VMEM] * 5
    )(tok, dy, qkv_weight, proj_weight, norm_gain.reshape(1, n_proj))
    gathered = [dense] + [passed_along(dense, "dp", -k) for k in range(1, parts)]
    south = passed_along(south, "lat", -1)
    corner = passed_diagonally(corner, -1)
    east = passed_along(east, "lon", -1)
    bias = call(
        bias_kernel,
        jax.ShapeDtypeStruct((2, H * WT, 128), F32),
        specs=[VMEM],
        flops=200000000,
    )(bias_table.reshape(H * ROWS, ROWS * SPAN))
    order = token_order()
    packed = parts * 3 * half // 4
    outs = [
        shaped(packed, WIDE, BF),
        shaped(packed, WIDE, F32),
        shaped(8, C, F32),
        jax.ShapeDtypeStruct((2, H * WT, 128), F32),
        shaped(3 * C, WT, F32),
        shaped(WT, C, F32),
        shaped(WT + 16, C, F32),
        shaped(3 * C, C, BF),
    ]
    scratch = [pltpu.VMEM((C, C), BF), pltpu.VMEM((4 * C, C), F32)]
    send, keep, gain_sum, scores_grad, grad_qkv, unit, scales, qkv_full = call(
        functools.partial(main_kernel, parts, 2 if fast else 1),
        outs,
        scratch,
        specs=[VMEM] * (7 + parts),
    )(south, corner, east, tok, dy, bias, jnp.asarray(order, BF), *gathered)
    if fast:
        got = exchanged(send, "lon", 1)
    table = call(table_kernel, shaped(TABLE, WIDE, BF), specs=[VMEM], flops=200000000)(scores_grad)
    if fast:
        piece = packed // 4
        mine, sent, to_lon, to_both = call(
            plane_kernel,
            [
                shaped(piece, WIDE, F32),
                shaped(piece + 8 + TABLE, WIDE, BF),
                shaped(piece, WIDE, BF),
                shaped(piece, WIDE, BF),
            ],
            specs=[VMEM] * 4,
        )(keep, got, gain_sum, table)
        from_both = exchanged_both(to_both)
        got = exchanged(sent, "dp", 1)
        from_lon = exchanged(to_lon, "lon", 3)
    quads, south = call(
        token_kernel,
        [shaped(2 * QUAD, C, BF), shaped(HALO, WIDE, BF)],
        specs=[VMEM] * 5,
        flops=100000000,
    )(grad_qkv, unit, scales, qkv_full, jnp.asarray(order.T, BF))
    if fast:
        lat_shape = shaped(piece + 8 + HALO, WIDE, BF)
        table_shape = shaped(TABLE, WIDE, BF)
        halo_shape = shaped(HALO, WIDE, BF)
        sent, table = call(plane_sum_kernel, [lat_shape, table_shape], specs=[VMEM] * 6)(
            mine, sent, from_both, got, from_lon, south
        )
        before = exchanged(sent, "lat", 1)
        sent = call(relay_kernel, lat_shape, specs=[VMEM] * 2)(sent, before)
        sent, table = tied(sent, table)
        got = exchanged(sent, "lat", 3)
        table_got = exchanged(table, "lon", 3)
        sent, south, east = call(
            lon_kernel, [lat_shape, halo_shape, halo_shape], specs=[VMEM] * 4
        )(sent, got, before, quads)
        sent, table_got = tied(sent, table_got)
        got = exchanged(sent, "lon", 3)
        table = call(sum_kernel, table_shape, specs=[VMEM] * 2)(table, table_got)
        table_got = exchanged(table, "lon", 1)
        east_got = exchanged(east, "lon", 1)
        east = call(choose_kernel, halo_shape, specs=[VMEM] * 2)(east_got, got)
    else:
        south = passed_along(south, "lat", 1)
        east = call(east_kernel, shaped(HALO, WIDE, BF), specs=[VMEM] * 2)(quads, south)
        east = passed_along(east, "lon", 1)
    tile = (WZ, WA, WL, C)
    finish = call(finish_kernel, jax.ShapeDtypeStruct(tile, BF), specs=[VMEM] * 4)
    hbm = pl.BlockSpec(memory_space=pltpu.HBM)
    if fast:
        sent = call(join_kernel, shaped(2 * piece + 8, WIDE, BF), specs=[VMEM] * 2)(sent, got)
        sent, table_got, east = tied(sent, table_got, east)
        got = exchanged(sent, "lon", 1)
        grad_table = call(
            last_table_kernel,
            jax.ShapeDtypeStruct((H, 1, POS), F32),
            [pltpu.VMEM((H, 1, POS), F32), pltpu.SemaphoreType.DMA],
            specs=[VMEM] * 2,
            out_specs=hbm,
        )(table, table_got).reshape(1, H, POS)
        grad_tokens = finish(dy, quads, south, east).reshape(tokens.shape)
        got, grad_tokens, grad_table = tied(got, grad_tokens, grad_table)
        grad_qkv_w, grad_proj, grad_gain = call(
            last_kernel,
            [shaped(n_qkv, C, F32), shaped(n_proj, C, F32), shaped(1, n_proj, F32)],
            [
                pltpu.VMEM((each, C), F32),
                pltpu.VMEM((1, n_proj), F32),
                pltpu.SemaphoreType.DMA((3,)),
            ],
            specs=[VMEM] * 2,
            out_specs=[hbm] * 3,
        )(sent, got)
        return grad_tokens, grad_qkv_w, grad_proj, grad_gain.reshape(n_proj), grad_table
    grad_tokens = finish(dy, quads, south, east).reshape(tokens.shape)
    pair = jnp.stack([keep, send.astype(F32)]).reshape(2, parts, packed // parts, WIDE)
    pair = jnp.where(side_index() == 0, pair, pair[::-1])
    pair = jax.vmap(jax.vmap(unfolded))(pair)
    dense_sum = lax.psum(pair.transpose(1, 0, 2, 3).reshape(parts * each, C), ("lon", "lat"))
    total = lax.psum_scatter(dense_sum, "dp", scatter_dimension=0, tiled=True)
    grad_gain = lax.psum(gain_sum[0], ("lon", "lat"))
    grad_gain = lax.psum_scatter(grad_gain, "dp", scatter_dimension=0, tiled=True)
    table = lax.psum(table.astype(F32), ("lon", "dp"))
    count = H * ROWS
    tail = table[count : count + ROWS, : H * SPAN].reshape(ROWS, H, SPAN)
    tail = tail.transpose(1, 0, 2).reshape(count, SPAN)
    table = jnp.concatenate([table[:count, :LEAD], tail], axis=1)
    return (
        grad_tokens,
        total[:n_qkv],
        total[n_qkv:],
        grad_gain,
        table.reshape(1, H, POS),
    )


def solution(mesh):
    spec = P("dp", None, "lat", "lon", None)
    return jax.shard_map(
        body,
        mesh=mesh,
        in_specs=(spec, spec, P("dp", None), P("dp", None), P("dp"), P("lat", None, None)),
        out_specs=(spec, P("dp", None), P("dp", None), P("dp"), P("lat", None, None)),
        check_vma=False,
    )
```

time: 46.6 us -> 43.9 us (0.942)
  waiting for transfers between devices: 22.4 us -> 13 us
  starting transfers between devices: 12.3 us -> 18.2 us
  Pallas kernels: 8.09 us -> 9.1 us
    ppermute x6 -> x10, waiting for transfers between devices: 20.8 us -> 10.6 us  [exchanged(): return lax.ppermute(value, axis, [(i, i ^ flip) for i in range(count)])]
    ppermute x6 -> x10, starting transfers between devices: 4.46 us -> 7.8 us  [exchanged(): return lax.ppermute(value, axis, [(i, i ^ flip) for i in range(count)])]
    ppermute x0 -> x1, starting transfers between devices: none -> 2.12 us  [exchanged_both(): return lax.ppermute(value, ('lon', 'dp'), pairs)]
    ppermute x0 -> x1, waiting for transfers between devices: none -> 2.08 us  [exchanged_both(): return lax.ppermute(value, ('lon', 'dp'), pairs)]
    ppermute x1, waiting for transfers between devices: 1.5 us -> 0.31 us  [passed_diagonally(): return lax.ppermute(value, ('lon', 'lat'), pairs)]
    pallas_call x9 -> x13, Pallas kernels: 6.98 us -> 7.93 us  [the longest x1 4.13 us: body(): call(functools.partial(main_kernel, parts, 2 if fast else 1), outs, scrat...]
    ppermute x3, starting transfers between devices: 7.24 us -> 8.01 us  [passed_along(): lax.ppermute(value, axis, [(i, (i + steps) % count) for i in range(count)])]
  transfers between devices with their start and end apart: 10 -> 15, of which waited for: 8 -> 8; matrix products, arithmetic and copies ran while one was open for 1% -> 1% of each run, Pallas kernels for 5% -> 9%
where the time goes in v3:
time: 43.9 us; the launch traced here: 43.8 us
  starting transfers between devices  18.2 us (41%)
  waiting for transfers between devices  13 us (30%)
  Pallas kernels  9.1 us (21%)
  local copies, waits for them, and re-layouts  2.46 us (6%)
  between operations  0.8 us (2%)
    ppermute x10, waiting for transfers between devices, exchanged(): return lax.ppermute(value, axis, [(i, i ^ flip) for i in range(count)])  10.6 us
    ppermute x3, starting transfers between devices, passed_along(): lax.ppermute(value, axis, [(i, (i + steps) % count) for i in range(count)])  8.01 us
    ppermute x10, starting transfers between devices, exchanged(): return lax.ppermute(value, axis, [(i, i ^ flip) for i in range(count)])  7.8 us
    pallas_call x1, Pallas kernels, body(): call(functools.partial(main_kernel, parts, 2 if fast else 1), outs, scrat...  4.13 us
    ppermute x1, starting transfers between devices, exchanged_both(): return lax.ppermute(value, ('lon', 'dp'), pairs)  2.12 us
    ppermute x1, waiting for transfers between devices, exchanged_both(): return lax.ppermute(value, ('lon', 'dp'), pairs)  2.08 us
    unnamed x13, local copies, waits for them, and re-layouts  1.36 us
    pallas_call x1, Pallas kernels, body(): call(bias_kernel, jax.ShapeDtypeStruct((2, H * WT, 128), F32), specs=[VME...  1.03 us
  transfers between devices with their start and end apart: 15, of which 8 were waited for; matrix products, arithmetic and copies ran while one was open for 1% of the time, Pallas kernels for 9%

profile of v3, /device:TPU:0, one launch (start us, length us, event | category | flops | bytes accessed | tf_op | source)
XLA Modules:
  0.0 43.8 jit_solution(2698672689658202617)
XLA Ops:
  0.7 1.0 %copy_bitcast_fusion = (bf16[2,6,12,192]{3,2,1,0:T(8,128)(2,1)S(1)}, bf16[2,6,12,192]{3,2,1,0:T(8,128)(2,1)S(1)}) fusion(bf16[1,2,6,12,192]{4,1,3,2,0:T(2,128)(2,1)} %param.9, bf16[1,2,6,12,192]{4,1,3,2,0:T(2,128)(2,1)} %param.8), kind=kLoop, calls=%fused_computation | loop fusion | bytes 221184 | tf_op jit(solution)/shard_map/reshape | solution.py:467
  1.7 0.6 %copy-done.4 = bf16[96]{0:T(256)(128)(2,1)S(1)} copy-done((bf16[96]{0:T(256)(128)(2,1)S(1)}, bf16[96]{0:T(256)(128)(2,1)}, u32[]{:S(2)}) %copy-start.4) | copy-done | bytes 216
  2.5 3.0 %collective-permute-start.3 = (bf16[400,192]{1,0:T(8,128)(2,1)S(1)}, bf16[400,192]{1,0:T(8,128)(2,1)S(1)}, u32[]{:S(2)}, u32[]{:S(2)}) collective-permute-start(bf16[400,192]{1,0:T(8,128)(2,1)S(1)} %get-tuple-element.44.refs_0_), channel_id=1, source_target_pairs={{0,1},{1,0},{2,3},{3,2},{4,5},{5,4},{6,7},{7,6},{8,9},{9,8},{10,11... | collective-permute-start | bytes 460808 | tf_op jit(solution)/shard_map/ppermute | solution.py:446
  5.5 3.6 %collective-permute-start = (bf16[72,256]{1,0:T(8,128)(2,1)S(1)}, bf16[72,256]{1,0:T(8,128)(2,1)S(1)}, u32[]{:S(2)}, u32[]{:S(2)}) collective-permute-start(bf16[72,256]{1,0:T(8,128)(2,1)S(1)} %get-tuple-element.41), channel_id=1, source_target_pairs={{0,6},{2,0},{4,2},{6,4},{1,7},{3,1},{5,3},{7,5},{8,14},{10,8},{12,... | collective-permute-start | bytes 110600 | tf_op jit(solution)/shard_map/ppermute | solution.py:446
  9.3 1.4 %collective-permute-start.2 = (bf16[72,256]{1,0:T(8,128)(2,1)S(1)}, bf16[72,256]{1,0:T(8,128)(2,1)S(1)}, u32[]{:S(2)}, u32[]{:S(2)}) collective-permute-start(bf16[72,256]{1,0:T(8,128)(2,1)S(1)} %get-tuple-element.43), channel_id=1, source_target_pairs={{0,24},{8,0},{16,8},{24,16},{1,25},{9,1},{17,9},{25,17},{2,26},{10... | collective-permute-start | bytes 110600 | tf_op jit(solution)/shard_map/ppermute | solution.py:446
  11.1 1.0 %shard_map.120.bias = f32[2,864,128]{2,1,0:T(8,128)S(1)} custom-call(f32[72,276]{1,0:T(8,128)S(1)} %reshape.34.table), custom_call_target="tpu_custom_call" | custom-call | flops 200000000 | bytes 1000000 | tf_op jit(solution)/shard_map/pallas_call | solution.py:477
  12.5 4.1 %shard_map.121 = (bf16[288,256]{1,0:T(8,128)(2,1)S(1)}, f32[288,256]{1,0:T(8,128)S(1)}, f32[8,192]{1,0:T(8,128)S(1)}, f32[2,864,128]{2,1,0:T(8,128)S(1)}, f32[57...) custom-call(bf16[72,256]{1,0:T(8,128)(2,1)S(1)} %collective-permute-done.south, ...), custom_call_target="tpu_custom_call" | custom-call | flops 1000000 | bytes 1000000 | tf_op jit(solution)/shard_map/pallas_call | solution.py:496
  16.6 0.6 %collective-permute-start.4 = (bf16[288,256]{1,0:T(8,128)(2,1)S(1)}, bf16[288,256]{1,0:T(8,128)(2,1)S(1)}, u32[]{:S(2)}, u32[]{:S(2)}) collective-permute-start(bf16[288,256]{1,0:T(8,128)(2,1)S(1)} %get-tuple-element.46), channel_id=1, source_target_pairs={{0,8},{8,0},{16,24},{24,16},{1,9},{9,1},{17,25},{25,17},{2,10},{10... | collective-permute-start | bytes 442376 | tf_op jit(solution)/shard_map/ppermute | solution.py:432
  17.2 0.8 %shard_map.122.table = bf16[88,256]{1,0:T(8,128)(2,1)S(1)} custom-call(f32[2,864,128]{2,1,0:T(8,128)S(1)} %get-tuple-element.48.scores_grad), custom_call_target="tpu_custom_call" | custom-call | flops 200000000 | bytes 1000000 | tf_op jit(solution)/shard_map/pallas_call | solution.py:504
  18.3 0.6 %collective-permute-start.6 = (bf16[168,256]{1,0:T(8,128)(2,1)S(1)}, bf16[168,256]{1,0:T(8,128)(2,1)S(1)}, u32[]{:S(2)}, u32[]{:S(2)}) collective-permute-start(bf16[168,256]{1,0:T(8,128)(2,1)S(1)} %get-tuple-element.50.sent), channel_id=1, source_target_pairs={{0,1},{1,0},{2,3},{3,2},{4,5},{5,4},{6,7},{7,6},{8,9},{9,8},{10,11... | collective-permute-start | bytes 258056 | tf_op jit(solution)/shard_map/ppermute | solution.py:432
  18.9 2.1 %collective-permute-start.5 = (bf16[72,256]{1,0:T(8,128)(2,1)S(1)}, bf16[72,256]{1,0:T(8,128)(2,1)S(1)}, u32[]{:S(2)}, u32[]{:S(2)}) collective-permute-start(bf16[72,256]{1,0:T(8,128)(2,1)S(1)} %get-tuple-element.51), channel_id=1, source_target_pairs={{0,25},{1,24},{8,17},{9,16},{16,9},{17,8},{24,1},{25,0},{2,27},{3,... | collective-permute-start | bytes 110600 | tf_op jit(solution)/shard_map/ppermute | solution.py:437
  21.0 0.6 %collective-permute-start.7 = (bf16[72,256]{1,0:T(8,128)(2,1)S(1)}, bf16[72,256]{1,0:T(8,128)(2,1)S(1)}, u32[]{:S(2)}, u32[]{:S(2)}) collective-permute-start(bf16[72,256]{1,0:T(8,128)(2,1)S(1)} %get-tuple-element.52), channel_id=1, source_target_pairs={{0,24},{8,16},{16,8},{24,0},{1,25},{9,17},{17,9},{25,1},{2,26},{10... | collective-permute-start | bytes 110600 | tf_op jit(solution)/shard_map/ppermute | solution.py:432
  21.6 0.7 %shard_map.124 = (bf16[96,192]{1,0:T(8,128)(2,1)S(1)}, bf16[72,256]{1,0:T(8,128)(2,1)S(1)}) custom-call(f32[576,144]{1,0:T(8,128)S(1)} %get-tuple-element.53.grad_qkv_t, f32[144,192]{1,0:T(8,128)S(1)} %get-tuple-element.54.unit, f32[160,192]{1,0:T(8,128)S(1)} %get-tuple-element.55.scales, bf16[576,192]{1,0:T(8,128)(2,1)S(1)} %get-tuple-element.56.qkv_w, ...), custom_call_target="tpu_custom_call" | custom-call | flops 100000000 | bytes 1000000 | tf_op jit(solution)/shard_map/pallas_call | solution.py:520
  22.2 2.1 %collective-permute-done.5.from_both = bf16[72,256]{1,0:T(8,128)(2,1)S(1)} collective-permute-done((bf16[72,256]{1,0:T(8,128)(2,1)S(1)}, bf16[72,256]{1,0:T(8,128)(2,1)S(1)}, u32[]{:S(2)}, u32[]{:S(2)}) %collective-permute-start.5) | collective-permute-done | bytes 36896 | tf_op jit(solution)/shard_map/ppermute | solution.py:437
  24.6 1.6 %collective-permute-start.8 = (bf16[152,256]{1,0:T(8,128)(2,1)S(1)}, bf16[152,256]{1,0:T(8,128)(2,1)S(1)}, u32[]{:S(2)}, u32[]{:S(2)}) collective-permute-start(bf16[152,256]{1,0:T(8,128)(2,1)S(1)} %get-tuple-element.58.sent), channel_id=1, source_target_pairs={{0,2},{2,0},{4,6},{6,4},{1,3},{3,1},{5,7},{7,5},{8,10},{10,8},{12,... | collective-permute-start | bytes 233480 | tf_op jit(solution)/shard_map/ppermute | solution.py:432
  26.2 3.3 %collective-permute-done.8.got.before = bf16[152,256]{1,0:T(8,128)(2,1)S(1)} collective-permute-done((bf16[152,256]{1,0:T(8,128)(2,1)S(1)}, bf16[152,256]{1,0:T(8,128)(2,1)S(1)}, u32[]{:S(2)}, u32[]{:S(2)}) %collective-permute-start.8) | collective-permute-done | bytes 77856 | tf_op jit(solution)/shard_map/ppermute | solution.py:432
  29.5 2.4 %collective-permute-start.9 = (bf16[152,256]{1,0:T(8,128)(2,1)S(1)}, bf16[152,256]{1,0:T(8,128)(2,1)S(1)}, u32[]{:S(2)}, u32[]{:S(2)}) collective-permute-start(bf16[152,256]{1,0:T(8,128)(2,1)S(1)} %shard_map.126.sent), channel_id=1, source_target_pairs={{0,6},{2,4},{4,2},{6,0},{1,7},{3,5},{5,3},{7,1},{8,14},{10,12},{12... | collective-permute-start | bytes 233480 | tf_op jit(solution)/shard_map/ppermute | solution.py:432
  32.0 0.6 %collective-permute-start.10 = (bf16[88,256]{1,0:T(8,128)(2,1)S(1)}, bf16[88,256]{1,0:T(8,128)(2,1)S(1)}, u32[]{:S(2)}, u32[]{:S(2)}) collective-permute-start(bf16[88,256]{1,0:T(8,128)(2,1)S(1)} %get-tuple-element.63.sent), channel_id=1, source_target_pairs={{0,24},{8,16},{16,8},{24,0},{1,25},{9,17},{17,9},{25,1},{2,26},{10... | collective-permute-start | bytes 135176 | tf_op jit(solution)/shard_map/ppermute | solution.py:432
  32.5 3.3 %collective-permute-done.9.got = bf16[152,256]{1,0:T(8,128)(2,1)S(1)} collective-permute-done((bf16[152,256]{1,0:T(8,128)(2,1)S(1)}, bf16[152,256]{1,0:T(8,128)(2,1)S(1)}, u32[]{:S(2)}, u32[]{:S(2)}) %collective-permute-start.9) | collective-permute-done | bytes 77856 | tf_op jit(solution)/shard_map/ppermute | solution.py:432
  36.5 0.7 %collective-permute-start.12 = (bf16[88,256]{1,0:T(8,128)(2,1)S(1)}, bf16[88,256]{1,0:T(8,128)(2,1)S(1)}, u32[]{:S(2)}, u32[]{:S(2)}) collective-permute-start(bf16[88,256]{1,0:T(8,128)(2,1)S(1)} %shard_map.129.sent), channel_id=1, source_target_pairs={{0,8},{8,0},{16,24},{24,16},{1,9},{9,1},{17,25},{25,17},{2,10},{10... | collective-permute-start | bytes 135176 | tf_op jit(solution)/shard_map/ppermute | solution.py:432
  37.3 3.5 %collective-permute-done.11.got.earlier = bf16[152,256]{1,0:T(8,128)(2,1)S(1)} collective-permute-done((bf16[152,256]{1,0:T(8,128)(2,1)S(1)}, bf16[152,256]{1,0:T(8,128)(2,1)S(1)}, u32[]{:S(2)}, u32[]{:S(2)}) %collective-permute-start.11) | collective-permute-done | bytes 77856 | tf_op jit(solution)/shard_map/ppermute | solution.py:432
  41.0 1.0 %shard_map.132 = f32[6,1,3312]{2,1,0:T(1,128)} custom-call(bf16[88,256]{1,0:T(8,128)(2,1)S(1)} %shard_map.129.sent, bf16[88,256]{1,0:T(8,128)(2,1)S(1)} %collective-permute-done.12.got), custom_call_target="tpu_custom_call" | custom-call | flops 1000000 | bytes 1000000 | tf_op jit(solution)/shard_map/pallas_call | solution.py:558
  42.2 0.7 %copy.15 = bf16[1,2,6,12,192]{4,1,3,2,0:T(2,128)(2,1)} copy(bf16[1,2,6,12,192]{4,3,2,1,0:T(8,128)(2,1)S(1)} %bitcast.8) | data formatting | bytes 110592
  42.9 0.8 %shard_map.133 = (f32[288,192]{1,0:T(8,128)}, f32[96,192]{1,0:T(8,128)}, f32[1,96]{1,0:T(1,128)}) custom-call(bf16[152,256]{1,0:T(8,128)(2,1)S(1)} %shard_map.128.sent, bf16[152,256]{1,0:T(8,128)(2,1)S(1)} %collective-permute-done.14.got), custom_call_target="tpu_custom_call" | custom-call | flops 1000000 | bytes 1000000 | tf_op jit(solution)/shard_map/pallas_call | solution.py:567
  (37 shorter events, 2.7 us)
Async XLA Ops:
  0.6 1.0 %copy-start.3 = (bf16[96,192]{1,0:T(8,128)(2,1)S(1)}, bf16[96,192]{1,0:T(8,128)(2,1)}, u32[]{:S(2)}) copy-start(bf16[96,192]{1,0:T(8,128)(2,1)} %proj.1) | copy-start | bytes 110596
  0.6 1.0 %copy-start = (bf16[288,192]{1,0:T(8,128)(2,1)S(1)}, bf16[288,192]{1,0:T(8,128)(2,1)}, u32[]{:S(2)}) copy-start(bf16[288,192]{1,0:T(8,128)(2,1)} %qkv.1) | copy-start | bytes 331780
  1.6 0.7 %copy-start.4 = (bf16[96]{0:T(256)(128)(2,1)S(1)}, bf16[96]{0:T(256)(128)(2,1)}, u32[]{:S(2)}) copy-start(bf16[96]{0:T(256)(128)(2,1)} %param.12) | copy-start | bytes 580
  2.3 8.5 %copy-start.5 = (f32[1,6,3312]{2,0,1:T(1,128)S(1)}, f32[1,6,3312]{2,0,1:T(1,128)}, u32[]{:S(2)}) copy-start(f32[1,6,3312]{2,0,1:T(1,128)} %param.13) | copy-start | bytes 238468
  2.5 10.0 %collective-permute-start.3 = (bf16[400,192]{1,0:T(8,128)(2,1)S(1)}, bf16[400,192]{1,0:T(8,128)(2,1)S(1)}, u32[]{:S(2)}, u32[]{:S(2)}) collective-permute-start(bf16[400,192]{1,0:T(8,128)(2,1)S(1)} %get-tuple-element.44.refs_0_), channel_id=1, source_target_pairs={{0,1},{1,0},{2,3},{3,2},{4,5},{5,4},{6,7},{7,6},{8,9},{9,8},{10,11... | collective-permute-start | bytes 460808 | tf_op jit(solution)/shard_map/ppermute | solution.py:446
  5.5 6.7 %collective-permute-start = (bf16[72,256]{1,0:T(8,128)(2,1)S(1)}, bf16[72,256]{1,0:T(8,128)(2,1)S(1)}, u32[]{:S(2)}, u32[]{:S(2)}) collective-permute-start(bf16[72,256]{1,0:T(8,128)(2,1)S(1)} %get-tuple-element.41), channel_id=1, source_target_pairs={{0,6},{2,0},{4,2},{6,4},{1,7},{3,1},{5,3},{7,5},{8,14},{10,8},{12,... | collective-permute-start | bytes 110600 | tf_op jit(solution)/shard_map/ppermute | solution.py:446
  9.1 3.4 %collective-permute-start.1 = (bf16[72,256]{1,0:T(8,128)(2,1)S(1)}, bf16[72,256]{1,0:T(8,128)(2,1)S(1)}, u32[]{:S(2)}, u32[]{:S(2)}) collective-permute-start(bf16[72,256]{1,0:T(8,128)(2,1)S(1)} %get-tuple-element.42), channel_id=1, source_target_pairs={{0,30},{2,24},{4,26},{6,28},{8,6},{10,0},{12,2},{14,4},{16,14},{18... | collective-permute-start | bytes 110600 | tf_op jit(solution)/shard_map/ppermute | solution.py:456
  9.3 3.1 %collective-permute-start.2 = (bf16[72,256]{1,0:T(8,128)(2,1)S(1)}, bf16[72,256]{1,0:T(8,128)(2,1)S(1)}, u32[]{:S(2)}, u32[]{:S(2)}) collective-permute-start(bf16[72,256]{1,0:T(8,128)(2,1)S(1)} %get-tuple-element.43), channel_id=1, source_target_pairs={{0,24},{8,0},{16,8},{24,16},{1,25},{9,1},{17,9},{25,17},{2,26},{10... | collective-permute-start | bytes 110600 | tf_op jit(solution)/shard_map/ppermute | solution.py:446
  11.1 1.4 %copy-start.2 = (bf16[144,192]{1,0:T(8,128)(2,1)S(1)}, bf16[144,192]{1,0:T(8,128)(2,1)}, u32[]{:S(2)}) copy-start(bf16[144,192]{1,0:T(8,128)(2,1)} %constant.4.clone.order) | copy-start | bytes 165892
  16.6 1.6 %collective-permute-start.4 = (bf16[288,256]{1,0:T(8,128)(2,1)S(1)}, bf16[288,256]{1,0:T(8,128)(2,1)S(1)}, u32[]{:S(2)}, u32[]{:S(2)}) collective-permute-start(bf16[288,256]{1,0:T(8,128)(2,1)S(1)} %get-tuple-element.46), channel_id=1, source_target_pairs={{0,8},{8,0},{16,24},{24,16},{1,9},{9,1},{17,25},{25,17},{2,10},{10... | collective-permute-start | bytes 442376 | tf_op jit(solution)/shard_map/ppermute | solution.py:432
  18.2 3.3 %copy-start.1 = (bf16[192,144]{1,0:T(8,128)(2,1)S(1)}, bf16[192,144]{1,0:T(8,128)(2,1)}, u32[]{:S(2)}) copy-start(bf16[192,144]{1,0:T(8,128)(2,1)} %constant.5.clone.order_t) | copy-start | bytes 165892
  18.3 6.3 %collective-permute-start.6 = (bf16[168,256]{1,0:T(8,128)(2,1)S(1)}, bf16[168,256]{1,0:T(8,128)(2,1)S(1)}, u32[]{:S(2)}, u32[]{:S(2)}) collective-permute-start(bf16[168,256]{1,0:T(8,128)(2,1)S(1)} %get-tuple-element.50.sent), channel_id=1, source_target_pairs={{0,1},{1,0},{2,3},{3,2},{4,5},{5,4},{6,7},{7,6},{8,9},{9,8},{10,11... | collective-permute-start | bytes 258056 | tf_op jit(solution)/shard_map/ppermute | solution.py:432
  18.9 5.4 %collective-permute-start.5 = (bf16[72,256]{1,0:T(8,128)(2,1)S(1)}, bf16[72,256]{1,0:T(8,128)(2,1)S(1)}, u32[]{:S(2)}, u32[]{:S(2)}) collective-permute-start(bf16[72,256]{1,0:T(8,128)(2,1)S(1)} %get-tuple-element.51), channel_id=1, source_target_pairs={{0,25},{1,24},{8,17},{9,16},{16,9},{17,8},{24,1},{25,0},{2,27},{3,... | collective-permute-start | bytes 110600 | tf_op jit(solution)/shard_map/ppermute | solution.py:437
  21.0 3.6 %collective-permute-start.7 = (bf16[72,256]{1,0:T(8,128)(2,1)S(1)}, bf16[72,256]{1,0:T(8,128)(2,1)S(1)}, u32[]{:S(2)}, u32[]{:S(2)}) collective-permute-start(bf16[72,256]{1,0:T(8,128)(2,1)S(1)} %get-tuple-element.52), channel_id=1, source_target_pairs={{0,24},{8,16},{16,8},{24,0},{1,25},{9,17},{17,9},{25,1},{2,26},{10... | collective-permute-start | bytes 110600 | tf_op jit(solution)/shard_map/ppermute | solution.py:432
  24.6 4.9 %collective-permute-start.8 = (bf16[152,256]{1,0:T(8,128)(2,1)S(1)}, bf16[152,256]{1,0:T(8,128)(2,1)S(1)}, u32[]{:S(2)}, u32[]{:S(2)}) collective-permute-start(bf16[152,256]{1,0:T(8,128)(2,1)S(1)} %get-tuple-element.58.sent), channel_id=1, source_target_pairs={{0,2},{2,0},{4,6},{6,4},{1,3},{3,1},{5,7},{7,5},{8,10},{10,8},{12,... | collective-permute-start | bytes 233480 | tf_op jit(solution)/shard_map/ppermute | solution.py:432
  29.5 6.3 %collective-permute-start.9 = (bf16[152,256]{1,0:T(8,128)(2,1)S(1)}, bf16[152,256]{1,0:T(8,128)(2,1)S(1)}, u32[]{:S(2)}, u32[]{:S(2)}) collective-permute-start(bf16[152,256]{1,0:T(8,128)(2,1)S(1)} %shard_map.126.sent), channel_id=1, source_target_pairs={{0,6},{2,4},{4,2},{6,0},{1,7},{3,5},{5,3},{7,1},{8,14},{10,12},{12... | collective-permute-start | bytes 233480 | tf_op jit(solution)/shard_map/ppermute | solution.py:432
  32.0 4.1 %collective-permute-start.10 = (bf16[88,256]{1,0:T(8,128)(2,1)S(1)}, bf16[88,256]{1,0:T(8,128)(2,1)S(1)}, u32[]{:S(2)}, u32[]{:S(2)}) collective-permute-start(bf16[88,256]{1,0:T(8,128)(2,1)S(1)} %get-tuple-element.63.sent), channel_id=1, source_target_pairs={{0,24},{8,16},{16,8},{24,0},{1,25},{9,17},{17,9},{25,1},{2,26},{10... | collective-permute-start | bytes 135176 | tf_op jit(solution)/shard_map/ppermute | solution.py:432
  36.1 4.7 %collective-permute-start.11 = (bf16[152,256]{1,0:T(8,128)(2,1)S(1)}, bf16[152,256]{1,0:T(8,128)(2,1)S(1)}, u32[]{:S(2)}, u32[]{:S(2)}) collective-permute-start(bf16[152,256]{1,0:T(8,128)(2,1)S(1)} %get-tuple-element.64.sent), channel_id=1, source_target_pairs={{0,24},{8,16},{16,8},{24,0},{1,25},{9,17},{17,9},{25,1},{2,26},{10... | collective-permute-start | bytes 233480 | tf_op jit(solution)/shard_map/ppermute | solution.py:432
  36.5 4.3 %collective-permute-start.12 = (bf16[88,256]{1,0:T(8,128)(2,1)S(1)}, bf16[88,256]{1,0:T(8,128)(2,1)S(1)}, u32[]{:S(2)}, u32[]{:S(2)}) collective-permute-start(bf16[88,256]{1,0:T(8,128)(2,1)S(1)} %shard_map.129.sent), channel_id=1, source_target_pairs={{0,8},{8,0},{16,24},{24,16},{1,9},{9,1},{17,25},{25,17},{2,10},{10... | collective-permute-start | bytes 135176 | tf_op jit(solution)/shard_map/ppermute | solution.py:432
  37.3 3.6 %collective-permute-start.13 = (bf16[72,256]{1,0:T(8,128)(2,1)S(1)}, bf16[72,256]{1,0:T(8,128)(2,1)S(1)}, u32[]{:S(2)}, u32[]{:S(2)}) collective-permute-start(bf16[72,256]{1,0:T(8,128)(2,1)S(1)} %get-tuple-element.66), channel_id=1, source_target_pairs={{0,8},{8,0},{16,24},{24,16},{1,9},{9,1},{17,25},{25,17},{2,10},{10... | collective-permute-start | bytes 110600 | tf_op jit(solution)/shard_map/ppermute | solution.py:432
  40.9 1.3 %collective-permute-start.14 = (bf16[152,256]{1,0:T(8,128)(2,1)S(1)}, bf16[152,256]{1,0:T(8,128)(2,1)S(1)}, u32[]{:S(2)}, u32[]{:S(2)}) collective-permute-start(bf16[152,256]{1,0:T(8,128)(2,1)S(1)} %shard_map.128.sent), channel_id=1, source_target_pairs={{0,8},{8,0},{16,24},{24,16},{1,9},{9,1},{17,25},{25,17},{2,10},{10... | collective-permute-start | bytes 233480 | tf_op jit(solution)/shard_map/ppermute | solution.py:432

commit v4 on v3

--- a/solution.py
+++ b/solution.py
@@ -191,39 +191,35 @@
     dy_t = dyw.astype(F32).T.astype(BF)
     scale = 1.0 / math.sqrt(HD)
 
-    def alone(part, head):
-        pieces = []
-        if head:
-            pieces.append(jnp.zeros((head * HD, WT), BF))
-        pieces.append(part)
-        if head < H - 1:
-            pieces.append(jnp.zeros(((H - 1 - head) * HD, WT), BF))
-        return jnp.concatenate(pieces, axis=0)
-
     def both(ref, at):
         rows = slice(at, at + WT)
         return jnp.concatenate([ref[0, rows], ref[1, rows, : WT - 128]], axis=1)
 
     attended_t, grad_q, grad_k, grad_v = [], [], [], []
-    for head in range(H):
-        at = head * HD
-        q_t = qkv_t[at : at + HD]
-        k_t = qkv_t[C + at : C + at + HD]
-        v_t = qkv_t[2 * C + at : 2 * C + at + HD]
-        scores = matmul(query, alone(k_t, head)) * scale + both(bias, head * WT)
-        expo = jnp.exp(scores - jnp.max(scores, axis=-1, keepdims=True))
-        probs = expo * (1.0 / jnp.sum(expo, axis=-1, keepdims=True))
-        probs_low = probs.astype(BF)
-        attended_t.append(matmul_t(v_t, probs_low))
-        grad_probs = matmul(grad_att, alone(v_t, head))
-        grad_v.append(matmul(grad_att_t[at : at + HD], probs_low))
-        mean = jnp.sum(probs * grad_probs, axis=-1, keepdims=True)
-        grad_scores = probs * (grad_probs - mean)
-        scores_grad[0, head * WT : (head + 1) * WT] = grad_scores[:, :128]
-        scores_grad[1, head * WT : (head + 1) * WT, : WT - 128] = grad_scores[:, 128:]
-        scores_low = grad_scores.astype(BF)
-        grad_q.append(matmul_t(k_t, scores_low) * scale)
-        grad_k.append(matmul(q_t, scores_low) * scale)
+    for group in range(0, H, 6):
+        heads = range(group, group + 6)
+        spans = [slice(head * HD, (head + 1) * HD) for head in heads]
+        q_t = [qkv_t[span] for span in spans]
+        k_t = [qkv_t[C:][span] for span in spans]
+        v_t = [qkv_t[2 * C :][span] for span in spans]
+        scores = [
+            matmul(query[:, span], k) * scale + both(bias, head * WT)
+            for head, span, k in zip(heads, spans, k_t)
+        ]
+        grad_probs = [matmul(grad_att[:, span], v) for span, v in zip(spans, v_t)]
+        expo = [jnp.exp(s - jnp.max(s, axis=-1, keepdims=True)) for s in scores]
+        probs = [e * (1.0 / jnp.sum(e, axis=-1, keepdims=True)) for e in expo]
+        probs_low = [p.astype(BF) for p in probs]
+        means = [jnp.sum(p * g, axis=-1, keepdims=True) for p, g in zip(probs, grad_probs)]
+        grad_scores = [p * (g - m) for p, g, m in zip(probs, grad_probs, means)]
+        scores_low = [g.astype(BF) for g in grad_scores]
+        attended_t += [matmul_t(v, p) for v, p in zip(v_t, probs_low)]
+        grad_v += [matmul(grad_att_t[span], p) for span, p in zip(spans, probs_low)]
+        grad_q += [matmul_t(k, g) * scale for k, g in zip(k_t, scores_low)]
+        grad_k += [matmul(q, g) * scale for q, g in zip(q_t, scores_low)]
+        for head, value in zip(heads, grad_scores):
+            scores_grad[0, head * WT : (head + 1) * WT] = value[:, :128]
+            scores_grad[1, head * WT : (head + 1) * WT, : WT - 128] = value[:, 128:]
     grad_qkv_t32 = jnp.concatenate(grad_q + grad_k + grad_v, axis=0)
     grad_qkv_t = grad_qkv_t32.astype(BF)
     grad_qkv_w = matmul(grad_qkv_t, normed)
@@ -285,21 +281,25 @@
     east[...] = folded(jnp.concatenate([quads[QUAD:].astype(F32), corner], axis=0)).astype(BF)
 
 
-def finish_kernel(dy, quads, south, east, out):
-    gap = jnp.zeros((WZ, SA, 4, C), F32)
-
-    def low(value):
-        return jnp.concatenate([value.reshape(WZ, SA, 8, C), gap], axis=2)
-
-    def high(value):
-        return jnp.concatenate([gap, value.reshape(WZ, SA, 8, C)], axis=2)
-
+def finish_kernel(dy, quads, south, east, out, out_s, sem):
+    gap = jnp.zeros((4, C), F32)
     lon_halo = unfolded(east[...].astype(F32))
     lat_halo = unfolded(south[...].astype(F32))[:QUAD]
-    upper = dy[:, :SA].astype(F32) + low(lon_halo[QUAD:]) + high(lat_halo)
-    lower = dy[:, SA:].astype(F32) + low(lon_halo[:QUAD]) + high(quads[:QUAD].astype(F32))
-    out[:, :SA] = upper.astype(BF)
-    out[:, SA:] = lower.astype(BF)
+    mine = quads[:QUAD].astype(F32)
+    levels = []
+    for z in range(WZ):
+        rows = []
+        for a in range(WA):
+            at = (z * SA + a % SA) * 8
+            low = lon_halo[at : at + 8] if a >= SA else lon_halo[QUAD + at : QUAD + at + 8]
+            high = mine[at : at + 8] if a >= SA else lat_halo[at : at + 8]
+            low, high = jnp.concatenate([low, gap]), jnp.concatenate([gap, high])
+            rows.append(dy[z, a].astype(F32) + low + high)
+        levels.append(jnp.concatenate(rows, axis=0))
+    out_s[...] = jnp.stack(levels, axis=1).astype(BF)
+    copy = pltpu.make_async_copy(out_s, out, sem)
+    copy.start()
+    copy.wait()
 
 
 def widened(rows):
@@ -376,21 +376,10 @@
     out[...] = jnp.where(odd, got[...].astype(F32), earlier).astype(BF)
 
 
-def last_table_kernel(sent, got, table_out, table_s, sem):
-    table = sent[...].astype(F32) + got[...].astype(F32)
-    count = H * ROWS
-    tail = table[count : count + ROWS]
-    tail = jnp.concatenate([tail[:, h * SPAN : (h + 1) * SPAN] for h in range(H)], axis=0)
-    table = jnp.concatenate([table[:count, :LEAD], tail], axis=1)
-    for h in range(H):
-        rows = [table[h * ROWS + a : h * ROWS + a + 1] for a in range(ROWS)]
-        table_s[h] = jnp.concatenate(rows, axis=1)
-    copy = pltpu.make_async_copy(table_s, table_out, sem)
-    copy.start()
-    copy.wait()
-
-
-def last_kernel(sent, got, qkv_out, proj_out, gain_out, dense_s, gain_s, sems):
+def last_kernel(
+    sent, got, table_sent, table_got, qkv_out, proj_out, gain_out, table_out,
+    dense_s, gain_s, table_s, sems,
+):
     sent, got = sent[...].astype(F32), got[...].astype(F32)
     rows = (sent.shape[0] - 8) // 2
     size = 4 * rows // 3
@@ -404,9 +393,19 @@
         pltpu.make_async_copy(dense_s.at[: 3 * size], qkv_out, sems.at[0]),
         pltpu.make_async_copy(dense_s.at[3 * size :], proj_out, sems.at[1]),
         pltpu.make_async_copy(gain_s, gain_out, sems.at[2]),
+        pltpu.make_async_copy(table_s, table_out, sems.at[3]),
     ]
-    for copy in copies:
+    for copy in copies[:3]:
         copy.start()
+    table = table_sent[...].astype(F32) + table_got[...].astype(F32)
+    count = H * ROWS
+    tail = table[count : count + ROWS]
+    tail = jnp.concatenate([tail[:, h * SPAN : (h + 1) * SPAN] for h in range(H)], axis=0)
+    table = jnp.concatenate([table[:count, :LEAD], tail], axis=1)
+    for h in range(H):
+        rows = [table[h * ROWS + a : h * ROWS + a + 1] for a in range(ROWS)]
+        table_s[h] = jnp.concatenate(rows, axis=1)
+    copies[3].start()
     for copy in copies:
         copy.wait()
 
@@ -548,35 +547,46 @@
         south = passed_along(south, "lat", 1)
         east = call(east_kernel, shaped(HALO, WIDE, BF), specs=[VMEM] * 2)(quads, south)
         east = passed_along(east, "lon", 1)
-    tile = (WZ, WA, WL, C)
-    finish = call(finish_kernel, jax.ShapeDtypeStruct(tile, BF), specs=[VMEM] * 4)
     hbm = pl.BlockSpec(memory_space=pltpu.HBM)
+    tile = (WA * WL, WZ, C)
+    finish = call(
+        finish_kernel,
+        jax.ShapeDtypeStruct(tile, BF),
+        [pltpu.VMEM(tile, BF), pltpu.SemaphoreType.DMA],
+        specs=[VMEM] * 4,
+        out_specs=hbm,
+    )
+
+    def tokens_of(columns):
+        return columns.reshape(WA, WL, WZ, C).transpose(2, 0, 1, 3)[None]
+
     if fast:
         sent = call(join_kernel, shaped(2 * piece + 8, WIDE, BF), specs=[VMEM] * 2)(sent, got)
         sent, table_got, east = tied(sent, table_got, east)
         got = exchanged(sent, "lon", 1)
-        grad_table = call(
-            last_table_kernel,
-            jax.ShapeDtypeStruct((H, 1, POS), F32),
-            [pltpu.VMEM((H, 1, POS), F32), pltpu.SemaphoreType.DMA],
-            specs=[VMEM] * 2,
-            out_specs=hbm,
-        )(table, table_got).reshape(1, H, POS)
-        grad_tokens = finish(dy, quads, south, east).reshape(tokens.shape)
-        got, grad_tokens, grad_table = tied(got, grad_tokens, grad_table)
-        grad_qkv_w, grad_proj, grad_gain = call(
+        grad_tokens = finish(dy, quads, south, east)
+        got, grad_tokens = tied(got, grad_tokens)
+        grad_tokens = tokens_of(grad_tokens)
+        grad_qkv_w, grad_proj, grad_gain, grad_table = call(
             last_kernel,
-            [shaped(n_qkv, C, F32), shaped(n_proj, C, F32), shaped(1, n_proj, F32)],
+            [
+                shaped(n_qkv, C, F32),
+                shaped(n_proj, C, F32),
+                shaped(1, n_proj, F32),
+                jax.ShapeDtypeStruct((H, 1, POS), F32),
+            ],
             [
                 pltpu.VMEM((each, C), F32),
                 pltpu.VMEM((1, n_proj), F32),
-                pltpu.SemaphoreType.DMA((3,)),
+                pltpu.VMEM((H, 1, POS), F32),
+                pltpu.SemaphoreType.DMA((4,)),
             ],
-            specs=[VMEM] * 2,
-            out_specs=[hbm] * 3,
-        )(sent, got)
-        return grad_tokens, grad_qkv_w, grad_proj, grad_gain.reshape(n_proj), grad_table
-    grad_tokens = finish(dy, quads, south, east).reshape(tokens.shape)
+            specs=[VMEM] * 4,
+            out_specs=[hbm] * 4,
+        )(sent, got, table, table_got)
+        grad_gain, grad_table = grad_gain.reshape(n_proj), grad_table.reshape(1, H, POS)
+        return grad_tokens, grad_qkv_w, grad_proj, grad_gain, grad_table
+    grad_tokens = tokens_of(finish(dy, quads, south, east))
     pair = jnp.stack([keep, send.astype(F32)]).reshape(2, parts, packed // parts, WIDE)
     pair = jnp.where(side_index() == 0, pair, pair[::-1])
     pair = jax.vmap(jax.vmap(unfolded))(pair)

time: 43.9 us -> 41.4 us (0.943)
  Pallas kernels: 9.1 us -> 6.98 us
  local copies, waits for them, and re-layouts: 2.46 us -> 1.75 us
    pallas_call x1, Pallas kernels: 4.13 us -> 2.02 us  [body(): call(functools.partial(main_kernel, parts, 2 if fast else 1), outs, scrat...]
    unnamed x13 -> x12, local copies, waits for them, and re-layouts: 1.36 us -> 0.65 us
    pallas_call x2 -> x1, Pallas kernels: 1.11 us -> 0.84 us  [body(): grad_tokens = finish(dy, quads, south, east)]
where the time goes in v4:
time: 41.4 us; the launch traced here: 41.2 us
  starting transfers between devices  18.2 us (44%)
  waiting for transfers between devices  13.3 us (32%)
  Pallas kernels  6.98 us (17%)
  local copies, waits for them, and re-layouts  1.75 us (4%)
  between operations  0.79 us (2%)
    ppermute x10, waiting for transfers between devices, exchanged(): return lax.ppermute(value, axis, [(i, i ^ flip) for i in range(count)])  10.9 us
    ppermute x3, starting transfers between devices, passed_along(): lax.ppermute(value, axis, [(i, (i + steps) % count) for i in range(count)])  8.01 us
    ppermute x10, starting transfers between devices, exchanged(): return lax.ppermute(value, axis, [(i, i ^ flip) for i in range(count)])  7.8 us
    ppermute x1, starting transfers between devices, exchanged_both(): return lax.ppermute(value, ('lon', 'dp'), pairs)  2.12 us
    ppermute x1, waiting for transfers between devices, exchanged_both(): return lax.ppermute(value, ('lon', 'dp'), pairs)  2.09 us
    pallas_call x1, Pallas kernels, body(): call(functools.partial(main_kernel, parts, 2 if fast else 1), outs, scrat...  2.02 us
    pallas_call x1, Pallas kernels, body(): call(last_kernel, [shaped(n_qkv, C, F32), shaped(n_proj, C, F32), shaped(...  1.12 us
    pallas_call x1, Pallas kernels, body(): call(bias_kernel, jax.ShapeDtypeStruct((2, H * WT, 128), F32), specs=[VME...  1.03 us
  transfers between devices with their start and end apart: 15, of which 8 were waited for; matrix products, arithmetic and copies ran while one was open for 1% of the time, Pallas kernels for 9%

profile of v4, /device:TPU:0, one launch (start us, length us, event | category | flops | bytes accessed | tf_op | source)
XLA Modules:
  0.0 41.2 jit_solution(18322165607803984255)
XLA Ops:
  0.7 1.0 %copy_bitcast_fusion = (bf16[2,6,12,192]{3,2,1,0:T(8,128)(2,1)S(1)}, bf16[2,6,12,192]{3,2,1,0:T(8,128)(2,1)S(1)}) fusion(bf16[1,2,6,12,192]{4,1,3,2,0:T(2,128)(2,1)} %param.9, bf16[1,2,6,12,192]{4,1,3,2,0:T(2,128)(2,1)} %param.8), kind=kLoop, calls=%fused_computation | loop fusion | bytes 221184 | tf_op jit(solution)/shard_map/reshape | solution.py:466
  1.7 0.6 %copy-done.4 = bf16[96]{0:T(256)(128)(2,1)S(1)} copy-done((bf16[96]{0:T(256)(128)(2,1)S(1)}, bf16[96]{0:T(256)(128)(2,1)}, u32[]{:S(2)}) %copy-start.4) | copy-done | bytes 216
  2.5 3.0 %collective-permute-start.3 = (bf16[400,192]{1,0:T(8,128)(2,1)S(1)}, bf16[400,192]{1,0:T(8,128)(2,1)S(1)}, u32[]{:S(2)}, u32[]{:S(2)}) collective-permute-start(bf16[400,192]{1,0:T(8,128)(2,1)S(1)} %get-tuple-element.44.refs_0_), channel_id=1, source_target_pairs={{0,1},{1,0},{2,3},{3,2},{4,5},{5,4},{6,7},{7,6},{8,9},{9,8},{10,11... | collective-permute-start | bytes 460808 | tf_op jit(solution)/shard_map/ppermute | solution.py:445
  5.5 3.6 %collective-permute-start = (bf16[72,256]{1,0:T(8,128)(2,1)S(1)}, bf16[72,256]{1,0:T(8,128)(2,1)S(1)}, u32[]{:S(2)}, u32[]{:S(2)}) collective-permute-start(bf16[72,256]{1,0:T(8,128)(2,1)S(1)} %get-tuple-element.41), channel_id=1, source_target_pairs={{0,6},{2,0},{4,2},{6,4},{1,7},{3,1},{5,3},{7,5},{8,14},{10,8},{12,... | collective-permute-start | bytes 110600 | tf_op jit(solution)/shard_map/ppermute | solution.py:445
  9.3 1.4 %collective-permute-start.2 = (bf16[72,256]{1,0:T(8,128)(2,1)S(1)}, bf16[72,256]{1,0:T(8,128)(2,1)S(1)}, u32[]{:S(2)}, u32[]{:S(2)}) collective-permute-start(bf16[72,256]{1,0:T(8,128)(2,1)S(1)} %get-tuple-element.43), channel_id=1, source_target_pairs={{0,24},{8,0},{16,8},{24,16},{1,25},{9,1},{17,9},{25,17},{2,26},{10... | collective-permute-start | bytes 110600 | tf_op jit(solution)/shard_map/ppermute | solution.py:445
  11.1 1.0 %shard_map.120.bias = f32[2,864,128]{2,1,0:T(8,128)S(1)} custom-call(f32[72,276]{1,0:T(8,128)S(1)} %reshape.34.table), custom_call_target="tpu_custom_call" | custom-call | flops 200000000 | bytes 1000000 | tf_op jit(solution)/shard_map/pallas_call | solution.py:476
  12.5 2.0 %shard_map.121 = (bf16[288,256]{1,0:T(8,128)(2,1)S(1)}, f32[288,256]{1,0:T(8,128)S(1)}, f32[8,192]{1,0:T(8,128)S(1)}, f32[2,864,128]{2,1,0:T(8,128)S(1)}, f32[57...) custom-call(bf16[72,256]{1,0:T(8,128)(2,1)S(1)} %collective-permute-done.south, ...), custom_call_target="tpu_custom_call" | custom-call | flops 1000000 | bytes 1000000 | tf_op jit(solution)/shard_map/pallas_call | solution.py:495
  14.5 0.6 %collective-permute-start.4 = (bf16[288,256]{1,0:T(8,128)(2,1)S(1)}, bf16[288,256]{1,0:T(8,128)(2,1)S(1)}, u32[]{:S(2)}, u32[]{:S(2)}) collective-permute-start(bf16[288,256]{1,0:T(8,128)(2,1)S(1)} %get-tuple-element.46), channel_id=1, source_target_pairs={{0,8},{8,0},{16,24},{24,16},{1,9},{9,1},{17,25},{25,17},{2,10},{10... | collective-permute-start | bytes 442376 | tf_op jit(solution)/shard_map/ppermute | solution.py:431
  15.1 0.8 %shard_map.122.table = bf16[88,256]{1,0:T(8,128)(2,1)S(1)} custom-call(f32[2,864,128]{2,1,0:T(8,128)S(1)} %get-tuple-element.48.scores_grad), custom_call_target="tpu_custom_call" | custom-call | flops 200000000 | bytes 1000000 | tf_op jit(solution)/shard_map/pallas_call | solution.py:503
  16.1 0.6 %collective-permute-start.6 = (bf16[168,256]{1,0:T(8,128)(2,1)S(1)}, bf16[168,256]{1,0:T(8,128)(2,1)S(1)}, u32[]{:S(2)}, u32[]{:S(2)}) collective-permute-start(bf16[168,256]{1,0:T(8,128)(2,1)S(1)} %get-tuple-element.50.sent), channel_id=1, source_target_pairs={{0,1},{1,0},{2,3},{3,2},{4,5},{5,4},{6,7},{7,6},{8,9},{9,8},{10,11... | collective-permute-start | bytes 258056 | tf_op jit(solution)/shard_map/ppermute | solution.py:431
  16.8 2.1 %collective-permute-start.5 = (bf16[72,256]{1,0:T(8,128)(2,1)S(1)}, bf16[72,256]{1,0:T(8,128)(2,1)S(1)}, u32[]{:S(2)}, u32[]{:S(2)}) collective-permute-start(bf16[72,256]{1,0:T(8,128)(2,1)S(1)} %get-tuple-element.51), channel_id=1, source_target_pairs={{0,25},{1,24},{8,17},{9,16},{16,9},{17,8},{24,1},{25,0},{2,27},{3,... | collective-permute-start | bytes 110600 | tf_op jit(solution)/shard_map/ppermute | solution.py:436
  18.9 0.6 %collective-permute-start.7 = (bf16[72,256]{1,0:T(8,128)(2,1)S(1)}, bf16[72,256]{1,0:T(8,128)(2,1)S(1)}, u32[]{:S(2)}, u32[]{:S(2)}) collective-permute-start(bf16[72,256]{1,0:T(8,128)(2,1)S(1)} %get-tuple-element.52), channel_id=1, source_target_pairs={{0,24},{8,16},{16,8},{24,0},{1,25},{9,17},{17,9},{25,1},{2,26},{10... | collective-permute-start | bytes 110600 | tf_op jit(solution)/shard_map/ppermute | solution.py:431
  19.4 0.7 %shard_map.124 = (bf16[96,192]{1,0:T(8,128)(2,1)S(1)}, bf16[72,256]{1,0:T(8,128)(2,1)S(1)}) custom-call(f32[576,144]{1,0:T(8,128)S(1)} %get-tuple-element.53.grad_qkv_t, f32[144,192]{1,0:T(8,128)S(1)} %get-tuple-element.54.unit, f32[160,192]{1,0:T(8,128)S(1)} %get-tuple-element.55.scales, bf16[576,192]{1,0:T(8,128)(2,1)S(1)} %get-tuple-element.56.qkv_w, ...), custom_call_target="tpu_custom_call" | custom-call | flops 100000000 | bytes 1000000 | tf_op jit(solution)/shard_map/pallas_call | solution.py:519
  20.1 2.1 %collective-permute-done.5.from_both = bf16[72,256]{1,0:T(8,128)(2,1)S(1)} collective-permute-done((bf16[72,256]{1,0:T(8,128)(2,1)S(1)}, bf16[72,256]{1,0:T(8,128)(2,1)S(1)}, u32[]{:S(2)}, u32[]{:S(2)}) %collective-permute-start.5) | collective-permute-done | bytes 36896 | tf_op jit(solution)/shard_map/ppermute | solution.py:436
  22.5 1.6 %collective-permute-start.8 = (bf16[152,256]{1,0:T(8,128)(2,1)S(1)}, bf16[152,256]{1,0:T(8,128)(2,1)S(1)}, u32[]{:S(2)}, u32[]{:S(2)}) collective-permute-start(bf16[152,256]{1,0:T(8,128)(2,1)S(1)} %get-tuple-element.58.sent), channel_id=1, source_target_pairs={{0,2},{2,0},{4,6},{6,4},{1,3},{3,1},{5,7},{7,5},{8,10},{10,8},{12,... | collective-permute-start | bytes 233480 | tf_op jit(solution)/shard_map/ppermute | solution.py:431
  24.1 3.3 %collective-permute-done.8.got.before = bf16[152,256]{1,0:T(8,128)(2,1)S(1)} collective-permute-done((bf16[152,256]{1,0:T(8,128)(2,1)S(1)}, bf16[152,256]{1,0:T(8,128)(2,1)S(1)}, u32[]{:S(2)}, u32[]{:S(2)}) %collective-permute-start.8) | collective-permute-done | bytes 77856 | tf_op jit(solution)/shard_map/ppermute | solution.py:431
  27.4 2.4 %collective-permute-start.9 = (bf16[152,256]{1,0:T(8,128)(2,1)S(1)}, bf16[152,256]{1,0:T(8,128)(2,1)S(1)}, u32[]{:S(2)}, u32[]{:S(2)}) collective-permute-start(bf16[152,256]{1,0:T(8,128)(2,1)S(1)} %shard_map.126.sent), channel_id=1, source_target_pairs={{0,6},{2,4},{4,2},{6,0},{1,7},{3,5},{5,3},{7,1},{8,14},{10,12},{12... | collective-permute-start | bytes 233480 | tf_op jit(solution)/shard_map/ppermute | solution.py:431
  29.8 0.6 %collective-permute-start.10 = (bf16[88,256]{1,0:T(8,128)(2,1)S(1)}, bf16[88,256]{1,0:T(8,128)(2,1)S(1)}, u32[]{:S(2)}, u32[]{:S(2)}) collective-permute-start(bf16[88,256]{1,0:T(8,128)(2,1)S(1)} %get-tuple-element.63.sent), channel_id=1, source_target_pairs={{0,24},{8,16},{16,8},{24,0},{1,25},{9,17},{17,9},{25,1},{2,26},{10... | collective-permute-start | bytes 135176 | tf_op jit(solution)/shard_map/ppermute | solution.py:431
  30.4 3.3 %collective-permute-done.9.got = bf16[152,256]{1,0:T(8,128)(2,1)S(1)} collective-permute-done((bf16[152,256]{1,0:T(8,128)(2,1)S(1)}, bf16[152,256]{1,0:T(8,128)(2,1)S(1)}, u32[]{:S(2)}, u32[]{:S(2)}) %collective-permute-start.9) | collective-permute-done | bytes 77856 | tf_op jit(solution)/shard_map/ppermute | solution.py:431
  34.0 0.4 %collective-permute-start.11 = (bf16[152,256]{1,0:T(8,128)(2,1)S(1)}, bf16[152,256]{1,0:T(8,128)(2,1)S(1)}, u32[]{:S(2)}, u32[]{:S(2)}) collective-permute-start(bf16[152,256]{1,0:T(8,128)(2,1)S(1)} %get-tuple-element.64.sent), channel_id=1, source_target_pairs={{0,24},{8,16},{16,8},{24,0},{1,25},{9,17},{17,9},{25,1},{2,26},{10... | collective-permute-start | bytes 233480 | tf_op jit(solution)/shard_map/ppermute | solution.py:431
  34.4 0.7 %collective-permute-start.12 = (bf16[88,256]{1,0:T(8,128)(2,1)S(1)}, bf16[88,256]{1,0:T(8,128)(2,1)S(1)}, u32[]{:S(2)}, u32[]{:S(2)}) collective-permute-start(bf16[88,256]{1,0:T(8,128)(2,1)S(1)} %shard_map.129.table_sent), channel_id=1, source_target_pairs={{0,8},{8,0},{16,24},{24,16},{1,9},{9,1},{17,25},{25,17},{2,10},{10... | collective-permute-start | bytes 135176 | tf_op jit(solution)/shard_map/ppermute | solution.py:431
  35.2 3.5 %collective-permute-done.11.got.earlier = bf16[152,256]{1,0:T(8,128)(2,1)S(1)} collective-permute-done((bf16[152,256]{1,0:T(8,128)(2,1)S(1)}, bf16[152,256]{1,0:T(8,128)(2,1)S(1)}, u32[]{:S(2)}, u32[]{:S(2)}) %collective-permute-start.11) | collective-permute-done | bytes 77856 | tf_op jit(solution)/shard_map/ppermute | solution.py:431
  38.9 0.8 %shard_map.131 = bf16[72,2,192]{2,1,0:T(2,128)(2,1)} custom-call(bf16[2,6,12,192]{3,2,1,0:T(8,128)(2,1)S(1)} %get-tuple-element.77.dy, bf16[96,192]{1,0:T(8,128)(2,1)S(1)} %get-tuple-element.61.quads, bf16[72,256]{1,0:T(8,128)(2,1)S(1)} %get-tuple-element.68.south, bf16[72,256]{1,0:T(8,128)(2,1)S(1)} %shard_map.130.east), custom_call_target="tpu_custom_call" | custom-call | flops 1000000 | bytes 1000000 | tf_op jit(solution)/shard_map/pallas_call | solution.py:567
  40.1 1.1 %shard_map.132 = (f32[288,192]{1,0:T(8,128)}, f32[96,192]{1,0:T(8,128)}, f32[1,96]{1,0:T(1,128)}, f32[6,1,3312]{2,1,0:T(1,128)}) custom-call(bf16[152,256]{1,0:T(8,128)(2,1)S(1)} %shard_map.128.sent, bf16[152,256]{1,0:T(8,128)(2,1)S(1)} %collective-permute-done.14.got, bf16[88,256]{1,0:T(8,128)(2,1)S(1)} %shard_map.129.table_sent, ...), custom_call_target="tpu_custom_call" | custom-call | flops 1000000 | bytes 1000000 | tf_op jit(solution)/shard_map/pallas_call | solution.py:570
  (35 shorter events, 2.5 us)
Async XLA Ops:
  0.6 1.0 %copy-start.3 = (bf16[96,192]{1,0:T(8,128)(2,1)S(1)}, bf16[96,192]{1,0:T(8,128)(2,1)}, u32[]{:S(2)}) copy-start(bf16[96,192]{1,0:T(8,128)(2,1)} %proj.1) | copy-start | bytes 110596
  0.6 1.0 %copy-start = (bf16[288,192]{1,0:T(8,128)(2,1)S(1)}, bf16[288,192]{1,0:T(8,128)(2,1)}, u32[]{:S(2)}) copy-start(bf16[288,192]{1,0:T(8,128)(2,1)} %qkv.1) | copy-start | bytes 331780
  1.6 0.7 %copy-start.4 = (bf16[96]{0:T(256)(128)(2,1)S(1)}, bf16[96]{0:T(256)(128)(2,1)}, u32[]{:S(2)}) copy-start(bf16[96]{0:T(256)(128)(2,1)} %param.12) | copy-start | bytes 580
  2.3 8.5 %copy-start.5 = (f32[1,6,3312]{2,0,1:T(1,128)S(1)}, f32[1,6,3312]{2,0,1:T(1,128)}, u32[]{:S(2)}) copy-start(f32[1,6,3312]{2,0,1:T(1,128)} %param.13) | copy-start | bytes 238468
  2.5 10.0 %collective-permute-start.3 = (bf16[400,192]{1,0:T(8,128)(2,1)S(1)}, bf16[400,192]{1,0:T(8,128)(2,1)S(1)}, u32[]{:S(2)}, u32[]{:S(2)}) collective-permute-start(bf16[400,192]{1,0:T(8,128)(2,1)S(1)} %get-tuple-element.44.refs_0_), channel_id=1, source_target_pairs={{0,1},{1,0},{2,3},{3,2},{4,5},{5,4},{6,7},{7,6},{8,9},{9,8},{10,11... | collective-permute-start | bytes 460808 | tf_op jit(solution)/shard_map/ppermute | solution.py:445
  5.5 6.7 %collective-permute-start = (bf16[72,256]{1,0:T(8,128)(2,1)S(1)}, bf16[72,256]{1,0:T(8,128)(2,1)S(1)}, u32[]{:S(2)}, u32[]{:S(2)}) collective-permute-start(bf16[72,256]{1,0:T(8,128)(2,1)S(1)} %get-tuple-element.41), channel_id=1, source_target_pairs={{0,6},{2,0},{4,2},{6,4},{1,7},{3,1},{5,3},{7,5},{8,14},{10,8},{12,... | collective-permute-start | bytes 110600 | tf_op jit(solution)/shard_map/ppermute | solution.py:445
  9.1 3.4 %collective-permute-start.1 = (bf16[72,256]{1,0:T(8,128)(2,1)S(1)}, bf16[72,256]{1,0:T(8,128)(2,1)S(1)}, u32[]{:S(2)}, u32[]{:S(2)}) collective-permute-start(bf16[72,256]{1,0:T(8,128)(2,1)S(1)} %get-tuple-element.42), channel_id=1, source_target_pairs={{0,30},{2,24},{4,26},{6,28},{8,6},{10,0},{12,2},{14,4},{16,14},{18... | collective-permute-start | bytes 110600 | tf_op jit(solution)/shard_map/ppermute | solution.py:455
  9.3 3.1 %collective-permute-start.2 = (bf16[72,256]{1,0:T(8,128)(2,1)S(1)}, bf16[72,256]{1,0:T(8,128)(2,1)S(1)}, u32[]{:S(2)}, u32[]{:S(2)}) collective-permute-start(bf16[72,256]{1,0:T(8,128)(2,1)S(1)} %get-tuple-element.43), channel_id=1, source_target_pairs={{0,24},{8,0},{16,8},{24,16},{1,25},{9,1},{17,9},{25,17},{2,26},{10... | collective-permute-start | bytes 110600 | tf_op jit(solution)/shard_map/ppermute | solution.py:445
  11.1 1.4 %copy-start.2 = (bf16[144,192]{1,0:T(8,128)(2,1)S(1)}, bf16[144,192]{1,0:T(8,128)(2,1)}, u32[]{:S(2)}) copy-start(bf16[144,192]{1,0:T(8,128)(2,1)} %constant.4.clone.order) | copy-start | bytes 165892
  14.5 1.6 %collective-permute-start.4 = (bf16[288,256]{1,0:T(8,128)(2,1)S(1)}, bf16[288,256]{1,0:T(8,128)(2,1)S(1)}, u32[]{:S(2)}, u32[]{:S(2)}) collective-permute-start(bf16[288,256]{1,0:T(8,128)(2,1)S(1)} %get-tuple-element.46), channel_id=1, source_target_pairs={{0,8},{8,0},{16,24},{24,16},{1,9},{9,1},{17,25},{25,17},{2,10},{10... | collective-permute-start | bytes 442376 | tf_op jit(solution)/shard_map/ppermute | solution.py:431
  16.1 3.3 %copy-start.1 = (bf16[192,144]{1,0:T(8,128)(2,1)S(1)}, bf16[192,144]{1,0:T(8,128)(2,1)}, u32[]{:S(2)}) copy-start(bf16[192,144]{1,0:T(8,128)(2,1)} %constant.5.clone.order_t) | copy-start | bytes 165892
  16.1 6.3 %collective-permute-start.6 = (bf16[168,256]{1,0:T(8,128)(2,1)S(1)}, bf16[168,256]{1,0:T(8,128)(2,1)S(1)}, u32[]{:S(2)}, u32[]{:S(2)}) collective-permute-start(bf16[168,256]{1,0:T(8,128)(2,1)S(1)} %get-tuple-element.50.sent), channel_id=1, source_target_pairs={{0,1},{1,0},{2,3},{3,2},{4,5},{5,4},{6,7},{7,6},{8,9},{9,8},{10,11... | collective-permute-start | bytes 258056 | tf_op jit(solution)/shard_map/ppermute | solution.py:431
  16.8 5.4 %collective-permute-start.5 = (bf16[72,256]{1,0:T(8,128)(2,1)S(1)}, bf16[72,256]{1,0:T(8,128)(2,1)S(1)}, u32[]{:S(2)}, u32[]{:S(2)}) collective-permute-start(bf16[72,256]{1,0:T(8,128)(2,1)S(1)} %get-tuple-element.51), channel_id=1, source_target_pairs={{0,25},{1,24},{8,17},{9,16},{16,9},{17,8},{24,1},{25,0},{2,27},{3,... | collective-permute-start | bytes 110600 | tf_op jit(solution)/shard_map/ppermute | solution.py:436
  18.9 3.6 %collective-permute-start.7 = (bf16[72,256]{1,0:T(8,128)(2,1)S(1)}, bf16[72,256]{1,0:T(8,128)(2,1)S(1)}, u32[]{:S(2)}, u32[]{:S(2)}) collective-permute-start(bf16[72,256]{1,0:T(8,128)(2,1)S(1)} %get-tuple-element.52), channel_id=1, source_target_pairs={{0,24},{8,16},{16,8},{24,0},{1,25},{9,17},{17,9},{25,1},{2,26},{10... | collective-permute-start | bytes 110600 | tf_op jit(solution)/shard_map/ppermute | solution.py:431
  22.5 4.9 %collective-permute-start.8 = (bf16[152,256]{1,0:T(8,128)(2,1)S(1)}, bf16[152,256]{1,0:T(8,128)(2,1)S(1)}, u32[]{:S(2)}, u32[]{:S(2)}) collective-permute-start(bf16[152,256]{1,0:T(8,128)(2,1)S(1)} %get-tuple-element.58.sent), channel_id=1, source_target_pairs={{0,2},{2,0},{4,6},{6,4},{1,3},{3,1},{5,7},{7,5},{8,10},{10,8},{12,... | collective-permute-start | bytes 233480 | tf_op jit(solution)/shard_map/ppermute | solution.py:431
  27.4 6.3 %collective-permute-start.9 = (bf16[152,256]{1,0:T(8,128)(2,1)S(1)}, bf16[152,256]{1,0:T(8,128)(2,1)S(1)}, u32[]{:S(2)}, u32[]{:S(2)}) collective-permute-start(bf16[152,256]{1,0:T(8,128)(2,1)S(1)} %shard_map.126.sent), channel_id=1, source_target_pairs={{0,6},{2,4},{4,2},{6,0},{1,7},{3,5},{5,3},{7,1},{8,14},{10,12},{12... | collective-permute-start | bytes 233480 | tf_op jit(solution)/shard_map/ppermute | solution.py:431
  29.8 4.1 %collective-permute-start.10 = (bf16[88,256]{1,0:T(8,128)(2,1)S(1)}, bf16[88,256]{1,0:T(8,128)(2,1)S(1)}, u32[]{:S(2)}, u32[]{:S(2)}) collective-permute-start(bf16[88,256]{1,0:T(8,128)(2,1)S(1)} %get-tuple-element.63.sent), channel_id=1, source_target_pairs={{0,24},{8,16},{16,8},{24,0},{1,25},{9,17},{17,9},{25,1},{2,26},{10... | collective-permute-start | bytes 135176 | tf_op jit(solution)/shard_map/ppermute | solution.py:431
  34.0 4.7 %collective-permute-start.11 = (bf16[152,256]{1,0:T(8,128)(2,1)S(1)}, bf16[152,256]{1,0:T(8,128)(2,1)S(1)}, u32[]{:S(2)}, u32[]{:S(2)}) collective-permute-start(bf16[152,256]{1,0:T(8,128)(2,1)S(1)} %get-tuple-element.64.sent), channel_id=1, source_target_pairs={{0,24},{8,16},{16,8},{24,0},{1,25},{9,17},{17,9},{25,1},{2,26},{10... | collective-permute-start | bytes 233480 | tf_op jit(solution)/shard_map/ppermute | solution.py:431
  34.4 4.3 %collective-permute-start.12 = (bf16[88,256]{1,0:T(8,128)(2,1)S(1)}, bf16[88,256]{1,0:T(8,128)(2,1)S(1)}, u32[]{:S(2)}, u32[]{:S(2)}) collective-permute-start(bf16[88,256]{1,0:T(8,128)(2,1)S(1)} %shard_map.129.table_sent), channel_id=1, source_target_pairs={{0,8},{8,0},{16,24},{24,16},{1,9},{9,1},{17,25},{25,17},{2,10},{10... | collective-permute-start | bytes 135176 | tf_op jit(solution)/shard_map/ppermute | solution.py:431
  35.1 3.6 %collective-permute-start.13 = (bf16[72,256]{1,0:T(8,128)(2,1)S(1)}, bf16[72,256]{1,0:T(8,128)(2,1)S(1)}, u32[]{:S(2)}, u32[]{:S(2)}) collective-permute-start(bf16[72,256]{1,0:T(8,128)(2,1)S(1)} %get-tuple-element.66), channel_id=1, source_target_pairs={{0,8},{8,0},{16,24},{24,16},{1,9},{9,1},{17,25},{25,17},{2,10},{10... | collective-permute-start | bytes 110600 | tf_op jit(solution)/shard_map/ppermute | solution.py:431
  38.7 1.3 %collective-permute-start.14 = (bf16[152,256]{1,0:T(8,128)(2,1)S(1)}, bf16[152,256]{1,0:T(8,128)(2,1)S(1)}, u32[]{:S(2)}, u32[]{:S(2)}) collective-permute-start(bf16[152,256]{1,0:T(8,128)(2,1)S(1)} %shard_map.128.sent), channel_id=1, source_target_pairs={{0,8},{8,0},{16,24},{24,16},{1,9},{9,1},{17,25},{25,17},{2,10},{10... | collective-permute-start | bytes 233480 | tf_op jit(solution)/shard_map/ppermute | solution.py:431

commit v5 on v4

--- a/solution.py
+++ b/solution.py
@@ -249,14 +249,17 @@
 def table_kernel(scores_grad, table):
     count = H * ROWS
     row, target = offsets(288, WT, 0)
-    total = jnp.zeros((count, 288), F32)
-    for u in range(WL):
-        onehot = jnp.where(row == target + u, 1.0, 0.0).astype(BF)
-        rows = pl.ds(u, count, stride=WL)
-        wide = jnp.concatenate(
-            [scores_grad[0, rows, :], scores_grad[1, rows, :][:, : WT - 128]], axis=1
-        )
-        total += matmul_t(wide.astype(BF), onehot)
+    onehots = [jnp.where(row == target + u, 1.0, 0.0).astype(BF) for u in range(WL)]
+    strides = [pl.ds(u, count, stride=WL) for u in range(WL)]
+    wide = [
+        jnp.concatenate([scores_grad[0, rows, :], scores_grad[1, rows, :][:, : WT - 128]], axis=1)
+        for rows in strides
+    ]
+    terms = [matmul_t(value.astype(BF), onehot) for value, onehot in zip(wide, onehots)]
+    while len(terms) > 1:
+        pairs = [sum(terms[k : k + 2]) for k in range(0, len(terms), 2)]
+        terms = pairs
+    total = terms[0]
     tail = total[:, LEAD : LEAD + SPAN]
     tail = jnp.concatenate([tail[h * ROWS : (h + 1) * ROWS] for h in range(H)], axis=1)
     tail = jnp.concatenate([tail, jnp.zeros((ROWS, WIDE - H * SPAN), F32)], axis=1)
@@ -376,10 +379,22 @@
     out[...] = jnp.where(odd, got[...].astype(F32), earlier).astype(BF)
 
 
+def table_rows_kernel(table_sent, table_got, out):
+    table = table_sent[...].astype(F32) + table_got[...].astype(F32)
+    count = H * ROWS
+    tail = table[count : count + ROWS]
+    tail = jnp.concatenate([tail[:, h * SPAN : (h + 1) * SPAN] for h in range(H)], axis=0)
+    table = jnp.concatenate([table[:count, :LEAD], tail], axis=1)
+    for h in range(H):
+        rows = [table[h * ROWS + a : h * ROWS + a + 1] for a in range(ROWS)]
+        out[h] = jnp.concatenate(rows, axis=1)
+
+
 def last_kernel(
-    sent, got, table_sent, table_got, qkv_out, proj_out, gain_out, table_out,
-    dense_s, gain_s, table_s, sems,
+    sent, got, table, qkv_out, proj_out, gain_out, table_out, dense_s, gain_s, sems
 ):
+    first = pltpu.make_async_copy(table, table_out, sems.at[3])
+    first.start()
     sent, got = sent[...].astype(F32), got[...].astype(F32)
     rows = (sent.shape[0] - 8) // 2
     size = 4 * rows // 3
@@ -393,20 +408,10 @@
         pltpu.make_async_copy(dense_s.at[: 3 * size], qkv_out, sems.at[0]),
         pltpu.make_async_copy(dense_s.at[3 * size :], proj_out, sems.at[1]),
         pltpu.make_async_copy(gain_s, gain_out, sems.at[2]),
-        pltpu.make_async_copy(table_s, table_out, sems.at[3]),
     ]
-    for copy in copies[:3]:
+    for copy in copies:
         copy.start()
-    table = table_sent[...].astype(F32) + table_got[...].astype(F32)
-    count = H * ROWS
-    tail = table[count : count + ROWS]
-    tail = jnp.concatenate([tail[:, h * SPAN : (h + 1) * SPAN] for h in range(H)], axis=0)
-    table = jnp.concatenate([table[:count, :LEAD], tail], axis=1)
-    for h in range(H):
-        rows = [table[h * ROWS + a : h * ROWS + a + 1] for a in range(ROWS)]
-        table_s[h] = jnp.concatenate(rows, axis=1)
-    copies[3].start()
-    for copy in copies:
+    for copy in copies + [first]:
         copy.wait()
 
 
@@ -565,7 +570,10 @@
         sent, table_got, east = tied(sent, table_got, east)
         got = exchanged(sent, "lon", 1)
         grad_tokens = finish(dy, quads, south, east)
-        got, grad_tokens = tied(got, grad_tokens)
+        table = call(
+            table_rows_kernel, jax.ShapeDtypeStruct((H, 1, POS), F32), specs=[VMEM] * 2
+        )(table, table_got)
+        got, grad_tokens, table = tied(got, grad_tokens, table)
         grad_tokens = tokens_of(grad_tokens)
         grad_qkv_w, grad_proj, grad_gain, grad_table = call(
             last_kernel,
@@ -578,12 +586,11 @@
             [
                 pltpu.VMEM((each, C), F32),
                 pltpu.VMEM((1, n_proj), F32),
-                pltpu.VMEM((H, 1, POS), F32),
                 pltpu.SemaphoreType.DMA((4,)),
             ],
-            specs=[VMEM] * 4,
+            specs=[VMEM] * 3,
             out_specs=[hbm] * 4,
-        )(sent, got, table, table_got)
+        )(sent, got, table)
         grad_gain, grad_table = grad_gain.reshape(n_proj), grad_table.reshape(1, H, POS)
         return grad_tokens, grad_qkv_w, grad_proj, grad_gain, grad_table
     grad_tokens = tokens_of(finish(dy, quads, south, east))

time: 41.4 us -> 41.2 us (level)
  transfers between devices with their start and end apart: 15 -> 15, of which waited for: 8 -> 7; matrix products, arithmetic and copies ran while one was open for 1% -> 1% of each run, Pallas kernels for 9% -> 10%
where the time goes in v5:
time: 41.2 us; the launch traced here: 41 us
  starting transfers between devices  18.2 us (44%)
  waiting for transfers between devices  12.9 us (31%)
  Pallas kernels  7.1 us (17%)
  local copies, waits for them, and re-layouts  1.75 us (4%)
  between operations  0.8 us (2%)
    ppermute x10, waiting for transfers between devices, exchanged(): return lax.ppermute(value, axis, [(i, i ^ flip) for i in range(count)])  10.5 us
    ppermute x3, starting transfers between devices, passed_along(): lax.ppermute(value, axis, [(i, (i + steps) % count) for i in range(count)])  8.01 us
    ppermute x10, starting transfers between devices, exchanged(): return lax.ppermute(value, axis, [(i, i ^ flip) for i in range(count)])  7.8 us
    ppermute x1, starting transfers between devices, exchanged_both(): return lax.ppermute(value, ('lon', 'dp'), pairs)  2.12 us
    ppermute x1, waiting for transfers between devices, exchanged_both(): return lax.ppermute(value, ('lon', 'dp'), pairs)  2.09 us
    pallas_call x1, Pallas kernels, body(): call(functools.partial(main_kernel, parts, 2 if fast else 1), outs, scrat...  2.02 us
    pallas_call x1, Pallas kernels, body(): call(bias_kernel, jax.ShapeDtypeStruct((2, H * WT, 128), F32), specs=[VME...  1.03 us
    reshape x1, local copies, waits for them, and re-layouts, body(): dy = grad_out.reshape(WZ, WA, WL, C)  0.98 us
  transfers between devices with their start and end apart: 15, of which 7 were waited for; matrix products, arithmetic and copies ran while one was open for 1% of the time, Pallas kernels for 10%

profile of v5, /device:TPU:0, one launch (start us, length us, event | category | flops | bytes accessed | tf_op | source)
XLA Modules:
  0.0 41.0 jit_solution(16793160591642692516)
XLA Ops:
  0.7 1.0 %copy_bitcast_fusion = (bf16[2,6,12,192]{3,2,1,0:T(8,128)(2,1)S(1)}, bf16[2,6,12,192]{3,2,1,0:T(8,128)(2,1)S(1)}) fusion(bf16[1,2,6,12,192]{4,1,3,2,0:T(2,128)(2,1)} %param.9, bf16[1,2,6,12,192]{4,1,3,2,0:T(2,128)(2,1)} %param.8), kind=kLoop, calls=%fused_computation | loop fusion | bytes 221184 | tf_op jit(solution)/shard_map/reshape | solution.py:471
  1.7 0.6 %copy-done.4 = bf16[96]{0:T(256)(128)(2,1)S(1)} copy-done((bf16[96]{0:T(256)(128)(2,1)S(1)}, bf16[96]{0:T(256)(128)(2,1)}, u32[]{:S(2)}) %copy-start.4) | copy-done | bytes 216
  2.5 3.0 %collective-permute-start.3 = (bf16[400,192]{1,0:T(8,128)(2,1)S(1)}, bf16[400,192]{1,0:T(8,128)(2,1)S(1)}, u32[]{:S(2)}, u32[]{:S(2)}) collective-permute-start(bf16[400,192]{1,0:T(8,128)(2,1)S(1)} %get-tuple-element.45.refs_0_), channel_id=1, source_target_pairs={{0,1},{1,0},{2,3},{3,2},{4,5},{5,4},{6,7},{7,6},{8,9},{9,8},{10,11... | collective-permute-start | bytes 460808 | tf_op jit(solution)/shard_map/ppermute | solution.py:450
  5.5 3.6 %collective-permute-start = (bf16[72,256]{1,0:T(8,128)(2,1)S(1)}, bf16[72,256]{1,0:T(8,128)(2,1)S(1)}, u32[]{:S(2)}, u32[]{:S(2)}) collective-permute-start(bf16[72,256]{1,0:T(8,128)(2,1)S(1)} %get-tuple-element.42), channel_id=1, source_target_pairs={{0,6},{2,0},{4,2},{6,4},{1,7},{3,1},{5,3},{7,5},{8,14},{10,8},{12,... | collective-permute-start | bytes 110600 | tf_op jit(solution)/shard_map/ppermute | solution.py:450
  9.3 1.4 %collective-permute-start.2 = (bf16[72,256]{1,0:T(8,128)(2,1)S(1)}, bf16[72,256]{1,0:T(8,128)(2,1)S(1)}, u32[]{:S(2)}, u32[]{:S(2)}) collective-permute-start(bf16[72,256]{1,0:T(8,128)(2,1)S(1)} %get-tuple-element.44), channel_id=1, source_target_pairs={{0,24},{8,0},{16,8},{24,16},{1,25},{9,1},{17,9},{25,17},{2,26},{10... | collective-permute-start | bytes 110600 | tf_op jit(solution)/shard_map/ppermute | solution.py:450
  11.1 1.0 %shard_map.120.bias = f32[2,864,128]{2,1,0:T(8,128)S(1)} custom-call(f32[72,276]{1,0:T(8,128)S(1)} %reshape.34.table), custom_call_target="tpu_custom_call" | custom-call | flops 200000000 | bytes 1000000 | tf_op jit(solution)/shard_map/pallas_call | solution.py:481
  12.5 2.0 %shard_map.121 = (bf16[288,256]{1,0:T(8,128)(2,1)S(1)}, f32[288,256]{1,0:T(8,128)S(1)}, f32[8,192]{1,0:T(8,128)S(1)}, f32[2,864,128]{2,1,0:T(8,128)S(1)}, f32[57...) custom-call(bf16[72,256]{1,0:T(8,128)(2,1)S(1)} %collective-permute-done.south, ...), custom_call_target="tpu_custom_call" | custom-call | flops 1000000 | bytes 1000000 | tf_op jit(solution)/shard_map/pallas_call | solution.py:500
  14.5 0.6 %collective-permute-start.4 = (bf16[288,256]{1,0:T(8,128)(2,1)S(1)}, bf16[288,256]{1,0:T(8,128)(2,1)S(1)}, u32[]{:S(2)}, u32[]{:S(2)}) collective-permute-start(bf16[288,256]{1,0:T(8,128)(2,1)S(1)} %get-tuple-element.47), channel_id=1, source_target_pairs={{0,8},{8,0},{16,24},{24,16},{1,9},{9,1},{17,25},{25,17},{2,10},{10... | collective-permute-start | bytes 442376 | tf_op jit(solution)/shard_map/ppermute | solution.py:436
  15.1 0.8 %shard_map.122.table = bf16[88,256]{1,0:T(8,128)(2,1)S(1)} custom-call(f32[2,864,128]{2,1,0:T(8,128)S(1)} %get-tuple-element.49.scores_grad), custom_call_target="tpu_custom_call" | custom-call | flops 200000000 | bytes 1000000 | tf_op jit(solution)/shard_map/pallas_call | solution.py:508
  16.1 0.6 %collective-permute-start.6 = (bf16[168,256]{1,0:T(8,128)(2,1)S(1)}, bf16[168,256]{1,0:T(8,128)(2,1)S(1)}, u32[]{:S(2)}, u32[]{:S(2)}) collective-permute-start(bf16[168,256]{1,0:T(8,128)(2,1)S(1)} %get-tuple-element.51.sent), channel_id=1, source_target_pairs={{0,1},{1,0},{2,3},{3,2},{4,5},{5,4},{6,7},{7,6},{8,9},{9,8},{10,11... | collective-permute-start | bytes 258056 | tf_op jit(solution)/shard_map/ppermute | solution.py:436
  16.8 2.1 %collective-permute-start.5 = (bf16[72,256]{1,0:T(8,128)(2,1)S(1)}, bf16[72,256]{1,0:T(8,128)(2,1)S(1)}, u32[]{:S(2)}, u32[]{:S(2)}) collective-permute-start(bf16[72,256]{1,0:T(8,128)(2,1)S(1)} %get-tuple-element.52), channel_id=1, source_target_pairs={{0,25},{1,24},{8,17},{9,16},{16,9},{17,8},{24,1},{25,0},{2,27},{3,... | collective-permute-start | bytes 110600 | tf_op jit(solution)/shard_map/ppermute | solution.py:441
  18.9 0.6 %collective-permute-start.7 = (bf16[72,256]{1,0:T(8,128)(2,1)S(1)}, bf16[72,256]{1,0:T(8,128)(2,1)S(1)}, u32[]{:S(2)}, u32[]{:S(2)}) collective-permute-start(bf16[72,256]{1,0:T(8,128)(2,1)S(1)} %get-tuple-element.53), channel_id=1, source_target_pairs={{0,24},{8,16},{16,8},{24,0},{1,25},{9,17},{17,9},{25,1},{2,26},{10... | collective-permute-start | bytes 110600 | tf_op jit(solution)/shard_map/ppermute | solution.py:436
  19.4 0.7 %shard_map.124 = (bf16[96,192]{1,0:T(8,128)(2,1)S(1)}, bf16[72,256]{1,0:T(8,128)(2,1)S(1)}) custom-call(f32[576,144]{1,0:T(8,128)S(1)} %get-tuple-element.54.grad_qkv_t, f32[144,192]{1,0:T(8,128)S(1)} %get-tuple-element.55.unit, f32[160,192]{1,0:T(8,128)S(1)} %get-tuple-element.56.scales, bf16[576,192]{1,0:T(8,128)(2,1)S(1)} %get-tuple-element.57.qkv_w, ...), custom_call_target="tpu_custom_call" | custom-call | flops 100000000 | bytes 1000000 | tf_op jit(solution)/shard_map/pallas_call | solution.py:524
  20.1 2.1 %collective-permute-done.5.from_both = bf16[72,256]{1,0:T(8,128)(2,1)S(1)} collective-permute-done((bf16[72,256]{1,0:T(8,128)(2,1)S(1)}, bf16[72,256]{1,0:T(8,128)(2,1)S(1)}, u32[]{:S(2)}, u32[]{:S(2)}) %collective-permute-start.5) | collective-permute-done | bytes 36896 | tf_op jit(solution)/shard_map/ppermute | solution.py:441
  22.5 1.6 %collective-permute-start.8 = (bf16[152,256]{1,0:T(8,128)(2,1)S(1)}, bf16[152,256]{1,0:T(8,128)(2,1)S(1)}, u32[]{:S(2)}, u32[]{:S(2)}) collective-permute-start(bf16[152,256]{1,0:T(8,128)(2,1)S(1)} %get-tuple-element.59.sent), channel_id=1, source_target_pairs={{0,2},{2,0},{4,6},{6,4},{1,3},{3,1},{5,7},{7,5},{8,10},{10,8},{12,... | collective-permute-start | bytes 233480 | tf_op jit(solution)/shard_map/ppermute | solution.py:436
  24.1 3.3 %collective-permute-done.8.got.before = bf16[152,256]{1,0:T(8,128)(2,1)S(1)} collective-permute-done((bf16[152,256]{1,0:T(8,128)(2,1)S(1)}, bf16[152,256]{1,0:T(8,128)(2,1)S(1)}, u32[]{:S(2)}, u32[]{:S(2)}) %collective-permute-start.8) | collective-permute-done | bytes 77856 | tf_op jit(solution)/shard_map/ppermute | solution.py:436
  27.4 2.4 %collective-permute-start.9 = (bf16[152,256]{1,0:T(8,128)(2,1)S(1)}, bf16[152,256]{1,0:T(8,128)(2,1)S(1)}, u32[]{:S(2)}, u32[]{:S(2)}) collective-permute-start(bf16[152,256]{1,0:T(8,128)(2,1)S(1)} %shard_map.126.sent), channel_id=1, source_target_pairs={{0,6},{2,4},{4,2},{6,0},{1,7},{3,5},{5,3},{7,1},{8,14},{10,12},{12... | collective-permute-start | bytes 233480 | tf_op jit(solution)/shard_map/ppermute | solution.py:436
  29.8 0.6 %collective-permute-start.10 = (bf16[88,256]{1,0:T(8,128)(2,1)S(1)}, bf16[88,256]{1,0:T(8,128)(2,1)S(1)}, u32[]{:S(2)}, u32[]{:S(2)}) collective-permute-start(bf16[88,256]{1,0:T(8,128)(2,1)S(1)} %get-tuple-element.64.sent), channel_id=1, source_target_pairs={{0,24},{8,16},{16,8},{24,0},{1,25},{9,17},{17,9},{25,1},{2,26},{10... | collective-permute-start | bytes 135176 | tf_op jit(solution)/shard_map/ppermute | solution.py:436
  30.4 3.3 %collective-permute-done.9.got = bf16[152,256]{1,0:T(8,128)(2,1)S(1)} collective-permute-done((bf16[152,256]{1,0:T(8,128)(2,1)S(1)}, bf16[152,256]{1,0:T(8,128)(2,1)S(1)}, u32[]{:S(2)}, u32[]{:S(2)}) %collective-permute-start.9) | collective-permute-done | bytes 77856 | tf_op jit(solution)/shard_map/ppermute | solution.py:436
  34.0 0.4 %collective-permute-start.11 = (bf16[152,256]{1,0:T(8,128)(2,1)S(1)}, bf16[152,256]{1,0:T(8,128)(2,1)S(1)}, u32[]{:S(2)}, u32[]{:S(2)}) collective-permute-start(bf16[152,256]{1,0:T(8,128)(2,1)S(1)} %get-tuple-element.65.sent), channel_id=1, source_target_pairs={{0,24},{8,16},{16,8},{24,0},{1,25},{9,17},{17,9},{25,1},{2,26},{10... | collective-permute-start | bytes 233480 | tf_op jit(solution)/shard_map/ppermute | solution.py:436
  34.4 0.7 %collective-permute-start.12 = (bf16[88,256]{1,0:T(8,128)(2,1)S(1)}, bf16[88,256]{1,0:T(8,128)(2,1)S(1)}, u32[]{:S(2)}, u32[]{:S(2)}) collective-permute-start(bf16[88,256]{1,0:T(8,128)(2,1)S(1)} %shard_map.129.table_sent), channel_id=1, source_target_pairs={{0,8},{8,0},{16,24},{24,16},{1,9},{9,1},{17,25},{25,17},{2,10},{10... | collective-permute-start | bytes 135176 | tf_op jit(solution)/shard_map/ppermute | solution.py:436
  35.2 3.5 %collective-permute-done.11.got.earlier = bf16[152,256]{1,0:T(8,128)(2,1)S(1)} collective-permute-done((bf16[152,256]{1,0:T(8,128)(2,1)S(1)}, bf16[152,256]{1,0:T(8,128)(2,1)S(1)}, u32[]{:S(2)}, u32[]{:S(2)}) %collective-permute-start.11) | collective-permute-done | bytes 77856 | tf_op jit(solution)/shard_map/ppermute | solution.py:436
  39.3 0.8 %shard_map.131 = bf16[72,2,192]{2,1,0:T(2,128)(2,1)} custom-call(bf16[2,6,12,192]{3,2,1,0:T(8,128)(2,1)S(1)} %get-tuple-element.79.dy, bf16[96,192]{1,0:T(8,128)(2,1)S(1)} %get-tuple-element.62.quads, bf16[72,256]{1,0:T(8,128)(2,1)S(1)} %get-tuple-element.69.south, bf16[72,256]{1,0:T(8,128)(2,1)S(1)} %shard_map.130.east), custom_call_target="tpu_custom_call" | custom-call | flops 1000000 | bytes 1000000 | tf_op jit(solution)/shard_map/pallas_call | solution.py:572
  40.1 0.9 %shard_map.133 = (f32[288,192]{1,0:T(8,128)}, f32[96,192]{1,0:T(8,128)}, f32[1,96]{1,0:T(1,128)}, f32[6,1,3312]{2,1,0:T(1,128)}) custom-call(bf16[152,256]{1,0:T(8,128)(2,1)S(1)} %shard_map.128.sent, bf16[152,256]{1,0:T(8,128)(2,1)S(1)} %collective-permute-done.14.got, f32[6,1,3312]{2,1,0:T(1,128)S(1)} %shard_map.132.table), custom_call_target="tpu_custom_call" | custom-call | flops 1000000 | bytes 1000000 | tf_op jit(solution)/shard_map/pallas_call | solution.py:578
  (36 shorter events, 2.5 us)
Async XLA Ops:
  0.6 1.0 %copy-start.3 = (bf16[96,192]{1,0:T(8,128)(2,1)S(1)}, bf16[96,192]{1,0:T(8,128)(2,1)}, u32[]{:S(2)}) copy-start(bf16[96,192]{1,0:T(8,128)(2,1)} %proj.1) | copy-start | bytes 110596
  0.6 1.0 %copy-start = (bf16[288,192]{1,0:T(8,128)(2,1)S(1)}, bf16[288,192]{1,0:T(8,128)(2,1)}, u32[]{:S(2)}) copy-start(bf16[288,192]{1,0:T(8,128)(2,1)} %qkv.1) | copy-start | bytes 331780
  1.6 0.7 %copy-start.4 = (bf16[96]{0:T(256)(128)(2,1)S(1)}, bf16[96]{0:T(256)(128)(2,1)}, u32[]{:S(2)}) copy-start(bf16[96]{0:T(256)(128)(2,1)} %param.12) | copy-start | bytes 580
  2.3 8.5 %copy-start.5 = (f32[1,6,3312]{2,0,1:T(1,128)S(1)}, f32[1,6,3312]{2,0,1:T(1,128)}, u32[]{:S(2)}) copy-start(f32[1,6,3312]{2,0,1:T(1,128)} %param.13) | copy-start | bytes 238468
  2.5 10.0 %collective-permute-start.3 = (bf16[400,192]{1,0:T(8,128)(2,1)S(1)}, bf16[400,192]{1,0:T(8,128)(2,1)S(1)}, u32[]{:S(2)}, u32[]{:S(2)}) collective-permute-start(bf16[400,192]{1,0:T(8,128)(2,1)S(1)} %get-tuple-element.45.refs_0_), channel_id=1, source_target_pairs={{0,1},{1,0},{2,3},{3,2},{4,5},{5,4},{6,7},{7,6},{8,9},{9,8},{10,11... | collective-permute-start | bytes 460808 | tf_op jit(solution)/shard_map/ppermute | solution.py:450
  5.5 6.7 %collective-permute-start = (bf16[72,256]{1,0:T(8,128)(2,1)S(1)}, bf16[72,256]{1,0:T(8,128)(2,1)S(1)}, u32[]{:S(2)}, u32[]{:S(2)}) collective-permute-start(bf16[72,256]{1,0:T(8,128)(2,1)S(1)} %get-tuple-element.42), channel_id=1, source_target_pairs={{0,6},{2,0},{4,2},{6,4},{1,7},{3,1},{5,3},{7,5},{8,14},{10,8},{12,... | collective-permute-start | bytes 110600 | tf_op jit(solution)/shard_map/ppermute | solution.py:450
  9.1 3.4 %collective-permute-start.1 = (bf16[72,256]{1,0:T(8,128)(2,1)S(1)}, bf16[72,256]{1,0:T(8,128)(2,1)S(1)}, u32[]{:S(2)}, u32[]{:S(2)}) collective-permute-start(bf16[72,256]{1,0:T(8,128)(2,1)S(1)} %get-tuple-element.43), channel_id=1, source_target_pairs={{0,30},{2,24},{4,26},{6,28},{8,6},{10,0},{12,2},{14,4},{16,14},{18... | collective-permute-start | bytes 110600 | tf_op jit(solution)/shard_map/ppermute | solution.py:460
  9.3 3.1 %collective-permute-start.2 = (bf16[72,256]{1,0:T(8,128)(2,1)S(1)}, bf16[72,256]{1,0:T(8,128)(2,1)S(1)}, u32[]{:S(2)}, u32[]{:S(2)}) collective-permute-start(bf16[72,256]{1,0:T(8,128)(2,1)S(1)} %get-tuple-element.44), channel_id=1, source_target_pairs={{0,24},{8,0},{16,8},{24,16},{1,25},{9,1},{17,9},{25,17},{2,26},{10... | collective-permute-start | bytes 110600 | tf_op jit(solution)/shard_map/ppermute | solution.py:450
  11.1 1.4 %copy-start.2 = (bf16[144,192]{1,0:T(8,128)(2,1)S(1)}, bf16[144,192]{1,0:T(8,128)(2,1)}, u32[]{:S(2)}) copy-start(bf16[144,192]{1,0:T(8,128)(2,1)} %constant.4.clone.order) | copy-start | bytes 165892
  14.5 1.6 %collective-permute-start.4 = (bf16[288,256]{1,0:T(8,128)(2,1)S(1)}, bf16[288,256]{1,0:T(8,128)(2,1)S(1)}, u32[]{:S(2)}, u32[]{:S(2)}) collective-permute-start(bf16[288,256]{1,0:T(8,128)(2,1)S(1)} %get-tuple-element.47), channel_id=1, source_target_pairs={{0,8},{8,0},{16,24},{24,16},{1,9},{9,1},{17,25},{25,17},{2,10},{10... | collective-permute-start | bytes 442376 | tf_op jit(solution)/shard_map/ppermute | solution.py:436
  16.1 3.3 %copy-start.1 = (bf16[192,144]{1,0:T(8,128)(2,1)S(1)}, bf16[192,144]{1,0:T(8,128)(2,1)}, u32[]{:S(2)}) copy-start(bf16[192,144]{1,0:T(8,128)(2,1)} %constant.5.clone.order_t) | copy-start | bytes 165892
  16.1 6.3 %collective-permute-start.6 = (bf16[168,256]{1,0:T(8,128)(2,1)S(1)}, bf16[168,256]{1,0:T(8,128)(2,1)S(1)}, u32[]{:S(2)}, u32[]{:S(2)}) collective-permute-start(bf16[168,256]{1,0:T(8,128)(2,1)S(1)} %get-tuple-element.51.sent), channel_id=1, source_target_pairs={{0,1},{1,0},{2,3},{3,2},{4,5},{5,4},{6,7},{7,6},{8,9},{9,8},{10,11... | collective-permute-start | bytes 258056 | tf_op jit(solution)/shard_map/ppermute | solution.py:436
  16.8 5.4 %collective-permute-start.5 = (bf16[72,256]{1,0:T(8,128)(2,1)S(1)}, bf16[72,256]{1,0:T(8,128)(2,1)S(1)}, u32[]{:S(2)}, u32[]{:S(2)}) collective-permute-start(bf16[72,256]{1,0:T(8,128)(2,1)S(1)} %get-tuple-element.52), channel_id=1, source_target_pairs={{0,25},{1,24},{8,17},{9,16},{16,9},{17,8},{24,1},{25,0},{2,27},{3,... | collective-permute-start | bytes 110600 | tf_op jit(solution)/shard_map/ppermute | solution.py:441
  18.9 3.6 %collective-permute-start.7 = (bf16[72,256]{1,0:T(8,128)(2,1)S(1)}, bf16[72,256]{1,0:T(8,128)(2,1)S(1)}, u32[]{:S(2)}, u32[]{:S(2)}) collective-permute-start(bf16[72,256]{1,0:T(8,128)(2,1)S(1)} %get-tuple-element.53), channel_id=1, source_target_pairs={{0,24},{8,16},{16,8},{24,0},{1,25},{9,17},{17,9},{25,1},{2,26},{10... | collective-permute-start | bytes 110600 | tf_op jit(solution)/shard_map/ppermute | solution.py:436
  22.5 4.9 %collective-permute-start.8 = (bf16[152,256]{1,0:T(8,128)(2,1)S(1)}, bf16[152,256]{1,0:T(8,128)(2,1)S(1)}, u32[]{:S(2)}, u32[]{:S(2)}) collective-permute-start(bf16[152,256]{1,0:T(8,128)(2,1)S(1)} %get-tuple-element.59.sent), channel_id=1, source_target_pairs={{0,2},{2,0},{4,6},{6,4},{1,3},{3,1},{5,7},{7,5},{8,10},{10,8},{12,... | collective-permute-start | bytes 233480 | tf_op jit(solution)/shard_map/ppermute | solution.py:436
  27.4 6.3 %collective-permute-start.9 = (bf16[152,256]{1,0:T(8,128)(2,1)S(1)}, bf16[152,256]{1,0:T(8,128)(2,1)S(1)}, u32[]{:S(2)}, u32[]{:S(2)}) collective-permute-start(bf16[152,256]{1,0:T(8,128)(2,1)S(1)} %shard_map.126.sent), channel_id=1, source_target_pairs={{0,6},{2,4},{4,2},{6,0},{1,7},{3,5},{5,3},{7,1},{8,14},{10,12},{12... | collective-permute-start | bytes 233480 | tf_op jit(solution)/shard_map/ppermute | solution.py:436
  29.8 4.1 %collective-permute-start.10 = (bf16[88,256]{1,0:T(8,128)(2,1)S(1)}, bf16[88,256]{1,0:T(8,128)(2,1)S(1)}, u32[]{:S(2)}, u32[]{:S(2)}) collective-permute-start(bf16[88,256]{1,0:T(8,128)(2,1)S(1)} %get-tuple-element.64.sent), channel_id=1, source_target_pairs={{0,24},{8,16},{16,8},{24,0},{1,25},{9,17},{17,9},{25,1},{2,26},{10... | collective-permute-start | bytes 135176 | tf_op jit(solution)/shard_map/ppermute | solution.py:436
  34.0 4.7 %collective-permute-start.11 = (bf16[152,256]{1,0:T(8,128)(2,1)S(1)}, bf16[152,256]{1,0:T(8,128)(2,1)S(1)}, u32[]{:S(2)}, u32[]{:S(2)}) collective-permute-start(bf16[152,256]{1,0:T(8,128)(2,1)S(1)} %get-tuple-element.65.sent), channel_id=1, source_target_pairs={{0,24},{8,16},{16,8},{24,0},{1,25},{9,17},{17,9},{25,1},{2,26},{10... | collective-permute-start | bytes 233480 | tf_op jit(solution)/shard_map/ppermute | solution.py:436
  34.4 4.3 %collective-permute-start.12 = (bf16[88,256]{1,0:T(8,128)(2,1)S(1)}, bf16[88,256]{1,0:T(8,128)(2,1)S(1)}, u32[]{:S(2)}, u32[]{:S(2)}) collective-permute-start(bf16[88,256]{1,0:T(8,128)(2,1)S(1)} %shard_map.129.table_sent), channel_id=1, source_target_pairs={{0,8},{8,0},{16,24},{24,16},{1,9},{9,1},{17,25},{25,17},{2,10},{10... | collective-permute-start | bytes 135176 | tf_op jit(solution)/shard_map/ppermute | solution.py:436
  35.1 3.6 %collective-permute-start.13 = (bf16[72,256]{1,0:T(8,128)(2,1)S(1)}, bf16[72,256]{1,0:T(8,128)(2,1)S(1)}, u32[]{:S(2)}, u32[]{:S(2)}) collective-permute-start(bf16[72,256]{1,0:T(8,128)(2,1)S(1)} %get-tuple-element.67), channel_id=1, source_target_pairs={{0,8},{8,0},{16,24},{24,16},{1,9},{9,1},{17,25},{25,17},{2,10},{10... | collective-permute-start | bytes 110600 | tf_op jit(solution)/shard_map/ppermute | solution.py:436
  38.7 1.4 %collective-permute-start.14 = (bf16[152,256]{1,0:T(8,128)(2,1)S(1)}, bf16[152,256]{1,0:T(8,128)(2,1)S(1)}, u32[]{:S(2)}, u32[]{:S(2)}) collective-permute-start(bf16[152,256]{1,0:T(8,128)(2,1)S(1)} %shard_map.128.sent), channel_id=1, source_target_pairs={{0,8},{8,0},{16,24},{24,16},{1,9},{9,1},{17,25},{25,17},{2,10},{10... | collective-permute-start | bytes 233480 | tf_op jit(solution)/shard_map/ppermute | solution.py:436
